TPU v7x, 32 devices: a whole 2x2x4 slice. The times are simulated.
32 devices in a mesh: head: 2 (over x), ctx: 16 (over z, y, core).
Axes of the slice: x: 2, y: 2, z: 4, core: 2. Of those that a mesh axis runs over, the one named last changes fastest.
Arguments:
- queries: bfloat16 [8192, 32, 128], P('ctx', 'head'), may hold values from -1.75 to 1.75
- keys: bfloat16 [8192, 32, 128], P('ctx', 'head'), may hold values from -1.75 to 1.75
- values: bfloat16 [8192, 32, 128], P('ctx', 'head'), may hold values from -6 to 6
- out_grad: bfloat16 [8192, 32, 128], P('ctx', 'head'), may hold values from -6 to 6
- gain: float32 [32, 128], P('head'), may hold values from 0.25 to 1.75
- decay_rate: float32 [32], P('head'), may hold values from 1e-05 to 0.03
- doc_lengths: int32 [32], replicated, may hold values from 1 to 4096, 8192 in all
Outputs:
- q_grad: bfloat16 [8192, 32, 128], P('ctx', 'head')
- k_grad: bfloat16 [8192, 32, 128], P('ctx', 'head')
- v_grad: bfloat16 [8192, 32, 128], P('ctx', 'head')
Inputs may be any that keep to these rules, and one draw needn't show every extreme that they name: `doc_lengths`: the lengths sum to 8192 and the longest is exactly 4096.
All inputs are finite; a program needn't handle non-finite values.
Results may differ from a plain program's by a relative error of at most 0.006.
Values sent between devices are 32-bit elements; how exact they have to be, the bound alone decides.
No kernel may reach another device: no remote copies, remote signals or barrier semaphores. Data moves between devices by JAX's collectives and lax.ppermute only.
A program may use at most 128 MiB of HBM per device.

v0:
```python
from functools import partial

import jax
import jax.numpy as jnp
from jax import lax
from jax.sharding import PartitionSpec as P

LEVELS = 3


epsilon = 1e-06


def passed_along(block, axis, distance):
    devices = range(lax.axis_size(axis))
    route = [(i - distance, i) for i in devices if i - distance in devices]
    return lax.ppermute(block, axis, route)


def mix(form, left, right):
    return jnp.einsum(
        form,
        left.astype(jnp.float32),
        right.astype(jnp.float32),
        preferred_element_type=jnp.float32,
    )


def segment_of(starts, positions):
    before = (starts[None, :] <= positions[:, None]).astype(jnp.int32)
    return jnp.sum(before, axis=1) - 1


def decay_mask(segment, decays):
    block_len = segment.shape[0]
    offsets = jnp.arange(block_len, dtype=jnp.int32)
    distance = offsets[:, None] - offsets[None, :]
    allowed = (distance >= 0) & (segment[:, None] == segment[None, :])
    weight = jnp.exp(-decays[:, None, None] * jnp.maximum(distance, 0).astype(jnp.float32)[None])
    return jnp.where(allowed[None], weight, jnp.float32(0.0))


def forward_block(decays, carry, block):
    carried, prev_seg = carry
    queries_blk, key_blk, values_blk, segment = block
    block_len = segment.shape[0]
    offsets = jnp.arange(block_len, dtype=jnp.float32)
    weight = decay_mask(segment, decays)
    scores = mix("thd,shd->hts", queries_blk, key_blk)
    weighted = (scores * weight).astype(jnp.bfloat16)
    output = mix("hts,shd->thd", weighted, values_blk)
    in_factor = jnp.where(
        (segment == prev_seg)[:, None],
        jnp.exp(-decays[None, :] * (offsets[:, None] + 1.0)),
        jnp.float32(0.0),
    )
    output = output + in_factor[:, :, None] * mix(
        "thd,hde->the", queries_blk, carried.astype(jnp.bfloat16)
    )
    last_seg = segment[-1]
    tail = jnp.where(
        (segment == last_seg)[:, None],
        jnp.exp(-decays[None, :] * (block_len - 1.0 - offsets)[:, None]),
        jnp.float32(0.0),
    )
    own_part = mix("shd,she->hde", (key_blk * tail[:, :, None]).astype(jnp.bfloat16), values_blk)
    keep_factor = jnp.where(prev_seg == last_seg, jnp.exp(-decays * block_len), jnp.float32(0.0))
    return (
        (keep_factor[:, None, None] * carried + own_part, last_seg),
        (output, carried, weighted),
    )


def gradient_block(decays, block):
    queries_blk, key_blk, values_blk, grad_blk, segment, carried, prev_seg, weighted = block
    block_len = segment.shape[0]
    offsets = jnp.arange(block_len, dtype=jnp.float32)
    weight = decay_mask(segment, decays)
    grad_scores = mix("thd,shd->hts", grad_blk, values_blk)
    grad_weights = (grad_scores * weight).astype(jnp.bfloat16)
    q_part = mix("hts,shd->thd", grad_weights, key_blk)
    k_part = mix("hts,thd->shd", grad_weights, queries_blk)
    v_part = mix("hts,thd->shd", weighted, grad_blk)
    in_factor = jnp.where(
        (segment == prev_seg)[:, None],
        jnp.exp(-decays[None, :] * (offsets[:, None] + 1.0)),
        jnp.float32(0.0),
    )
    q_part = q_part + in_factor[:, :, None] * mix(
        "the,hde->thd", grad_blk, carried.astype(jnp.bfloat16)
    )
    return (q_part, k_part, v_part)


def reverse_block(decays, carry, block):
    carried, next_seg = carry
    queries_blk, key_blk, values_blk, grad_blk, segment = block
    block_len = segment.shape[0]
    offsets = jnp.arange(block_len, dtype=jnp.float32)
    in_factor = jnp.where(
        (segment == next_seg)[:, None],
        jnp.exp(-decays[None, :] * (block_len - offsets[:, None])),
        jnp.float32(0.0),
    )
    packed = carried.astype(jnp.bfloat16)
    k_extra = in_factor[:, :, None] * mix("she,hde->shd", values_blk, packed)
    v_extra = in_factor[:, :, None] * mix("shd,hde->she", key_blk, packed)
    first_seg = segment[0]
    lead = jnp.where(
        (segment == first_seg)[:, None],
        jnp.exp(-decays[None, :] * offsets[:, None]),
        jnp.float32(0.0),
    )
    own_part = mix("thd,the->hde", (queries_blk * lead[:, :, None]).astype(jnp.bfloat16), grad_blk)
    keep_factor = jnp.where(first_seg == next_seg, jnp.exp(-decays * block_len), jnp.float32(0.0))
    return ((keep_factor[:, None, None] * carried + own_part, first_seg), (k_extra, v_extra))


def in_blocks(array, blocks):
    return array.reshape((blocks, array.shape[0] // blocks) + array.shape[1:])


def chain_combine(earlier, latter):
    return (earlier[0] * latter[0], latter[0][:, None, None] * earlier[1] + latter[1])


def local(queries, keys, values, out_grad, gain, decay_rate, doc_lengths):
    tok_rows, head_count, head_dim = queries.shape
    block_len = min(512, tok_rows)
    blocks = tok_rows // block_len
    norm_width = head_count * head_dim * lax.axis_size("head")
    first_row = lax.axis_index("ctx") * tok_rows
    starts = jnp.cumsum(doc_lengths) - doc_lengths
    positions = first_row + jnp.arange(tok_rows, dtype=jnp.int32)
    segment = segment_of(starts, positions)
    prev_seg = segment_of(starts, jnp.reshape(first_row - 1, (1,)))[0]
    next_seg = segment_of(starts, jnp.reshape(first_row + tok_rows, (1,)))[0]
    offsets = jnp.arange(tok_rows, dtype=jnp.float32)
    query_b = in_blocks(queries, blocks)
    key_b = in_blocks(keys, blocks)
    value_b = in_blocks(values, blocks)
    seg_b = in_blocks(segment, blocks)
    zero_state = jnp.zeros((head_count, head_dim, head_dim), jnp.float32)
    shard_fade = jnp.exp(-decay_rate * tok_rows)
    (own_state, last_seg), (outs_local, entry_states, weighted_b) = lax.scan(
        partial(forward_block, decay_rate), (zero_state, prev_seg), (query_b, key_b, value_b, seg_b)
    )
    forward_summary = (jnp.where(prev_seg == segment[-1], shard_fade, jnp.float32(0.0)), own_state)
    forward_in = passed_along((forward_summary[0], forward_summary[1]), "ctx", 1)
    for level in range(LEVELS):
        earlier = passed_along((forward_in[0], forward_in[1]), "ctx", 1 << level)
        forward_in = chain_combine(earlier, forward_in)
    state_in = forward_in[1].astype(jnp.bfloat16)
    in_factor = jnp.where(
        (segment == prev_seg)[:, None],
        jnp.exp(-decay_rate[None, :] * (offsets[:, None] + 1.0)),
        jnp.float32(0.0),
    )
    attn_out = outs_local.reshape(tok_rows, head_count, head_dim)
    attn_out = attn_out + in_factor[:, :, None] * mix("thd,hde->the", queries, state_in)
    gained = gain[None] * out_grad.astype(jnp.float32)
    squares = jnp.sum(attn_out * attn_out, axis=(1, 2))
    cross = jnp.sum(gained * attn_out, axis=(1, 2))
    squares, cross = lax.psum((squares, cross), "head")
    inverse = 1.0 / jnp.sqrt(squares / norm_width + epsilon)
    grad_o = (
        gained * inverse[:, None, None]
        - attn_out * (cross * inverse * inverse * inverse / norm_width)[:, None, None]
    ).astype(jnp.bfloat16)
    grad_b = in_blocks(grad_o, blocks)
    (own_grad, first_seg), (k_extra, v_extra) = lax.scan(
        partial(reverse_block, decay_rate),
        (zero_state, next_seg),
        (query_b, key_b, value_b, grad_b, seg_b),
        reverse=True,
    )
    gradient_summary = (jnp.where(segment[0] == next_seg, shard_fade, jnp.float32(0.0)), own_grad)
    gradient_in = passed_along((gradient_summary[0], gradient_summary[1]), "ctx", -1)
    for level in range(LEVELS):
        earlier = passed_along((gradient_in[0], gradient_in[1]), "ctx", -(1 << level))
        gradient_in = chain_combine(earlier, gradient_in)
    prev_blocks = jnp.concatenate([jnp.reshape(prev_seg, (1,)), seg_b[:-1, -1]])
    q_part, k_part, v_part = lax.map(
        partial(gradient_block, decay_rate),
        (query_b, key_b, value_b, grad_b, seg_b, entry_states, prev_blocks, weighted_b),
    )
    shape = (tok_rows, head_count, head_dim)
    q_grad = q_part.reshape(shape) + in_factor[:, :, None] * mix("the,hde->thd", grad_o, state_in)
    back_factor = jnp.where(
        (segment == next_seg)[:, None],
        jnp.exp(-decay_rate[None, :] * (tok_rows - offsets[:, None])),
        jnp.float32(0.0),
    )
    packed = gradient_in[1].astype(jnp.bfloat16)
    k_grad = (k_part + k_extra).reshape(shape) + back_factor[:, :, None] * mix(
        "she,hde->shd", values, packed
    )
    v_grad = (v_part + v_extra).reshape(shape) + back_factor[:, :, None] * mix(
        "shd,hde->she", keys, packed
    )
    return (q_grad.astype(jnp.bfloat16), k_grad.astype(jnp.bfloat16), v_grad.astype(jnp.bfloat16))


def solution(mesh):
    in_specs = (
        P("ctx", "head", None),
        P("ctx", "head", None),
        P("ctx", "head", None),
        P("ctx", "head", None),
        P("head", None),
        P("head"),
        P(),
    )
    out_specs = (P("ctx", "head", None), P("ctx", "head", None), P("ctx", "head", None))
    return jax.shard_map(local, mesh=mesh, in_specs=in_specs, out_specs=out_specs, check_vma=False)
```

profile of v0, /device:TPU:12, one launch (start us, length us, event | category | flops | bytes accessed | tf_op | source)
XLA Modules:
  0.0 229.1 jit_solution(10041496581794094571)
XLA Ops:
  8.1 2.6 %multiply_convert_fusion.3 = bf16[512,16,128]{2,1,0:T(8,128)(2,1)S(1)} fusion(bf16[512,16,128]{2,1,0:T(8,128)(2,1)} %param.8, f32[512,16]{1,0:T(8,128)S(1)} %copy.90), kind=kLoop, calls=%fused_computation.26 | loop fusion | flops 3145728 | bytes 4227072 | tf_op jit(solution)/shard_map/while/body/eval_jaxpr/convert_element_type | solution.py:66
  14.7 14.2 %collective-permute-done.3 = f32[16,128,128]{2,1,0:T(8,128)S(1)} collective-permute-done((f32[16,128,128]{2,1,0:T(8,128)S(1)}, f32[16,128,128]{2,1,0:T(8,128)S(1)}, u32[]{:S(2)}, u32[]{:S(2)}) %collective-permute-start.3) | collective-permute-done | bytes 1048608 | tf_op jit(solution)/shard_map/ppermute | solution.py:17
  30.8 4.4 %collective-permute-start = (f32[16]{0:T(128)S(1)}, f32[16]{0:T(128)S(1)}, u32[]{:S(2)}, u32[]{:S(2)}) collective-permute-start(f32[16]{0:T(128)S(1)} %get-tuple-element.141), channel_id=1, source_target_pairs={{0,1},{1,2},{2,3},{3,4},{4,5},{5,6},{6,7},{7,8},{8,9},{9,10},{10,1... | collective-permute-start | bytes 200 | tf_op jit(solution)/shard_map/ppermute | solution.py:17
  35.4 9.6 %collective-permute-done = f32[16]{0:T(128)S(1)} collective-permute-done((f32[16]{0:T(128)S(1)}, f32[16]{0:T(128)S(1)}, u32[]{:S(2)}, u32[]{:S(2)}) %collective-permute-start) | collective-permute-done | bytes 96 | tf_op jit(solution)/shard_map/ppermute | solution.py:17
  45.2 5.2 %collective-permute-start.5 = (f32[16,128,128]{2,1,0:T(8,128)S(1)}, f32[16,128,128]{2,1,0:T(8,128)S(1)}, u32[]{:S(2)}, u32[]{:S(2)}) collective-permute-start(f32[16,128,128]{2,1,0:T(8,128)S(1)} %multiply_add_fusion.3), channel_id=1, source_target_pairs={{0,2},{1,3},{2,4},{3,5},{4,6},{5,7},{6,8},{7,9},{8,10},{9,11},{10,... | collective-permute-start | bytes 3145736 | tf_op jit(solution)/shard_map/ppermute | solution.py:17
  52.5 7.7 %multiply_convert_fusion.1 = bf16[16,512,512]{2,1,0:T(8,128)(2,1)} fusion(f32[512,512]{1,0:T(8,128)S(1)} %maximum_convert_fusion, f32[16]{0:T(128)S(1)} %get-tuple-element.142, pred[512,512]{1,0:T(8,128)(4,1)S(1)} %fusion.41, bf16[512,16,128]{2,1,0:T(8,128)(2,1)S(1)} %copy-done.2, bf16[512,16,128]{2,1,0:T(8,128)(2,1)S(1)} %copy-done), kind=kOutput, calls=%fused_computation.1 | convolution fusion | flops 1090519040 | bytes 13893696 | tf_op jit(solution)/shard_map/while/body/eval_jaxpr/thd,shd->hts/dot_general | solution.py:21
  60.3 10.7 %collective-permute-done.1 = f32[16]{0:T(128)S(1)} collective-permute-done((f32[16]{0:T(128)S(1)}, f32[16]{0:T(128)S(1)}, u32[]{:S(2)}, u32[]{:S(2)}) %collective-permute-start.1) | collective-permute-done | bytes 96 | tf_op jit(solution)/shard_map/ppermute | solution.py:17
  72.4 3.5 %collective-permute-start.6 = (f32[16,128,128]{2,1,0:T(8,128)S(1)}, f32[16,128,128]{2,1,0:T(8,128)}, u32[]{:S(2)}, u32[]{:S(2)}) collective-permute-start(f32[16,128,128]{2,1,0:T(8,128)S(1)} %multiply_add_fusion.2), channel_id=1, source_target_pairs={{0,4},{1,5},{2,6},{3,7},{4,8},{5,9},{6,10},{7,11},{8,12},{9,13},{1... | collective-permute-start | bytes 3145736 | tf_op jit(solution)/shard_map/ppermute | solution.py:17
  75.9 3.0 %fusion.30 = f32[16,128,512]{2,1,0:T(8,128)} fusion(bf16[512,16,128]{2,1,0:T(8,128)(2,1)S(1)} %copy-done), kind=kOutput, calls=%fused_computation.43 | convolution fusion | flops 268435456 | bytes 6291456 | tf_op jit(solution)/shard_map/while/body/eval_jaxpr/thd,hde->the/dot_general | solution.py:21
  81.2 8.2 %fusion.33 = f32[16,512,128]{1,2,0:T(8,128)} fusion(bf16[16,512,512]{2,1,0:T(8,128)(2,1)} %multiply_convert_fusion.1, bf16[512,16,128]{2,1,0:T(8,128)(2,1)S(1)} %copy-done.6), kind=kOutput, calls=%fused_computation.46 | convolution fusion | flops 1073741824 | bytes 14680064 | tf_op jit(solution)/shard_map/while/body/eval_jaxpr/hts,shd->thd/dot_general | solution.py:21
  89.4 3.7 %collective-permute-start.2 = (f32[16]{0:T(128)S(1)}, f32[16]{0:T(128)S(1)}, u32[]{:S(2)}, u32[]{:S(2)}) collective-permute-start(f32[16]{0:T(128)S(1)} %mul.394), channel_id=1, source_target_pairs={{0,2},{1,3},{2,4},{3,5},{4,6},{5,7},{6,8},{7,9},{8,10},{9,11},{10,... | collective-permute-start | bytes 200 | tf_op jit(solution)/shard_map/ppermute | solution.py:17
  93.2 4.3 %copy.84 = bf16[512,16,128]{0,2,1:T(8,128)(2,1)} copy(bf16[512,16,128]{2,1,0:T(8,128)(2,1)} %param.10) | data formatting | bytes 4194304 | tf_op args[3]
  100.0 6.5 %multiply_reduce_fusion.1 = (f32[512]{0:T(512)S(1)}, f32[512]{0:T(512)S(1)}, f32[512,16,128]{0,2,1:T(8,128)}) fusion(bf16[512,16,128]{0,2,1:T(8,128)(2,1)} %copy.84, f32[16,128]{1,0:T(8,128)S(1)} %copy-done.17, bf16[16,128,128]{2,1,0:T(8,128)(2,1)S(1)} %add_convert_fusion.1, bf16[512,16,128]{2,1,0:T(8,128)(2,1)S(1)} %copy-done, ...), kind=kOutput, calls=%fused_computation.25 | convolution fusion | flops 278920192 | bytes 17346560 | tf_op jit(solution)/shard_map/thd,hde->the/dot_general | solution.py:21
  106.5 4.9 %all-reduce = (f32[512]{0:T(512)S(1)}, f32[512]{0:T(512)S(1)}) all-reduce(f32[512]{0:T(512)S(1)} %get-tuple-element.92, f32[512]{0:T(512)S(1)} %get-tuple-element.91), channel_id=1, replica_groups=mesh['head'=2,'ctx'=16] {'head'}, use_global_device_ids=true, to_apply=%region_6.7 | all-reduce | flops 1024 | bytes 8192 | tf_op jit(solution)/shard_map/psum | solution.py:164
  111.5 3.8 %subtract_convert_fusion = bf16[512,16,128]{0,2,1:T(8,128)(2,1)S(1)} fusion(f32[512,16,128]{0,2,1:T(8,128)} %get-tuple-element.143, bf16[512,16,128]{0,2,1:T(8,128)(2,1)} %copy.84, f32[512]{0:T(512)S(1)} %get-tuple-element.122, f32[512]{0:T(512)S(1)} %get-tuple-element.121, f32[16,128]{1,0:T(8,128)S(1)} %copy-done.17), kind=kLoop, calls=%fused_computation.23 | loop fusion | flops 6291456 | bytes 8400896 | tf_op jit(solution)/shard_map/convert_element_type | solution.py:169
  118.6 3.4 %collective-permute-start.7 = (f32[16]{0:T(128)S(1)}, f32[16]{0:T(128)S(1)}, u32[]{:S(2)}, u32[]{:S(2)}) collective-permute-start(f32[16]{0:T(128)S(1)} %get-tuple-element.98), channel_id=1, source_target_pairs={{1,0},{2,1},{3,2},{4,3},{5,4},{6,5},{7,6},{8,7},{9,8},{10,9},{11,1... | collective-permute-start | bytes 200 | tf_op jit(solution)/shard_map/ppermute | solution.py:17
  122.0 8.9 %collective-permute-done.7 = f32[16]{0:T(128)S(1)} collective-permute-done((f32[16]{0:T(128)S(1)}, f32[16]{0:T(128)S(1)}, u32[]{:S(2)}, u32[]{:S(2)}) %collective-permute-start.7) | collective-permute-done | bytes 96 | tf_op jit(solution)/shard_map/ppermute | solution.py:17
  131.0 3.9 %collective-permute-start.8 = (f32[16]{0:T(128)S(1)}, f32[16]{0:T(128)S(1)}, u32[]{:S(2)}, u32[]{:S(2)}) collective-permute-start(f32[16]{0:T(128)S(1)} %collective-permute-done.7), channel_id=1, source_target_pairs={{1,0},{2,1},{3,2},{4,3},{5,4},{6,5},{7,6},{8,7},{9,8},{10,9},{11,1... | collective-permute-start | bytes 200 | tf_op jit(solution)/shard_map/ppermute | solution.py:17
  134.8 2.7 %fusion.22 = f32[16,128,512]{1,2,0:T(8,128)} fusion(bf16[512,16,128]{2,1,0:T(8,128)(2,1)S(1)} %copy-done.3), kind=kOutput, calls=%fused_computation.35 | convolution fusion | flops 268435456 | bytes 6291456 | tf_op jit(solution)/shard_map/while/body/eval_jaxpr/shd,hde->she/dot_general | solution.py:21
  137.5 4.3 %collective-permute-start.9 = (f32[16]{0:T(128)S(1)}, f32[16]{0:T(128)S(1)}, u32[]{:S(2)}, u32[]{:S(2)}) collective-permute-start(f32[16]{0:T(128)S(1)} %mul.425), channel_id=1, source_target_pairs={{2,0},{3,1},{4,2},{5,3},{6,4},{7,5},{8,6},{9,7},{10,8},{11,9},{12,... | collective-permute-start | bytes 200 | tf_op jit(solution)/shard_map/ppermute | solution.py:17
  141.9 2.7 %collective-permute-start.11 = (f32[16,128,128]{2,1,0:T(8,128)S(1)}, f32[16,128,128]{2,1,0:T(8,128)S(1)}, u32[]{:S(2)}, u32[]{:S(2)}) collective-permute-start(f32[16,128,128]{2,1,0:T(8,128)S(1)} %collective-permute-done.10), channel_id=1, source_target_pairs={{1,0},{2,1},{3,2},{4,3},{5,4},{6,5},{7,6},{8,7},{9,8},{10,9},{11,1... | collective-permute-start | bytes 3145736 | tf_op jit(solution)/shard_map/ppermute | solution.py:17
  144.6 2.6 %fusion.36 = f32[16,128,512]{1,2,0:T(8,128)} fusion(bf16[512,16,128]{2,1,0:T(8,128)(2,1)S(1)} %copy-done.7), kind=kOutput, calls=%fused_computation.49 | convolution fusion | flops 268435456 | bytes 6291456 | tf_op jit(solution)/shard_map/while/body/eval_jaxpr/she,hde->shd/dot_general | solution.py:21
  147.2 7.0 %multiply_convert_fusion = bf16[16,512,512]{2,1,0:T(8,128)(2,1)} fusion(bf16[512,16,128]{0,2,1:T(8,128)(2,1)S(1)} %subtract_convert_fusion, f32[512,512]{1,0:T(8,128)S(1)} %copy-done.14, f32[16]{0:T(128)S(1)} %get-tuple-element.142, pred[512,512]{1,0:T(8,128)(4,1)S(1)} %copy-done.16, bf16[512,16,128]{2,1,0:T(8,128)(2,1)S(1)} %copy-done.7), kind=kOutput, calls=%fused_computation | convolution fusion | flops 1090519040 | bytes 13893696 | tf_op jit(solution)/shard_map/while/body/eval_jaxpr/thd,shd->hts/dot_general | solution.py:21
  160.2 6.3 %fusion.24 = f32[16,512,128]{1,2,0:T(8,128)S(1)} fusion(bf16[16,512,512]{2,1,0:T(8,128)(2,1)} %multiply_convert_fusion, bf16[512,16,128]{2,1,0:T(8,128)(2,1)S(1)} %copy-done.3), kind=kOutput, calls=%fused_computation.37 | convolution fusion | flops 1073741824 | bytes 14680064 | tf_op jit(solution)/shard_map/while/body/eval_jaxpr/hts,shd->thd/dot_general | solution.py:21
  169.3 4.5 %copy.118 = bf16[512,16,128]{2,1,0:T(8,128)(2,1)} copy(bf16[512,16,128]{0,2,1:T(8,128)(2,1)} %fusion.7) | data formatting | bytes 4194304
  173.8 12.7 %collective-permute-done.12 = f32[16,128,128]{2,1,0:T(8,128)} collective-permute-done((f32[16,128,128]{2,1,0:T(8,128)}, f32[16,128,128]{2,1,0:T(8,128)}, u32[]{:S(2)}, u32[]{:S(2)}) %collective-permute-start.12) | collective-permute-done | bytes 1048608 | tf_op jit(solution)/shard_map/ppermute | solution.py:17
  190.5 7.9 %fusion.55 = f32[16,128,512]{1,2,0:T(8,128)} fusion(bf16[512,16,128]{0,2,1:T(8,128)(2,1)S(1)} %subtract_convert_fusion, bf16[16,512,512]{2,1,0:T(8,128)(2,1)} %multiply_convert_fusion.1), kind=kOutput, calls=%fused_computation.99 | convolution fusion | flops 1073741824 | bytes 14680064 | tf_op jit(solution)/shard_map/while/body/eval_jaxpr/hts,thd->shd/dot_general | solution.py:21
  198.4 6.3 %fusion.27 = f32[16,512,128]{2,1,0:T(8,128)S(1)} fusion(bf16[16,512,512]{2,1,0:T(8,128)(2,1)} %multiply_convert_fusion, bf16[512,16,128]{2,1,0:T(8,128)(2,1)S(1)} %copy-done.1), kind=kOutput, calls=%fused_computation.40 | convolution fusion | flops 1073741824 | bytes 14680064 | tf_op jit(solution)/shard_map/while/body/eval_jaxpr/hts,thd->shd/dot_general | solution.py:21
  204.6 11.2 %collective-permute-done.13 = f32[16,128,128]{2,1,0:T(8,128)} collective-permute-done((f32[16,128,128]{2,1,0:T(8,128)S(1)}, f32[16,128,128]{2,1,0:T(8,128)}, u32[]{:S(2)}, u32[]{:S(2)}) %collective-permute-start.13) | collective-permute-done | bytes 1048608 | tf_op jit(solution)/shard_map/ppermute | solution.py:17
  217.3 4.3 %fusion.1 = bf16[512,16,128]{2,0,1:T(8,128)(2,1)S(1)} fusion(f32[16,128,512]{1,2,0:T(8,128)} %fusion.22, f32[16,128,512]{1,2,0:T(8,128)S(1)} %copy-done.9, bf16[16,128,128]{2,1,0:T(8,128)(2,1)S(1)} %add_convert_fusion, f32[512,16]{0,1:T(8,128)S(1)} %get-tuple-element.123, bf16[512,16,128]{2,1,0:T(8,128)(2,1)S(1)} %copy-done.4), kind=kOutput, calls=%fused_computation.5 | convolution fusion | flops 273678336 | bytes 13139968 | tf_op jit(solution)/shard_map/shd,hde->she/dot_general | solution.py:21
  221.6 2.7 %copy.120 = bf16[512,16,128]{2,1,0:T(8,128)(2,1)} copy(bf16[512,16,128]{2,0,1:T(8,128)(2,1)S(1)} %fusion.1) | data formatting | bytes 4194304
  226.4 2.7 %copy.119 = bf16[512,16,128]{2,1,0:T(8,128)(2,1)} copy(bf16[512,16,128]{2,0,1:T(8,128)(2,1)S(1)} %fusion.4) | data formatting | bytes 4194304
  (84 shorter events, 39.2 us)
Async XLA Ops:
  8.1 2.6 %copy-start.5 = (bf16[512,16,128]{2,1,0:T(8,128)(2,1)S(1)}, bf16[512,16,128]{2,1,0:T(8,128)(2,1)}, u32[]{:S(2)}) copy-start(bf16[512,16,128]{2,1,0:T(8,128)(2,1)} %param.9) | copy-start | bytes 6291460
  10.8 41.7 %copy-start = (bf16[512,16,128]{2,1,0:T(8,128)(2,1)S(1)}, bf16[512,16,128]{2,1,0:T(8,128)(2,1)}, u32[]{:S(2)}) copy-start(bf16[512,16,128]{2,1,0:T(8,128)(2,1)} %param.7) | copy-start | bytes 6291460
  10.8 41.7 %copy-start.2 = (bf16[512,16,128]{2,1,0:T(8,128)(2,1)S(1)}, bf16[512,16,128]{2,1,0:T(8,128)(2,1)}, u32[]{:S(2)}) copy-start(bf16[512,16,128]{2,1,0:T(8,128)(2,1)} %param.8) | copy-start | bytes 6291460
  12.7 16.1 %collective-permute-start.3 = (f32[16,128,128]{2,1,0:T(8,128)S(1)}, f32[16,128,128]{2,1,0:T(8,128)S(1)}, u32[]{:S(2)}, u32[]{:S(2)}) collective-permute-start(f32[16,128,128]{2,1,0:T(8,128)S(1)} %fusion.15), channel_id=1, source_target_pairs={{0,1},{1,2},{2,3},{3,4},{4,5},{5,6},{6,7},{7,8},{8,9},{9,10},{10,1... | collective-permute-start | bytes 3145736 | tf_op jit(solution)/shard_map/ppermute | solution.py:17
  28.9 16.2 %collective-permute-start.4 = (f32[16,128,128]{2,1,0:T(8,128)S(1)}, f32[16,128,128]{2,1,0:T(8,128)S(1)}, u32[]{:S(2)}, u32[]{:S(2)}) collective-permute-start(f32[16,128,128]{2,1,0:T(8,128)S(1)} %collective-permute-done.3), channel_id=1, source_target_pairs={{0,1},{1,2},{2,3},{3,4},{4,5},{5,6},{6,7},{7,8},{8,9},{9,10},{10,1... | collective-permute-start | bytes 3145736 | tf_op jit(solution)/shard_map/ppermute | solution.py:17
  30.8 14.3 %collective-permute-start = (f32[16]{0:T(128)S(1)}, f32[16]{0:T(128)S(1)}, u32[]{:S(2)}, u32[]{:S(2)}) collective-permute-start(f32[16]{0:T(128)S(1)} %get-tuple-element.141), channel_id=1, source_target_pairs={{0,1},{1,2},{2,3},{3,4},{4,5},{5,6},{6,7},{7,8},{8,9},{9,10},{10,1... | collective-permute-start | bytes 200 | tf_op jit(solution)/shard_map/ppermute | solution.py:17
  35.4 24.9 %copy-start.15 = (pred[512,512]{1,0:T(8,128)(4,1)}, pred[512,512]{1,0:T(8,128)(4,1)S(1)}, u32[]{:S(2)}) copy-start(pred[512,512]{1,0:T(8,128)(4,1)S(1)} %fusion.41) | copy-start | bytes 786436
  45.2 27.0 %collective-permute-start.5 = (f32[16,128,128]{2,1,0:T(8,128)S(1)}, f32[16,128,128]{2,1,0:T(8,128)S(1)}, u32[]{:S(2)}, u32[]{:S(2)}) collective-permute-start(f32[16,128,128]{2,1,0:T(8,128)S(1)} %multiply_add_fusion.3), channel_id=1, source_target_pairs={{0,2},{1,3},{2,4},{3,5},{4,6},{5,7},{6,8},{7,9},{8,10},{9,11},{10,... | collective-permute-start | bytes 3145736 | tf_op jit(solution)/shard_map/ppermute | solution.py:17
  50.6 9.7 %copy-start.13 = (f32[512,512]{1,0:T(8,128)}, f32[512,512]{1,0:T(8,128)S(1)}, u32[]{:S(2)}) copy-start(f32[512,512]{1,0:T(8,128)S(1)} %maximum_convert_fusion) | copy-start | bytes 3145732
  50.6 20.3 %collective-permute-start.1 = (f32[16]{0:T(128)S(1)}, f32[16]{0:T(128)S(1)}, u32[]{:S(2)}, u32[]{:S(2)}) collective-permute-start(f32[16]{0:T(128)S(1)} %collective-permute-done), channel_id=1, source_target_pairs={{0,1},{1,2},{2,3},{3,4},{4,5},{5,6},{6,7},{7,8},{8,9},{9,10},{10,1... | collective-permute-start | bytes 200 | tf_op jit(solution)/shard_map/ppermute | solution.py:17
  72.4 8.8 %copy-start.12 = (f32[16,128,128]{2,1,0:T(8,128)}, f32[16,128,128]{2,1,0:T(8,128)S(1)}, u32[]{:S(2)}) copy-start(f32[16,128,128]{2,1,0:T(8,128)S(1)} %multiply_add_fusion.2) | copy-start | bytes 3145732
  72.4 25.9 %collective-permute-start.6 = (f32[16,128,128]{2,1,0:T(8,128)S(1)}, f32[16,128,128]{2,1,0:T(8,128)}, u32[]{:S(2)}, u32[]{:S(2)}) collective-permute-start(f32[16,128,128]{2,1,0:T(8,128)S(1)} %multiply_add_fusion.2), channel_id=1, source_target_pairs={{0,4},{1,5},{2,6},{3,7},{4,8},{5,9},{6,10},{7,11},{8,12},{9,13},{1... | collective-permute-start | bytes 3145736 | tf_op jit(solution)/shard_map/ppermute | solution.py:17
  79.0 2.2 copy-start.6
  89.4 10.6 %copy-start.17 = (f32[16,128]{1,0:T(8,128)S(1)}, f32[16,128]{1,0:T(8,128)}, u32[]{:S(2)}) copy-start(f32[16,128]{1,0:T(8,128)} %param.11) | copy-start | bytes 24580
  89.4 8.0 %collective-permute-start.2 = (f32[16]{0:T(128)S(1)}, f32[16]{0:T(128)S(1)}, u32[]{:S(2)}, u32[]{:S(2)}) collective-permute-start(f32[16]{0:T(128)S(1)} %mul.394), channel_id=1, source_target_pairs={{0,2},{1,3},{2,4},{3,5},{4,6},{5,7},{6,8},{7,9},{8,10},{9,11},{10,... | collective-permute-start | bytes 200 | tf_op jit(solution)/shard_map/ppermute | solution.py:17
  111.4 3.8 %copy-start.11 = (bf16[512,16,128]{2,1,0:T(8,128)(2,1)S(1)}, bf16[512,16,128]{2,1,0:T(8,128)(2,1)}, u32[]{:S(2)}) copy-start(bf16[512,16,128]{2,1,0:T(8,128)(2,1)} %multiply_convert_fusion.2) | copy-start | bytes 6291460
  115.3 19.6 %copy-start.3 = (bf16[512,16,128]{2,1,0:T(8,128)(2,1)S(1)}, bf16[512,16,128]{2,1,0:T(8,128)(2,1)}, u32[]{:S(2)}) copy-start(bf16[512,16,128]{2,1,0:T(8,128)(2,1)} %param.8) | copy-start | bytes 6291460
  116.6 28.0 %copy-start.7 = (bf16[512,16,128]{2,1,0:T(8,128)(2,1)S(1)}, bf16[512,16,128]{2,1,0:T(8,128)(2,1)}, u32[]{:S(2)}) copy-start(bf16[512,16,128]{2,1,0:T(8,128)(2,1)} %param.9) | copy-start | bytes 6291460
  116.6 25.3 %collective-permute-start.10 = (f32[16,128,128]{2,1,0:T(8,128)S(1)}, f32[16,128,128]{2,1,0:T(8,128)S(1)}, u32[]{:S(2)}, u32[]{:S(2)}) collective-permute-start(f32[16,128,128]{2,1,0:T(8,128)S(1)} %fusion.18), channel_id=1, source_target_pairs={{1,0},{2,1},{3,2},{4,3},{5,4},{6,5},{7,6},{8,7},{9,8},{10,9},{11,1... | collective-permute-start | bytes 3145736 | tf_op jit(solution)/shard_map/ppermute | solution.py:17
  118.6 12.3 %collective-permute-start.7 = (f32[16]{0:T(128)S(1)}, f32[16]{0:T(128)S(1)}, u32[]{:S(2)}, u32[]{:S(2)}) collective-permute-start(f32[16]{0:T(128)S(1)} %get-tuple-element.98), channel_id=1, source_target_pairs={{1,0},{2,1},{3,2},{4,3},{5,4},{6,5},{7,6},{8,7},{9,8},{10,9},{11,1... | collective-permute-start | bytes 200 | tf_op jit(solution)/shard_map/ppermute | solution.py:17
  131.0 6.5 %collective-permute-start.8 = (f32[16]{0:T(128)S(1)}, f32[16]{0:T(128)S(1)}, u32[]{:S(2)}, u32[]{:S(2)}) collective-permute-start(f32[16]{0:T(128)S(1)} %collective-permute-done.7), channel_id=1, source_target_pairs={{1,0},{2,1},{3,2},{4,3},{5,4},{6,5},{7,6},{8,7},{9,8},{10,9},{11,1... | collective-permute-start | bytes 200 | tf_op jit(solution)/shard_map/ppermute | solution.py:17
  137.5 9.7 %copy-start.14 = (f32[512,512]{1,0:T(8,128)S(1)}, f32[512,512]{1,0:T(8,128)}, u32[]{:S(2)}) copy-start(f32[512,512]{1,0:T(8,128)} %copy-done.13) | copy-start | bytes 3145732
  137.5 9.7 %copy-start.16 = (pred[512,512]{1,0:T(8,128)(4,1)S(1)}, pred[512,512]{1,0:T(8,128)(4,1)}, u32[]{:S(2)}) copy-start(pred[512,512]{1,0:T(8,128)(4,1)} %copy-done.15) | copy-start | bytes 786436
  137.5 9.7 %collective-permute-start.9 = (f32[16]{0:T(128)S(1)}, f32[16]{0:T(128)S(1)}, u32[]{:S(2)}, u32[]{:S(2)}) collective-permute-start(f32[16]{0:T(128)S(1)} %mul.425), channel_id=1, source_target_pairs={{2,0},{3,1},{4,2},{5,3},{6,4},{7,5},{8,6},{9,7},{10,8},{11,9},{12,... | collective-permute-start | bytes 200 | tf_op jit(solution)/shard_map/ppermute | solution.py:17
  141.9 15.0 %collective-permute-start.11 = (f32[16,128,128]{2,1,0:T(8,128)S(1)}, f32[16,128,128]{2,1,0:T(8,128)S(1)}, u32[]{:S(2)}, u32[]{:S(2)}) collective-permute-start(f32[16,128,128]{2,1,0:T(8,128)S(1)} %collective-permute-done.10), channel_id=1, source_target_pairs={{1,0},{2,1},{3,2},{4,3},{5,4},{6,5},{7,6},{8,7},{9,8},{10,9},{11,1... | collective-permute-start | bytes 3145736 | tf_op jit(solution)/shard_map/ppermute | solution.py:17
  158.0 28.5 %collective-permute-start.12 = (f32[16,128,128]{2,1,0:T(8,128)}, f32[16,128,128]{2,1,0:T(8,128)}, u32[]{:S(2)}, u32[]{:S(2)}) collective-permute-start(f32[16,128,128]{2,1,0:T(8,128)} %multiply_add_fusion.1), channel_id=1, source_target_pairs={{2,0},{3,1},{4,2},{5,3},{6,4},{7,5},{8,6},{9,7},{10,8},{11,9},{12,... | collective-permute-start | bytes 3145736 | tf_op jit(solution)/shard_map/ppermute | solution.py:17
  188.2 10.2 %copy-start.1 = (bf16[512,16,128]{2,1,0:T(8,128)(2,1)S(1)}, bf16[512,16,128]{2,1,0:T(8,128)(2,1)}, u32[]{:S(2)}) copy-start(bf16[512,16,128]{2,1,0:T(8,128)(2,1)} %param.7) | copy-start | bytes 6291460
  188.2 27.6 %collective-permute-start.13 = (f32[16,128,128]{2,1,0:T(8,128)S(1)}, f32[16,128,128]{2,1,0:T(8,128)}, u32[]{:S(2)}, u32[]{:S(2)}) collective-permute-start(f32[16,128,128]{2,1,0:T(8,128)S(1)} %multiply_add_fusion), channel_id=1, source_target_pairs={{4,0},{5,1},{6,2},{7,3},{8,4},{9,5},{10,6},{11,7},{12,8},{13,9},{1... | collective-permute-start | bytes 3145736 | tf_op jit(solution)/shard_map/ppermute | solution.py:17
  198.4 18.9 %copy-start.4 = (bf16[512,16,128]{2,1,0:T(8,128)(2,1)S(1)}, bf16[512,16,128]{2,1,0:T(8,128)(2,1)}, u32[]{:S(2)}) copy-start(bf16[512,16,128]{2,1,0:T(8,128)(2,1)} %param.8) | copy-start | bytes 6291460
  198.4 18.9 %copy-start.9 = (f32[16,128,512]{1,2,0:T(8,128)S(1)}, f32[16,128,512]{1,2,0:T(8,128)}, u32[]{:S(2)}) copy-start(f32[16,128,512]{1,2,0:T(8,128)} %fusion.55) | copy-start | bytes 12582916
  217.3 7.0 %copy-start.10 = (f32[16,128,512]{1,2,0:T(8,128)S(1)}, f32[16,128,512]{1,2,0:T(8,128)}, u32[]{:S(2)}) copy-start(f32[16,128,512]{1,2,0:T(8,128)} %fusion.36) | copy-start | bytes 12582916
  221.6 2.7 %copy-start.8 = (bf16[512,16,128]{2,1,0:T(8,128)(2,1)S(1)}, bf16[512,16,128]{2,1,0:T(8,128)(2,1)}, u32[]{:S(2)}) copy-start(bf16[512,16,128]{2,1,0:T(8,128)(2,1)} %param.9) | copy-start | bytes 6291460
where the time goes:
time: 230 us; the launch traced here: 229 us
  waiting for transfers between devices  72 us (31%)
  matrix products  70.6 us (31%)
  starting transfers between devices  43.4 us (19%)
  other arithmetic  18.8 us (8%)
  local copies, waits for them, and re-layouts  15.7 us (7%)
  blocking collectives  4.91 us (2%)
  between operations  3.62 us (2%)
    ppermute x14, waiting for transfers between devices, passed_along(): return lax.ppermute(block, axis, route)  72 us
    dot_general x16, matrix products, mix(): jnp.einsum(form, left.astype(jnp.float32), right.astype(jnp.float32), pre...  70.6 us
    ppermute x14, starting transfers between devices, passed_along(): return lax.ppermute(block, axis, route)  43.4 us
    unnamed x40, local copies, waits for them, and re-layouts  14.2 us
    psum x1, blocking collectives, local(): squares, cross = lax.psum((squares, cross), 'head')  4.91 us
  transfers between devices with their start and end apart: 14, of which 9 were waited for; matrix products, arithmetic and copies ran while one was open for 29% of the time, Pallas kernels for 0%

commit v1 on v0

v1 whole, which is shorter than its diff:
```python
from functools import partial

import jax
import jax.numpy as jnp
from jax import lax
from jax.experimental import pallas as pl
from jax.experimental.pallas import tpu as pltpu
from jax.sharding import PartitionSpec as P

EPSILON = 1e-06
LONGEST = 4096
FAR = 1e30
F32 = jnp.float32
BF16 = jnp.bfloat16


def dot(left, right, dims):
    return lax.dot_general(left, right, (dims, ((), ())), preferred_element_type=F32)


NN = ((1,), (0,))
NT = ((1,), (1,))
TN = ((0,), (0,))


def column(tokens, width):
    return lax.broadcasted_iota(jnp.int32, (tokens, width), 0)


def put_halves(core, ref, h, mine, other):
    half = mine.shape[0]
    ref[h, pl.ds(pl.multiple_of(core * half, half), half), :] = mine.astype(ref.dtype)
    ref[h, pl.ds(pl.multiple_of((1 - core) * half, half), half), :] = other.astype(ref.dtype)


def split_halves(core, state, send_ref, keep_ref, h):
    half = state.shape[0] // 2
    low, high = state[:half], state[half:]
    keep_ref[h] = jnp.where(core == 0, low, high)
    send_ref[h] = jnp.where(core == 0, high, low)


def state_kernel(first, docs_ref, rate_ref, k_ref, v_ref, kh_ref, vh_ref, send_ref, keep_ref):
    tokens, heads, dim = k_ref.shape
    index = lax.axis_index("ctx")
    end = (index + 1) * tokens

    def scan(j, carry):
        start, last = carry
        last = jnp.where(start <= end - 1, start, last)
        return (start + docs_ref[j], last)

    _, last = lax.fori_loop(0, docs_ref.shape[0], scan, (jnp.int32(0), jnp.int32(0)))
    row = column(tokens, dim)
    distance = jnp.where(
        row + index * tokens >= last, (tokens - 1 - row).astype(F32), F32(FAR)
    )
    kh_ref[...] = jnp.swapaxes(k_ref[...], 0, 1)
    vh_ref[...] = jnp.swapaxes(v_ref[...], 0, 1)
    core = index & 1
    for h in range(heads):
        tail = jnp.exp(-rate_ref[first + h] * distance)
        faded = (kh_ref[h].astype(F32) * tail).astype(BF16)
        split_halves(core, dot(faded, vh_ref[h], TN), send_ref, keep_ref, h)


def scores_kernel(first, rows, rate_ref, q_ref, g_ref, kh_ref, vh_ref, dist_ref, qh_ref, gh_ref, out_ref, probs_ref):
    tokens, heads, dim = q_ref.shape
    qh_ref[...] = jnp.swapaxes(q_ref[...], 0, 1)
    gh_ref[...] = jnp.swapaxes(g_ref[...], 0, 1)

    def head(h, carry):
        rate = rate_ref[first + h]
        for low in range(0, tokens, rows):
            top = low + rows
            scores = dot(qh_ref[h, low:top, :], kh_ref[h, :top, :], NT)
            decay = jnp.exp(-rate * dist_ref[low:top, :top])
            probs = (scores * decay).astype(BF16)
            probs_ref[h, low:top, :top] = probs
            out_ref[h, low:top, :] = dot(probs, vh_ref[h, :top, :], NN).astype(BF16)
        return carry

    lax.fori_loop(0, heads, head, 0)


def attend_kernel(first, begin, final, info_ref, rate_ref, qh_ref, gh_ref, local_ref, gain_ref, mine_ref, other_ref, *refs):
    if not begin:
        sum_ref, refs = refs[0], refs[1:]
    attn_ref, state_ref, stats_ref = refs[:3]
    heads, tokens, dim = qh_ref.shape
    core = info_ref[0] & 1
    row = column(tokens, dim)
    distance = jnp.where(
        row + info_ref[1] < info_ref[2], (row + 1).astype(F32), F32(FAR)
    )
    if begin:
        squares = jnp.zeros((tokens, dim), F32)
        cross = jnp.zeros((tokens, dim), F32)
    else:
        squares, cross = sum_ref[0], sum_ref[1]
    for h in range(heads):
        put_halves(core, state_ref, h, mine_ref[h], other_ref[h])
        factor = jnp.exp(-rate_ref[first + h] * distance)
        attn = local_ref[h].astype(F32) + factor * dot(qh_ref[h], state_ref[h], NN)
        attn_ref[h] = attn.astype(BF16)
        squares += attn * attn
        cross += gain_ref[h : h + 1, :] * gh_ref[h].astype(F32) * attn
    if final:
        stats_ref[0:1, :] = jnp.sum(jnp.swapaxes(squares, 0, 1), axis=0, keepdims=True)
        stats_ref[1:2, :] = jnp.sum(jnp.swapaxes(cross, 0, 1), axis=0, keepdims=True)
    else:
        stats_ref[0] = squares
        stats_ref[1] = cross


def norm_kernel(first, width, parts, info_ref, rate_ref, *refs):
    stats_refs, refs = refs[:parts], refs[parts:]
    attn_ref, gh_ref, qh_ref, gain_ref, grad_ref, send_ref, keep_ref = refs
    heads, tokens, dim = qh_ref.shape
    core = info_ref[0] & 1
    stats = stats_refs[0][...]
    for ref in stats_refs[1:]:
        stats = stats + ref[...]
    squares, cross = stats[0:1, :], stats[1:2, :]
    inverse = 1.0 / jnp.sqrt(squares / width + EPSILON)
    scale = cross * inverse * inverse * inverse / width
    inverse = jnp.swapaxes(jnp.broadcast_to(inverse, (dim, tokens)), 0, 1)
    scale = jnp.swapaxes(jnp.broadcast_to(scale, (dim, tokens)), 0, 1)
    row = column(tokens, dim)
    distance = jnp.where(row + info_ref[1] < info_ref[3], row.astype(F32), F32(FAR))
    for h in range(heads):
        gained = gain_ref[h : h + 1, :] * gh_ref[h].astype(F32)
        grad = (gained * inverse - attn_ref[h].astype(F32) * scale).astype(BF16)
        grad_ref[h] = grad
        lead = jnp.exp(-rate_ref[first + h] * distance)
        faded = (qh_ref[h].astype(F32) * lead).astype(BF16)
        split_halves(core, dot(faded, grad, TN), send_ref, keep_ref, h)


def grads_kernel(first, rows, info_ref, rate_ref, grad_ref, qh_ref, kh_ref, vh_ref, probs_ref, dist_ref, state_ref, *refs):
    dq_ref, dk_ref, dv_ref, dqh_ref = refs[-4:]
    heads, tokens, dim = qh_ref.shape
    row = column(tokens, dim)
    distance = jnp.where(
        row + info_ref[1] < info_ref[2], (row + 1).astype(F32), F32(FAR)
    )

    def head(h, carry):
        rate = rate_ref[first + h]
        factor = jnp.exp(-rate * distance)
        dk = dv = None
        for low in range(tokens - rows, -1, -rows):
            top = low + rows
            grad = grad_ref[h, low:top, :]
            raw = dot(grad, vh_ref[h, :top, :], NT)
            weights = (raw * jnp.exp(-rate * dist_ref[low:top, :top])).astype(BF16)
            dq = dot(weights, kh_ref[h, :top, :], NN)
            dq += factor[low:top] * dot(grad, state_ref[h], NT)
            dqh_ref[h, low:top, :] = dq.astype(BF16)
            dk_new = dot(weights, qh_ref[h, low:top, :], TN)
            dv_new = dot(probs_ref[h, low:top, :top], grad, TN)
            if dk is not None:
                dk_new += dk[:top]
                dv_new += dv[:top]
            dk, dv = dk_new, dv_new
            dk_ref[h, low:top, :] = dk[low:top].astype(BF16)
            dv_ref[h, low:top, :] = dv[low:top].astype(BF16)
        return carry

    lax.fori_loop(0, heads, head, 0)
    dq_ref[...] = jnp.swapaxes(dqh_ref[...], 0, 1)


def finish_kernel(first, info_ref, rate_ref, kh_ref, vh_ref, dk_part_ref, dv_part_ref, mine_ref, other_ref, *refs):
    dk_ref, dv_ref, dkh_ref, dvh_ref, state_ref = refs[-5:]
    heads, tokens, dim = kh_ref.shape
    core = info_ref[0] & 1
    row = column(tokens, dim)
    distance = jnp.where(
        row + info_ref[1] >= info_ref[4], (tokens - row).astype(F32), F32(FAR)
    )
    for h in range(heads):
        put_halves(core, state_ref, h, mine_ref[h], other_ref[h])
        factor = jnp.exp(-rate_ref[first + h] * distance)
        dk = dk_part_ref[h].astype(F32) + factor * dot(vh_ref[h], state_ref[h], NT)
        dv = dv_part_ref[h].astype(F32) + factor * dot(kh_ref[h], state_ref[h], NN)
        dkh_ref[h] = dk.astype(BF16)
        dvh_ref[h] = dv.astype(BF16)
    dk_ref[...] = jnp.swapaxes(dkh_ref[...], 0, 1)
    dv_ref[...] = jnp.swapaxes(dvh_ref[...], 0, 1)


def send(block, axis, target):
    count = lax.axis_size(axis)
    route = [(i, target(i)) for i in range(count) if 0 <= target(i) < count]
    return lax.ppermute(block, axis, route)


def weight_table(index, tokens, starts, rates, rows, shift):
    xors, ands, adds, xors2, ands2, adds2 = (jnp.array(c, jnp.int32) for c in zip(*rows))
    begin = (((index ^ xors) & ands) + adds) * tokens
    end = (((index ^ xors2) & ands2) + adds2) * tokens
    seg = lambda p: jnp.sum((starts[None, :] <= (p - shift)[:, None]).astype(jnp.int32), axis=1)
    fade = jnp.exp(-rates[None, :] * jnp.abs(end - begin).astype(F32)[:, None])
    return jnp.where((seg(begin) == seg(end))[:, None], fade, F32(0.0))


def hop_count(tokens):
    return -(-LONGEST // (4 * tokens))


def forward_rows(hops):
    c, p = ~1, ~3
    rows = [
        (0, -1, 1, 0, c, 2),
        (1, -1, 1, 0, c, 2),
        (0, c, 2, 0, p, 4),
        (2, c, 2, 0, p, 4),
        (0, p, 0, 0, p, 2),
        (0, c, 0, 0, c, 1),
    ]
    return rows + [(0, p, -4 * hop, 0, p, 0) for hop in range(hops)]


def backward_rows(hops):
    c, p = ~1, ~3
    rows = [
        (0, -1, 0, 0, c, 0),
        (1, -1, 0, 0, c, 0),
        (0, c, 0, 0, p, 0),
        (2, c, 0, 0, p, 0),
        (0, p, 4, 0, p, 2),
        (0, c, 2, 0, c, 1),
    ]
    return rows + [(0, p, 4 + 4 * hop, 0, p, 4) for hop in range(hops)]


def entering_state(send_half, keep_half, table, index, forward, hops):
    core, side = index & 1, (index >> 1) & 1
    core_first = core == (0 if forward else 1)
    side_first = side == (0 if forward else 1)
    step = 4 if forward else -4
    w = [table[j][:, None, None] for j in range(table.shape[0])]
    quarter = keep_half.shape[1] // 2
    one, zero = F32(1.0), F32(0.0)
    pick = lambda block, at: jnp.where(at == 0, block[:, :quarter], block[:, quarter:])

    came_half = send(send_half, "ctx", lambda i: i ^ 1)
    chip = w[0] * keep_half + w[1] * came_half
    earlier_half = jnp.where(core_first, keep_half, came_half)

    keep_part, send_part = pick(chip, side), pick(chip, 1 - side)
    came_part = send(send_part, "ctx", lambda i: i ^ 2)
    moving = w[2] * keep_part + w[3] * came_part
    earlier_part = jnp.where(side_first, keep_part, came_part)

    total = None
    for hop in range(hops):
        moving = send(moving, "ctx", lambda i: i + step)
        total = moving if total is None else total + w[6 + hop] * moving

    later = w[4] * total + earlier_part
    own = jnp.where(side_first, total, later)
    came = send(jnp.where(side_first, later, total), "ctx", lambda i: i ^ 2)
    half = jnp.where(
        side == 0,
        jnp.concatenate([own, came], axis=1),
        jnp.concatenate([came, own], axis=1),
    )
    later_half = w[5] * half + earlier_half
    mine = jnp.where(core_first, half, later_half)
    other = send(jnp.where(core_first, later_half, half), "ctx", lambda i: i ^ 1)
    return mine, other


def head_sum_parts(stats):
    count = lax.axis_size("head")
    if count & (count - 1):
        return [stats] + [
            lax.ppermute(stats, "head", [(i, (i + d) % count) for i in range(count)])
            for d in range(1, count)
        ]
    parts, bit = [stats], 1
    while bit < count:
        stats = parts[0] if len(parts) == 1 else parts[0] + parts[1]
        parts = [stats, send(stats, "head", lambda i: i ^ bit)]
        bit *= 2
    return parts


SMEM = pl.BlockSpec(memory_space=pltpu.SMEM)


def whole(array):
    zeros = (0,) * array.ndim
    return pl.BlockSpec(array.shape, lambda i: zeros)


def run(kernel, name, args, specs, outs, out_specs=None, scratch=(), alias=None, cost=(0, 0)):
    specs = [whole(a) if s is None else s for a, s in zip(args, specs)]
    out_specs = [whole(o) if s is None else s for o, s in zip(outs, out_specs or [None] * len(outs))]
    return pl.pallas_call(
        kernel,
        out_shape=outs,
        grid=(1,),
        in_specs=specs,
        out_specs=out_specs,
        scratch_shapes=scratch,
        input_output_aliases=alias or {},
        name=name,
        cost_estimate=pl.CostEstimate(flops=cost[0], bytes_accessed=cost[1], transcendentals=0),
        compiler_params=pltpu.CompilerParams(vmem_limit_bytes=48 << 20),
    )(*args)


def local(queries, keys, values, out_grad, gain, rates, docs):
    tokens, heads, dim = queries.shape
    count = 8 if heads % 8 == 0 else heads
    chunks = range(heads // count)
    rows = tokens // 2
    hops = hop_count(tokens)
    width = heads * dim * lax.axis_size("head")
    index = lax.axis_index("ctx").astype(jnp.int32)
    base = index * tokens
    shape = lambda *s, t=BF16: jax.ShapeDtypeStruct(s, t)
    major = shape(count, tokens, dim)
    half = shape(count, dim // 2, dim, t=F32)
    token_block = lambda c: pl.BlockSpec((tokens, count, dim), lambda i: (0, c, 0))
    gain_block = lambda c: pl.BlockSpec((count, dim), lambda i: (c, 0))
    unit = count * tokens * dim

    kh, vh, sends, keeps = [], [], [], []
    for c in chunks:
        a, b, s, k = run(
            partial(state_kernel, c * count),
            f"state{c}",
            [docs, rates, keys, values],
            [SMEM, SMEM, token_block(c), token_block(c)],
            [major, major, half, half],
            cost=(2 * unit * dim, 8 * unit),
        )
        kh.append(a), vh.append(b), sends.append(s), keeps.append(k)

    order = jnp.arange(docs.shape[0], dtype=jnp.int32)
    starts = jnp.sum(jnp.where(order[None, :] < order[:, None], docs[None, :], 0), axis=1)
    inf = jnp.int32(1 << 30)
    limits = jnp.stack(
        [
            index,
            base,
            jnp.min(jnp.where(starts >= base, starts, inf)),
            jnp.min(jnp.where(starts > base, starts, inf)),
            jnp.max(jnp.where(starts <= base + tokens, starts, 0)),
        ]
    )
    spots = jnp.arange(tokens, dtype=jnp.int32)
    begins = jnp.max(
        jnp.where(starts[None, :] <= (base + spots)[:, None], starts[None, :], 0), axis=1
    )
    distance = jnp.where(
        (spots[None, :] <= spots[:, None]) & (base + spots[None, :] >= begins[:, None]),
        (spots[:, None] - spots[None, :]).astype(F32),
        F32(FAR),
    )
    ahead = weight_table(index, tokens, starts, rates, forward_rows(hops), 1)
    back = weight_table(index, tokens, starts, rates, backward_rows(hops), 0)
    part = lambda table, c: table[:, c * count : (c + 1) * count]

    qh, gh, local_out, probs = [], [], [], []
    for c in chunks:
        a, b, o, p = run(
            partial(scores_kernel, c * count, rows),
            f"scores{c}",
            [rates, queries, out_grad, kh[c], vh[c], distance],
            [SMEM, token_block(c), token_block(c), None, None, None],
            [major, major, major, shape(count, tokens, tokens)],
            cost=(4 * unit * tokens, 24 * unit),
        )
        qh.append(a), gh.append(b), local_out.append(o), probs.append(p)

    attn, states = [], []
    stats = None
    for c in chunks:
        mine, other = entering_state(sends[c], keeps[c], part(ahead, c), index, True, hops)
        begin, final = c == 0, c == chunks[-1]
        args = [limits, rates, qh[c], gh[c], local_out[c], gain, mine, other]
        specs = [SMEM, SMEM, None, None, None, gain_block(c), None, None]
        if not begin:
            args.append(stats), specs.append(None)
        a, s, stats = run(
            partial(attend_kernel, c * count, begin, final),
            f"attend{c}",
            args,
            specs,
            [major, shape(count, dim, dim), shape(2, tokens, t=F32) if final else shape(2, tokens, dim, t=F32)],
            cost=(2 * unit * dim, 12 * unit),
        )
        attn.append(a), states.append(s)
    parts = head_sum_parts(stats)

    grads, sends, keeps = [], [], []
    for c in chunks:
        g, s, k = run(
            partial(norm_kernel, c * count, width, len(parts)),
            f"norm{c}",
            [limits, rates, *parts, attn[c], gh[c], qh[c], gain],
            [SMEM, SMEM] + [None] * (len(parts) + 3) + [gain_block(c)],
            [major, half, half],
            cost=(2 * unit * dim, 8 * unit),
        )
        grads.append(g), sends.append(s), keeps.append(k)

    full = shape(tokens, heads, dim)
    dq, dk_part, dv_part = None, [], []
    for c in chunks:
        args = [limits, rates, grads[c], qh[c], kh[c], vh[c], probs[c], distance, states[c]]
        specs = [SMEM, SMEM] + [None] * 7
        alias = {}
        if dq is not None:
            alias = {len(args): 0}
            args.append(dq), specs.append(pl.BlockSpec(memory_space=pl.ANY))
        dq, a, b = run(
            partial(grads_kernel, c * count, rows),
            f"grads{c}",
            args,
            specs,
            [full, major, major],
            [token_block(c), None, None],
            scratch=[pltpu.VMEM((count, tokens, dim), BF16)],
            alias=alias,
            cost=(8 * unit * tokens, 32 * unit),
        )
        dk_part.append(a), dv_part.append(b)

    dk = dv = None
    for c in chunks:
        mine, other = entering_state(sends[c], keeps[c], part(back, c), index, False, hops)
        args = [limits, rates, kh[c], vh[c], dk_part[c], dv_part[c], mine, other]
        specs = [SMEM, SMEM] + [None] * 6
        alias = {}
        if dk is not None:
            alias = {len(args): 0, len(args) + 1: 1}
            args += [dk, dv]
            specs += [pl.BlockSpec(memory_space=pl.ANY)] * 2
        dk, dv = run(
            partial(finish_kernel, c * count),
            f"finish{c}",
            args,
            specs,
            [full, full],
            [token_block(c), token_block(c)],
            scratch=[pltpu.VMEM((count, tokens, dim), BF16)] * 2 + [pltpu.VMEM((count, dim, dim), BF16)],
            alias=alias,
            cost=(4 * unit * dim, 14 * unit),
        )
    return dq, dk, dv


def solution(mesh):
    token, head = P("ctx", "head", None), P("head")
    return jax.shard_map(
        local,
        mesh=mesh,
        in_specs=(token, token, token, token, P("head", None), head, P()),
        out_specs=(token, token, token),
        check_vma=False,
    )
```

time: 230 us -> 142 us (0.62)
  matrix products: 70.6 us -> 0 us
  Pallas kernels: 0 us -> 58.2 us
  waiting for transfers between devices: 72 us -> 26.9 us
  starting transfers between devices: 43.4 us -> 32 us
  other arithmetic: 18.8 us -> 11 us
  local copies, waits for them, and re-layouts: 15.7 us -> 10.4 us
  blocking collectives: 4.91 us -> 0 us
  between operations: 3.62 us -> 1.26 us
    dot_general x16 -> x0, matrix products: 70.6 us -> none  [mix(): jnp.einsum(form, left.astype(jnp.float32), right.astype(jnp.float32), pre...]
    pallas_call x0 -> x12, Pallas kernels: none -> 58.2 us  [run(): pl.pallas_call(kernel, out_shape=outs, grid=(1,), in_specs=specs, out_spe...]
    ppermute x14 -> x25, waiting for transfers between devices: 72 us -> 26.9 us  [send(): return lax.ppermute(block, axis, route)]
    convert_element_type x6 -> x1, other arithmetic: 11.9 us -> 0.01 us  [weight_table(): fade = jnp.exp(-rates[None, :] * jnp.abs(end - begin).astype(F32)[:, None])]
    ppermute x14 -> x25, starting transfers between devices: 43.4 us -> 32 us  [send(): return lax.ppermute(block, axis, route)]
    select_n x1 -> x14, other arithmetic: 0.09 us -> 6.87 us  [the longest x4 2.92 us: entering_state(): jnp.where(core_first, later_half, half)]
    unnamed x40 -> x72, local copies, waits for them, and re-layouts: 14.2 us -> 7.61 us
    psum x1 -> x0, blocking collectives: 4.91 us -> none  [local(): squares, cross = lax.psum((squares, cross), 'head')]
  transfers between devices with their start and end apart: 14 -> 25, of which waited for: 9 -> 13; matrix products, arithmetic and copies ran while one was open for 29% -> 10% of each run, Pallas kernels for 0% -> 35%
where the time goes in v1:
time: 142 us; the launch traced here: 140 us
  Pallas kernels  58.2 us (41%)
  starting transfers between devices  32 us (23%)
  waiting for transfers between devices  26.9 us (19%)
  other arithmetic  11 us (8%)
  local copies, waits for them, and re-layouts  10.4 us (7%)
    pallas_call x12, Pallas kernels, run(): pl.pallas_call(kernel, out_shape=outs, grid=(1,), in_specs=specs, out_spe...  58.2 us
    ppermute x25, starting transfers between devices, send(): return lax.ppermute(block, axis, route)  32 us
    ppermute x25, waiting for transfers between devices, send(): return lax.ppermute(block, axis, route)  26.9 us
    unnamed x72, local copies, waits for them, and re-layouts  7.61 us
    select_n x4, other arithmetic, entering_state(): jnp.where(core_first, later_half, half)  2.92 us
  transfers between devices with their start and end apart: 25, of which 13 were waited for; matrix products, arithmetic and copies ran while one was open for 10% of the time, Pallas kernels for 35%

profile of v1, /device:TPU:12, one launch (start us, length us, event | category | flops | bytes accessed | tf_op | source)
XLA Modules:
  0.0 139.6 jit_solution(8393007348914171729)
XLA Ops:
  0.6 1.6 %copy-done.8 = bf16[512,16,128]{2,1,0:T(8,128)(2,1)S(1)} copy-done((bf16[512,16,128]{2,1,0:T(8,128)(2,1)S(1)}, bf16[512,16,128]{2,1,0:T(8,128)(2,1)}, u32[]{:S(2)}) %copy-start.8) | copy-done | bytes 2097176
  3.5 2.9 %state1.1 = (bf16[8,512,128]{2,1,0:T(8,128)(2,1)S(1)}, bf16[8,512,128]{2,1,0:T(8,128)(2,1)S(1)}, f32[8,64,128]{2,1,0:T(8,128)S(1)}, f32[8,64,128]{2,1,0:T(8,128)S(1)}) custom-call(s32[32]{0:T(128)S(1)} %copy-done.23, f32[16]{0:T(128)S(1)} %copy-done.21, bf16[512,16,128]{2,1,0:T(8,128)(2,1)S(1)} %copy-done.8, bf16[512,16,128]{2,1,0:T(8,128)(2,1)} %v_ref.3), custom_call_target="tpu_custom_call" | custom-call | flops 134217728 | bytes 4194304 | tf_op jit(solution)/shard_map/state1/pallas_call | solution.py:302
  6.6 3.0 %state0.1 = (bf16[8,512,128]{2,1,0:T(8,128)(2,1)S(1)}, bf16[8,512,128]{2,1,0:T(8,128)(2,1)S(1)}, f32[8,64,128]{2,1,0:T(8,128)S(1)}, f32[8,64,128]{2,1,0:T(8,128)S(1)}) custom-call(s32[32]{0:T(128)S(1)} %copy-done.23, f32[16]{0:T(128)S(1)} %copy-done.21, bf16[512,16,128]{2,1,0:T(8,128)(2,1)S(1)} %copy-done.8, bf16[512,16,128]{2,1,0:T(8,128)(2,1)} %v_ref.3), custom_call_target="tpu_custom_call" | custom-call | flops 134217728 | bytes 4194304 | tf_op jit(solution)/shard_map/state0/pallas_call | solution.py:302
  14.5 1.6 %collective-permute-start.7 = (f32[8,32,128]{2,1,0:T(8,128)S(1)}, f32[8,32,128]{2,1,0:T(8,128)S(1)}, u32[]{:S(2)}, u32[]{:S(2)}) collective-permute-start(f32[8,32,128]{2,1,0:T(8,128)S(1)} %slice_select_fusion.4), channel_id=1, source_target_pairs={{0,2},{1,3},{2,0},{3,1},{4,6},{5,7},{6,4},{7,5},{8,10},{9,11},{10,... | collective-permute-start | bytes 393224 | tf_op jit(solution)/shard_map/ppermute | solution.py:196
  16.1 4.1 %collective-permute-done.1 = f32[8,32,128]{2,1,0:T(8,128)S(1)} collective-permute-done((f32[8,32,128]{2,1,0:T(8,128)S(1)}, f32[8,32,128]{2,1,0:T(8,128)S(1)}, u32[]{:S(2)}, u32[]{:S(2)}) %collective-permute-start.1) | collective-permute-done | bytes 131104 | tf_op jit(solution)/shard_map/ppermute | solution.py:196
  20.3 3.5 %collective-permute-start.2 = (f32[8,32,128]{2,1,0:T(8,128)S(1)}, f32[8,32,128]{2,1,0:T(8,128)S(1)}, u32[]{:S(2)}, u32[]{:S(2)}) collective-permute-start(f32[8,32,128]{2,1,0:T(8,128)S(1)} %multiply_add_fusion.11), channel_id=1, source_target_pairs={{0,4},{1,5},{2,6},{3,7},{4,8},{5,9},{6,10},{7,11},{8,12},{9,13},{1... | collective-permute-start | bytes 393224 | tf_op jit(solution)/shard_map/ppermute | solution.py:196
  23.9 3.5 %collective-permute-start.8 = (f32[8,32,128]{2,1,0:T(8,128)S(1)}, f32[8,32,128]{2,1,0:T(8,128)S(1)}, u32[]{:S(2)}, u32[]{:S(2)}) collective-permute-start(f32[8,32,128]{2,1,0:T(8,128)S(1)} %multiply_add_fusion.9), channel_id=1, source_target_pairs={{0,4},{1,5},{2,6},{3,7},{4,8},{5,9},{6,10},{7,11},{8,12},{9,13},{1... | collective-permute-start | bytes 393224 | tf_op jit(solution)/shard_map/ppermute | solution.py:196
  27.8 3.5 %collective-permute-start.3 = (f32[8,32,128]{2,1,0:T(8,128)S(1)}, f32[8,32,128]{2,1,0:T(8,128)S(1)}, u32[]{:S(2)}, u32[]{:S(2)}) collective-permute-start(f32[8,32,128]{2,1,0:T(8,128)S(1)} %collective-permute-done.2), channel_id=1, source_target_pairs={{0,4},{1,5},{2,6},{3,7},{4,8},{5,9},{6,10},{7,11},{8,12},{9,13},{1... | collective-permute-start | bytes 393224 | tf_op jit(solution)/shard_map/ppermute | solution.py:196
  32.5 4.0 %collective-permute-start.9 = (f32[8,32,128]{2,1,0:T(8,128)S(1)}, f32[8,32,128]{2,1,0:T(8,128)S(1)}, u32[]{:S(2)}, u32[]{:S(2)}) collective-permute-start(f32[8,32,128]{2,1,0:T(8,128)S(1)} %collective-permute-done.8), channel_id=1, source_target_pairs={{0,4},{1,5},{2,6},{3,7},{4,8},{5,9},{6,10},{7,11},{8,12},{9,13},{1... | collective-permute-start | bytes 393224 | tf_op jit(solution)/shard_map/ppermute | solution.py:196
  37.2 2.1 %collective-permute-done.9 = f32[8,32,128]{2,1,0:T(8,128)S(1)} collective-permute-done((f32[8,32,128]{2,1,0:T(8,128)S(1)}, f32[8,32,128]{2,1,0:T(8,128)S(1)}, u32[]{:S(2)}, u32[]{:S(2)}) %collective-permute-start.9) | collective-permute-done | bytes 131104 | tf_op jit(solution)/shard_map/ppermute | solution.py:196
  40.0 1.6 %collective-permute-done.4 = f32[8,32,128]{2,1,0:T(8,128)S(1)} collective-permute-done((f32[8,32,128]{2,1,0:T(8,128)S(1)}, f32[8,32,128]{2,1,0:T(8,128)S(1)}, u32[]{:S(2)}, u32[]{:S(2)}) %collective-permute-start.4) | collective-permute-done | bytes 131104 | tf_op jit(solution)/shard_map/ppermute | solution.py:196
  42.5 2.0 %collective-permute-done.10 = f32[8,32,128]{2,1,0:T(8,128)S(1)} collective-permute-done((f32[8,32,128]{2,1,0:T(8,128)S(1)}, f32[8,32,128]{2,1,0:T(8,128)S(1)}, u32[]{:S(2)}, u32[]{:S(2)}) %collective-permute-start.10) | collective-permute-done | bytes 131104 | tf_op jit(solution)/shard_map/ppermute | solution.py:196
  46.1 2.0 %stack.23.info_ref = s32[5]{0:T(128)S(1)} concatenate(s32[1]{0:T(128)} %bitcast, s32[1]{0:T(128)} %bitcast.1, s32[1]{0:T(128)} %bitcast.2, s32[1]{0:T(128)} %bitcast.3, s32[1]{0:T(128)} %bitcast.4), dimensions={0} | concatenate | bytes 40 | tf_op jit(solution)/shard_map/stack | solution.py:347
  48.1 8.8 %scores1.1 = (bf16[8,512,128]{2,1,0:T(8,128)(2,1)S(1)}, bf16[8,512,128]{2,1,0:T(8,128)(2,1)S(1)}, bf16[8,512,128]{2,1,0:T(8,128)(2,1)S(1)}, bf16[8,512,512]{2,1,0:T(8,128)(2,1)}) custom-call(f32[16]{0:T(128)S(1)} %copy-done.22, bf16[512,16,128]{2,1,0:T(8,128)(2,1)} %q_ref.3, bf16[512,16,128]{2,1,0:T(8,128)(2,1)} %g_ref.3, ...), custom_call_target="tpu_custom_call" | custom-call | flops 1073741824 | bytes 12582912 | tf_op jit(solution)/shard_map/scores1/pallas_call | solution.py:302
  56.9 8.7 %scores0.1 = (bf16[8,512,128]{2,1,0:T(8,128)(2,1)S(1)}, bf16[8,512,128]{2,1,0:T(8,128)(2,1)S(1)}, bf16[8,512,128]{2,1,0:T(8,128)(2,1)S(1)}, bf16[8,512,512]{2,1,0:T(8,128)(2,1)}) custom-call(f32[16]{0:T(128)S(1)} %copy-done.22, bf16[512,16,128]{2,1,0:T(8,128)(2,1)} %q_ref.3, bf16[512,16,128]{2,1,0:T(8,128)(2,1)} %g_ref.3, ...), custom_call_target="tpu_custom_call" | custom-call | flops 1073741824 | bytes 12582912 | tf_op jit(solution)/shard_map/scores0/pallas_call | solution.py:302
  65.6 2.0 %attend0.1 = (bf16[8,512,128]{2,1,0:T(8,128)(2,1)S(1)}, bf16[8,128,128]{2,1,0:T(8,128)(2,1)S(1)}, f32[2,512,128]{2,1,0:T(8,128)S(1)}) custom-call(s32[5]{0:T(128)S(1)} %stack.23.info_ref, f32[16]{0:T(128)S(1)} %copy-done.22, bf16[8,512,128]{2,1,0:T(8,128)(2,1)S(1)} %get-tuple-element.50.qh_ref.refs_4_, ...), custom_call_target="tpu_custom_call" | custom-call | flops 134217728 | bytes 6291456 | tf_op jit(solution)/shard_map/attend0/pallas_call | solution.py:302
  67.7 2.3 %attend1.1 = (bf16[8,512,128]{2,1,0:T(8,128)(2,1)S(1)}, bf16[8,128,128]{2,1,0:T(8,128)(2,1)S(1)}, f32[2,512]{1,0:T(2,128)S(1)}) custom-call(s32[5]{0:T(128)S(1)} %stack.23.info_ref, f32[16]{0:T(128)S(1)} %copy-done.22, bf16[8,512,128]{2,1,0:T(8,128)(2,1)S(1)} %get-tuple-element.43.qh_ref.refs_4_, bf16[8,512,128]{2,1,0:T(8,128)(2,1)S(1)} %get-tuple-element.44.gh_ref.refs_3_, ...), custom_call_target="tpu_custom_call" | custom-call | flops 134217728 | bytes 6291456 | tf_op jit(solution)/shard_map/attend1/pallas_call | solution.py:302
  72.2 2.1 %collective-permute-done.12.refs_1_ = f32[2,512]{1,0:T(2,128)S(1)} collective-permute-done((f32[2,512]{1,0:T(2,128)S(1)}, f32[2,512]{1,0:T(2,128)S(1)}, u32[]{:S(2)}, u32[]{:S(2)}) %collective-permute-start.12) | collective-permute-done | bytes 4128 | tf_op jit(solution)/shard_map/ppermute | solution.py:196
  74.3 1.9 %norm1.1 = (bf16[8,512,128]{2,1,0:T(8,128)(2,1)S(1)}, f32[8,64,128]{2,1,0:T(8,128)S(1)}, f32[8,64,128]{2,1,0:T(8,128)S(1)}) custom-call(s32[5]{0:T(128)S(1)} %stack.23.info_ref, f32[16]{0:T(128)S(1)} %copy-done.22, f32[2,512]{1,0:T(2,128)S(1)} %get-tuple-element.56.refs_0_, f32[2,512]{1,0:T(2,128)S(1)} %collective-permute-done.12.refs_1_, ...), custom_call_target="tpu_custom_call" | custom-call | flops 134217728 | bytes 4194304 | tf_op jit(solution)/shard_map/norm1/pallas_call | solution.py:302
  77.8 1.8 %norm0.1 = (bf16[8,512,128]{2,1,0:T(8,128)(2,1)S(1)}, f32[8,64,128]{2,1,0:T(8,128)S(1)}, f32[8,64,128]{2,1,0:T(8,128)S(1)}) custom-call(s32[5]{0:T(128)S(1)} %stack.23.info_ref, f32[16]{0:T(128)S(1)} %copy-done.22, f32[2,512]{1,0:T(2,128)S(1)} %get-tuple-element.56.refs_0_, f32[2,512]{1,0:T(2,128)S(1)} %collective-permute-done.12.refs_1_, ...), custom_call_target="tpu_custom_call" | custom-call | flops 134217728 | bytes 4194304 | tf_op jit(solution)/shard_map/norm0/pallas_call | solution.py:302
  83.5 4.1 %collective-permute-done.14 = f32[8,32,128]{2,1,0:T(8,128)S(1)} collective-permute-done((f32[8,32,128]{2,1,0:T(8,128)S(1)}, f32[8,32,128]{2,1,0:T(8,128)S(1)}, u32[]{:S(2)}, u32[]{:S(2)}) %collective-permute-start.14) | collective-permute-done | bytes 131104 | tf_op jit(solution)/shard_map/ppermute | solution.py:196
  88.4 1.9 %collective-permute-start.15 = (f32[8,32,128]{2,1,0:T(8,128)S(1)}, f32[8,32,128]{2,1,0:T(8,128)}, u32[]{:S(2)}, u32[]{:S(2)}) collective-permute-start(f32[8,32,128]{2,1,0:T(8,128)S(1)} %get-tuple-element.88), channel_id=1, source_target_pairs={{4,0},{5,1},{6,2},{7,3},{8,4},{9,5},{10,6},{11,7},{12,8},{13,9},{1... | collective-permute-start | bytes 393224 | tf_op jit(solution)/shard_map/ppermute | solution.py:196
  91.0 1.9 %collective-permute-start.21 = (f32[8,32,128]{2,1,0:T(8,128)}, f32[8,32,128]{2,1,0:T(8,128)}, u32[]{:S(2)}, u32[]{:S(2)}) collective-permute-start(f32[8,32,128]{2,1,0:T(8,128)} %get-tuple-element.86), channel_id=1, source_target_pairs={{4,0},{5,1},{6,2},{7,3},{8,4},{9,5},{10,6},{11,7},{12,8},{13,9},{1... | collective-permute-start | bytes 393224 | tf_op jit(solution)/shard_map/ppermute | solution.py:196
  93.0 3.3 %collective-permute-done.15 = f32[8,32,128]{2,1,0:T(8,128)} collective-permute-done((f32[8,32,128]{2,1,0:T(8,128)S(1)}, f32[8,32,128]{2,1,0:T(8,128)}, u32[]{:S(2)}, u32[]{:S(2)}) %collective-permute-start.15) | collective-permute-done | bytes 131104 | tf_op jit(solution)/shard_map/ppermute | solution.py:196
  96.3 2.1 %collective-permute-start.16 = (f32[8,32,128]{2,1,0:T(8,128)}, f32[8,32,128]{2,1,0:T(8,128)}, u32[]{:S(2)}, u32[]{:S(2)}) collective-permute-start(f32[8,32,128]{2,1,0:T(8,128)} %collective-permute-done.15), channel_id=1, source_target_pairs={{4,0},{5,1},{6,2},{7,3},{8,4},{9,5},{10,6},{11,7},{12,8},{13,9},{1... | collective-permute-start | bytes 393224 | tf_op jit(solution)/shard_map/ppermute | solution.py:196
  99.0 1.9 %collective-permute-start.22 = (f32[8,32,128]{2,1,0:T(8,128)}, f32[8,32,128]{2,1,0:T(8,128)S(1)}, u32[]{:S(2)}, u32[]{:S(2)}) collective-permute-start(f32[8,32,128]{2,1,0:T(8,128)} %collective-permute-done.21), channel_id=1, source_target_pairs={{4,0},{5,1},{6,2},{7,3},{8,4},{9,5},{10,6},{11,7},{12,8},{13,9},{1... | collective-permute-start | bytes 393224 | tf_op jit(solution)/shard_map/ppermute | solution.py:196
  100.9 3.6 %collective-permute-done.16 = f32[8,32,128]{2,1,0:T(8,128)} collective-permute-done((f32[8,32,128]{2,1,0:T(8,128)}, f32[8,32,128]{2,1,0:T(8,128)}, u32[]{:S(2)}, u32[]{:S(2)}) %collective-permute-start.16) | collective-permute-done | bytes 131104 | tf_op jit(solution)/shard_map/ppermute | solution.py:196
  109.0 1.9 %collective-permute-done.17 = f32[8,32,128]{2,1,0:T(8,128)S(1)} collective-permute-done((f32[8,32,128]{2,1,0:T(8,128)S(1)}, f32[8,32,128]{2,1,0:T(8,128)S(1)}, u32[]{:S(2)}, u32[]{:S(2)}) %collective-permute-start.17) | collective-permute-done | bytes 131104 | tf_op jit(solution)/shard_map/ppermute | solution.py:196
  112.8 10.6 %grads0.1 = (bf16[512,16,128]{2,1,0:T(8,128)(2,1)}, bf16[8,512,128]{2,1,0:T(8,128)(2,1)S(1)}, bf16[8,512,128]{2,1,0:T(8,128)(2,1)S(1)}) custom-call(s32[5]{0:T(128)S(1)} %stack.23.info_ref, f32[16]{0:T(128)S(1)} %copy-done.22, bf16[8,512,128]{2,1,0:T(8,128)(2,1)S(1)} %copy-done.12, bf16[8,512,128]{2,1,0:T(8,128)(2,1)S(1)} %get-tuple-element.50.qh_ref.refs_4_, ...), custom_call_target="tpu_custom_call" | custom-call | flops 2147483648 | bytes 16777216 | tf_op jit(solution)/shard_map/grads0/pallas_call | solution.py:302
  123.4 10.6 %grads1.1 = (bf16[512,16,128]{2,1,0:T(8,128)(2,1)}, bf16[8,512,128]{2,1,0:T(8,128)(2,1)S(1)}, bf16[8,512,128]{2,1,0:T(8,128)(2,1)S(1)}) custom-call(s32[5]{0:T(128)S(1)} %stack.23.info_ref, f32[16]{0:T(128)S(1)} %copy-done.22, bf16[8,512,128]{2,1,0:T(8,128)(2,1)S(1)} %copy-done.10, ...), custom_call_target="tpu_custom_call", output_to_operand_aliasing={{0}: (9, {})} | custom-call | flops 2147483648 | bytes 16777216 | tf_op jit(solution)/shard_map/grads1/pallas_call | solution.py:302
  134.0 2.8 %finish0.1 = (bf16[512,16,128]{2,1,0:T(8,128)(2,1)}, bf16[512,16,128]{2,1,0:T(8,128)(2,1)}) custom-call(s32[5]{0:T(128)S(1)} %stack.23.info_ref, f32[16]{0:T(128)S(1)} %copy-done.22, bf16[8,512,128]{2,1,0:T(8,128)(2,1)S(1)} %copy-done.4, bf16[8,512,128]{2,1,0:T(8,128)(2,1)S(1)} %copy-done.7, bf16[8,512,128]{2,1,0:T(8,128)(2,1)S(1)} %get-tuple-element.71.dk_part_ref, ...), custom_call_target="tpu_custom_call" | custom-call | flops 268435456 | bytes 7340032 | tf_op jit(solution)/shard_map/finish0/pallas_call | solution.py:302
  136.8 2.8 %finish1.1 = (bf16[512,16,128]{2,1,0:T(8,128)(2,1)}, bf16[512,16,128]{2,1,0:T(8,128)(2,1)}) custom-call(s32[5]{0:T(128)S(1)} %stack.23.info_ref, f32[16]{0:T(128)S(1)} %copy-done.22, bf16[8,512,128]{2,1,0:T(8,128)(2,1)S(1)} %get-tuple-element.41.kh_ref, bf16[8,512,128]{2,1,0:T(8,128)(2,1)S(1)} %copy-done.1, ...), custom_call_target="tpu_custom_call", output_to_operand_aliasing={{0}: (8, {}), {1}: (9, {})} | custom-call | flops 268435456 | bytes 7340032 | tf_op jit(solution)/shard_map/finish1/pallas_call | solution.py:302
  (136 shorter events, 27.9 us)
Async XLA Ops:
  6.4 41.7 %copy-start = (bf16[8,512,128]{2,1,0:T(8,128)(2,1)}, bf16[8,512,128]{2,1,0:T(8,128)(2,1)S(1)}, u32[]{:S(2)}) copy-start(bf16[8,512,128]{2,1,0:T(8,128)(2,1)S(1)} %get-tuple-element.42.vh_ref) | copy-start | bytes 3145732
  6.5 6.2 %collective-permute-start = (f32[8,64,128]{2,1,0:T(8,128)S(1)}, f32[8,64,128]{2,1,0:T(8,128)}, u32[]{:S(2)}, u32[]{:S(2)}) collective-permute-start(f32[8,64,128]{2,1,0:T(8,128)S(1)} %get-tuple-element.47), channel_id=1, source_target_pairs={{0,1},{1,0},{2,3},{3,2},{4,5},{5,4},{6,7},{7,6},{8,9},{9,8},{10,11... | collective-permute-start | bytes 786440 | tf_op jit(solution)/shard_map/ppermute | solution.py:196
  11.6 2.8 %collective-permute-start.6 = (f32[8,64,128]{2,1,0:T(8,128)S(1)}, f32[8,64,128]{2,1,0:T(8,128)S(1)}, u32[]{:S(2)}, u32[]{:S(2)}) collective-permute-start(f32[8,64,128]{2,1,0:T(8,128)S(1)} %get-tuple-element.54), channel_id=1, source_target_pairs={{0,1},{1,0},{2,3},{3,2},{4,5},{5,4},{6,7},{7,6},{8,9},{9,8},{10,11... | collective-permute-start | bytes 786440 | tf_op jit(solution)/shard_map/ppermute | solution.py:196
  13.8 6.4 %collective-permute-start.1 = (f32[8,32,128]{2,1,0:T(8,128)S(1)}, f32[8,32,128]{2,1,0:T(8,128)S(1)}, u32[]{:S(2)}, u32[]{:S(2)}) collective-permute-start(f32[8,32,128]{2,1,0:T(8,128)S(1)} %slice_select_fusion.6), channel_id=1, source_target_pairs={{0,2},{1,3},{2,0},{3,1},{4,6},{5,7},{6,4},{7,5},{8,10},{9,11},{10,... | collective-permute-start | bytes 393224 | tf_op jit(solution)/shard_map/ppermute | solution.py:196
  14.4 27.2 %copy-start.24 = (f32[8,64,128]{2,1,0:T(8,128)}, f32[8,64,128]{2,1,0:T(8,128)S(1)}, u32[]{:S(2)}) copy-start(f32[8,64,128]{2,1,0:T(8,128)S(1)} %collective-permute-done.6) | copy-start | bytes 786436
  14.5 9.3 %collective-permute-start.7 = (f32[8,32,128]{2,1,0:T(8,128)S(1)}, f32[8,32,128]{2,1,0:T(8,128)S(1)}, u32[]{:S(2)}, u32[]{:S(2)}) collective-permute-start(f32[8,32,128]{2,1,0:T(8,128)S(1)} %slice_select_fusion.4), channel_id=1, source_target_pairs={{0,2},{1,3},{2,0},{3,1},{4,6},{5,7},{6,4},{7,5},{8,10},{9,11},{10,... | collective-permute-start | bytes 393224 | tf_op jit(solution)/shard_map/ppermute | solution.py:196
  20.3 7.4 %collective-permute-start.2 = (f32[8,32,128]{2,1,0:T(8,128)S(1)}, f32[8,32,128]{2,1,0:T(8,128)S(1)}, u32[]{:S(2)}, u32[]{:S(2)}) collective-permute-start(f32[8,32,128]{2,1,0:T(8,128)S(1)} %multiply_add_fusion.11), channel_id=1, source_target_pairs={{0,4},{1,5},{2,6},{3,7},{4,8},{5,9},{6,10},{7,11},{8,12},{9,13},{1... | collective-permute-start | bytes 393224 | tf_op jit(solution)/shard_map/ppermute | solution.py:196
  23.9 8.5 %collective-permute-start.8 = (f32[8,32,128]{2,1,0:T(8,128)S(1)}, f32[8,32,128]{2,1,0:T(8,128)S(1)}, u32[]{:S(2)}, u32[]{:S(2)}) collective-permute-start(f32[8,32,128]{2,1,0:T(8,128)S(1)} %multiply_add_fusion.9), channel_id=1, source_target_pairs={{0,4},{1,5},{2,6},{3,7},{4,8},{5,9},{6,10},{7,11},{8,12},{9,13},{1... | collective-permute-start | bytes 393224 | tf_op jit(solution)/shard_map/ppermute | solution.py:196
  27.8 8.7 %collective-permute-start.3 = (f32[8,32,128]{2,1,0:T(8,128)S(1)}, f32[8,32,128]{2,1,0:T(8,128)S(1)}, u32[]{:S(2)}, u32[]{:S(2)}) collective-permute-start(f32[8,32,128]{2,1,0:T(8,128)S(1)} %collective-permute-done.2), channel_id=1, source_target_pairs={{0,4},{1,5},{2,6},{3,7},{4,8},{5,9},{6,10},{7,11},{8,12},{9,13},{1... | collective-permute-start | bytes 393224 | tf_op jit(solution)/shard_map/ppermute | solution.py:196
  32.5 6.9 %collective-permute-start.9 = (f32[8,32,128]{2,1,0:T(8,128)S(1)}, f32[8,32,128]{2,1,0:T(8,128)S(1)}, u32[]{:S(2)}, u32[]{:S(2)}) collective-permute-start(f32[8,32,128]{2,1,0:T(8,128)S(1)} %collective-permute-done.8), channel_id=1, source_target_pairs={{0,4},{1,5},{2,6},{3,7},{4,8},{5,9},{6,10},{7,11},{8,12},{9,13},{1... | collective-permute-start | bytes 393224 | tf_op jit(solution)/shard_map/ppermute | solution.py:196
  36.5 11.7 %copy-start.22 = (f32[16]{0:T(128)S(1)}, f32[16]{0:T(128)}, u32[]{:S(2)}) copy-start(f32[16]{0:T(128)} %rate_ref.23) | copy-start | bytes 196
  36.6 5.0 %collective-permute-start.4 = (f32[8,32,128]{2,1,0:T(8,128)S(1)}, f32[8,32,128]{2,1,0:T(8,128)S(1)}, u32[]{:S(2)}, u32[]{:S(2)}) collective-permute-start(f32[8,32,128]{2,1,0:T(8,128)S(1)} %get-tuple-element.100), channel_id=1, source_target_pairs={{0,2},{1,3},{2,0},{3,1},{4,6},{5,7},{6,4},{7,5},{8,10},{9,11},{10,... | collective-permute-start | bytes 393224 | tf_op jit(solution)/shard_map/ppermute | solution.py:196
  39.4 5.0 %collective-permute-start.10 = (f32[8,32,128]{2,1,0:T(8,128)S(1)}, f32[8,32,128]{2,1,0:T(8,128)S(1)}, u32[]{:S(2)}, u32[]{:S(2)}) collective-permute-start(f32[8,32,128]{2,1,0:T(8,128)S(1)} %get-tuple-element.98), channel_id=1, source_target_pairs={{0,2},{1,3},{2,0},{3,1},{4,6},{5,7},{6,4},{7,5},{8,10},{9,11},{10,... | collective-permute-start | bytes 393224 | tf_op jit(solution)/shard_map/ppermute | solution.py:196
  42.4 25.2 %collective-permute-start.5 = (f32[8,64,128]{2,1,0:T(8,128)}, f32[8,64,128]{2,1,0:T(8,128)}, u32[]{:S(2)}, u32[]{:S(2)}) collective-permute-start(f32[8,64,128]{2,1,0:T(8,128)} %get-tuple-element.96), channel_id=1, source_target_pairs={{0,1},{1,0},{2,3},{3,2},{4,5},{5,4},{6,7},{7,6},{8,9},{9,8},{10,11... | collective-permute-start | bytes 786440 | tf_op jit(solution)/shard_map/ppermute | solution.py:196
  45.4 20.2 %collective-permute-start.11 = (f32[8,64,128]{2,1,0:T(8,128)}, f32[8,64,128]{2,1,0:T(8,128)}, u32[]{:S(2)}, u32[]{:S(2)}) collective-permute-start(f32[8,64,128]{2,1,0:T(8,128)} %get-tuple-element.94), channel_id=1, source_target_pairs={{0,1},{1,0},{2,3},{3,2},{4,5},{5,4},{6,7},{7,6},{8,9},{9,8},{10,11... | collective-permute-start | bytes 786440 | tf_op jit(solution)/shard_map/ppermute | solution.py:196
  70.7 3.6 %collective-permute-start.12 = (f32[2,512]{1,0:T(2,128)S(1)}, f32[2,512]{1,0:T(2,128)S(1)}, u32[]{:S(2)}, u32[]{:S(2)}) collective-permute-start(f32[2,512]{1,0:T(2,128)S(1)} %get-tuple-element.56.refs_0_), channel_id=1, source_target_pairs={{0,16},{16,0},{1,17},{17,1},{2,18},{18,2},{3,19},{19,3},{4,20},{20... | collective-permute-start | bytes 12296 | tf_op jit(solution)/shard_map/ppermute | solution.py:196
  77.1 4.0 %collective-permute-start.13 = (f32[8,64,128]{2,1,0:T(8,128)S(1)}, f32[8,64,128]{2,1,0:T(8,128)S(1)}, u32[]{:S(2)}, u32[]{:S(2)}) collective-permute-start(f32[8,64,128]{2,1,0:T(8,128)S(1)} %get-tuple-element.70), channel_id=1, source_target_pairs={{0,1},{1,0},{2,3},{3,2},{4,5},{5,4},{6,7},{7,6},{8,9},{9,8},{10,11... | collective-permute-start | bytes 786440 | tf_op jit(solution)/shard_map/ppermute | solution.py:196
  80.6 1.7 %collective-permute-start.19 = (f32[8,64,128]{2,1,0:T(8,128)S(1)}, f32[8,64,128]{2,1,0:T(8,128)S(1)}, u32[]{:S(2)}, u32[]{:S(2)}) collective-permute-start(f32[8,64,128]{2,1,0:T(8,128)S(1)} %get-tuple-element.74), channel_id=1, source_target_pairs={{0,1},{1,0},{2,3},{3,2},{4,5},{5,4},{6,7},{7,6},{8,9},{9,8},{10,11... | collective-permute-start | bytes 786440 | tf_op jit(solution)/shard_map/ppermute | solution.py:196
  81.2 6.4 %collective-permute-start.14 = (f32[8,32,128]{2,1,0:T(8,128)S(1)}, f32[8,32,128]{2,1,0:T(8,128)S(1)}, u32[]{:S(2)}, u32[]{:S(2)}) collective-permute-start(f32[8,32,128]{2,1,0:T(8,128)S(1)} %slice_select_fusion.2), channel_id=1, source_target_pairs={{0,2},{1,3},{2,0},{3,1},{4,6},{5,7},{6,4},{7,5},{8,10},{9,11},{10,... | collective-permute-start | bytes 393224 | tf_op jit(solution)/shard_map/ppermute | solution.py:196
  82.4 7.9 %collective-permute-start.20 = (f32[8,32,128]{2,1,0:T(8,128)S(1)}, f32[8,32,128]{2,1,0:T(8,128)S(1)}, u32[]{:S(2)}, u32[]{:S(2)}) collective-permute-start(f32[8,32,128]{2,1,0:T(8,128)S(1)} %slice_select_fusion), channel_id=1, source_target_pairs={{0,2},{1,3},{2,0},{3,1},{4,6},{5,7},{6,4},{7,5},{8,10},{9,11},{10,... | collective-permute-start | bytes 393224 | tf_op jit(solution)/shard_map/ppermute | solution.py:196
  88.4 7.9 %collective-permute-start.15 = (f32[8,32,128]{2,1,0:T(8,128)S(1)}, f32[8,32,128]{2,1,0:T(8,128)}, u32[]{:S(2)}, u32[]{:S(2)}) collective-permute-start(f32[8,32,128]{2,1,0:T(8,128)S(1)} %get-tuple-element.88), channel_id=1, source_target_pairs={{4,0},{5,1},{6,2},{7,3},{8,4},{9,5},{10,6},{11,7},{12,8},{13,9},{1... | collective-permute-start | bytes 393224 | tf_op jit(solution)/shard_map/ppermute | solution.py:196
  91.0 8.0 %collective-permute-start.21 = (f32[8,32,128]{2,1,0:T(8,128)}, f32[8,32,128]{2,1,0:T(8,128)}, u32[]{:S(2)}, u32[]{:S(2)}) collective-permute-start(f32[8,32,128]{2,1,0:T(8,128)} %get-tuple-element.86), channel_id=1, source_target_pairs={{4,0},{5,1},{6,2},{7,3},{8,4},{9,5},{10,6},{11,7},{12,8},{13,9},{1... | collective-permute-start | bytes 393224 | tf_op jit(solution)/shard_map/ppermute | solution.py:196
  96.3 8.3 %collective-permute-start.16 = (f32[8,32,128]{2,1,0:T(8,128)}, f32[8,32,128]{2,1,0:T(8,128)}, u32[]{:S(2)}, u32[]{:S(2)}) collective-permute-start(f32[8,32,128]{2,1,0:T(8,128)} %collective-permute-done.15), channel_id=1, source_target_pairs={{4,0},{5,1},{6,2},{7,3},{8,4},{9,5},{10,6},{11,7},{12,8},{13,9},{1... | collective-permute-start | bytes 393224 | tf_op jit(solution)/shard_map/ppermute | solution.py:196
  98.4 14.2 %copy-start.14 = (f32[8,64,128]{2,1,0:T(8,128)S(1)}, f32[8,64,128]{2,1,0:T(8,128)}, u32[]{:S(2)}) copy-start(f32[8,64,128]{2,1,0:T(8,128)} %copy-done.13) | copy-start | bytes 786436
  98.4 14.2 %copy-start.27 = (f32[8,64,128]{2,1,0:T(8,128)S(1)}, f32[8,64,128]{2,1,0:T(8,128)}, u32[]{:S(2)}) copy-start(f32[8,64,128]{2,1,0:T(8,128)} %copy-done.26) | copy-start | bytes 786436
  99.0 7.4 %collective-permute-start.22 = (f32[8,32,128]{2,1,0:T(8,128)}, f32[8,32,128]{2,1,0:T(8,128)S(1)}, u32[]{:S(2)}, u32[]{:S(2)}) collective-permute-start(f32[8,32,128]{2,1,0:T(8,128)} %collective-permute-done.21), channel_id=1, source_target_pairs={{4,0},{5,1},{6,2},{7,3},{8,4},{9,5},{10,6},{11,7},{12,8},{13,9},{1... | collective-permute-start | bytes 393224 | tf_op jit(solution)/shard_map/ppermute | solution.py:196
  105.8 5.0 %collective-permute-start.17 = (f32[8,32,128]{2,1,0:T(8,128)S(1)}, f32[8,32,128]{2,1,0:T(8,128)S(1)}, u32[]{:S(2)}, u32[]{:S(2)}) collective-permute-start(f32[8,32,128]{2,1,0:T(8,128)S(1)} %get-tuple-element.104), channel_id=1, source_target_pairs={{0,2},{1,3},{2,0},{3,1},{4,6},{5,7},{6,4},{7,5},{8,10},{9,11},{10,... | collective-permute-start | bytes 393224 | tf_op jit(solution)/shard_map/ppermute | solution.py:196
  107.5 5.0 %collective-permute-start.23 = (f32[8,32,128]{2,1,0:T(8,128)S(1)}, f32[8,32,128]{2,1,0:T(8,128)S(1)}, u32[]{:S(2)}, u32[]{:S(2)}) collective-permute-start(f32[8,32,128]{2,1,0:T(8,128)S(1)} %get-tuple-element.102), channel_id=1, source_target_pairs={{0,2},{1,3},{2,0},{3,1},{4,6},{5,7},{6,4},{7,5},{8,10},{9,11},{10,... | collective-permute-start | bytes 393224 | tf_op jit(solution)/shard_map/ppermute | solution.py:196
  111.9 24.9 %collective-permute-start.18 = (f32[8,64,128]{2,1,0:T(8,128)S(1)}, f32[8,64,128]{2,1,0:T(8,128)S(1)}, u32[]{:S(2)}, u32[]{:S(2)}) collective-permute-start(f32[8,64,128]{2,1,0:T(8,128)S(1)} %get-tuple-element.92), channel_id=1, source_target_pairs={{0,1},{1,0},{2,3},{3,2},{4,5},{5,4},{6,7},{7,6},{8,9},{9,8},{10,11... | collective-permute-start | bytes 786440 | tf_op jit(solution)/shard_map/ppermute | solution.py:196
  112.7 21.3 %collective-permute-start.24 = (f32[8,64,128]{2,1,0:T(8,128)S(1)}, f32[8,64,128]{2,1,0:T(8,128)S(1)}, u32[]{:S(2)}, u32[]{:S(2)}) collective-permute-start(f32[8,64,128]{2,1,0:T(8,128)S(1)} %get-tuple-element.90), channel_id=1, source_target_pairs={{0,1},{1,0},{2,3},{3,2},{4,5},{5,4},{6,7},{7,6},{8,9},{9,8},{10,11... | collective-permute-start | bytes 786440 | tf_op jit(solution)/shard_map/ppermute | solution.py:196
  112.8 10.6 %copy-start.10 = (bf16[8,512,128]{2,1,0:T(8,128)(2,1)S(1)}, bf16[8,512,128]{2,1,0:T(8,128)(2,1)}, u32[]{:S(2)}) copy-start(bf16[8,512,128]{2,1,0:T(8,128)(2,1)} %copy-done.9) | copy-start | bytes 3145732
  112.8 10.6 %copy-start.19 = (bf16[8,128,128]{2,1,0:T(8,128)(2,1)S(1)}, bf16[8,128,128]{2,1,0:T(8,128)(2,1)}, u32[]{:S(2)}) copy-start(bf16[8,128,128]{2,1,0:T(8,128)(2,1)} %copy-done.18) | copy-start | bytes 786436
  (29 other events, 148.1 us)

commit v2 on v1

v2 whole, which is shorter than its diff:
```python
from functools import partial

import jax
import jax.numpy as jnp
from jax import lax
from jax.experimental import pallas as pl
from jax.experimental.pallas import tpu as pltpu
from jax.sharding import PartitionSpec as P


EPSILON = 1e-06
LONGEST = 4096
FAR = 1e30
APART = 1 << 30
F32 = jnp.float32
BF16 = jnp.bfloat16


def dot(left, right, dims):
    return lax.dot_general(left, right, (dims, ((), ())), preferred_element_type=F32)


NN = ((1,), (0,))
NT = ((1,), (1,))
TN = ((0,), (0,))


def column(tokens, width):
    return lax.broadcasted_iota(jnp.int32, (tokens, width), 0)


def put_halves(core, ref, h, mine, other):
    half = mine.shape[0]
    ref[h, pl.ds(pl.multiple_of(core * half, half), half), :] = mine.astype(ref.dtype)
    ref[h, pl.ds(pl.multiple_of((1 - core) * half, half), half), :] = other.astype(ref.dtype)


def split_halves(core, state, send_ref, keep_ref, h):
    half = state.shape[0] // 2
    low, high = state[:half], state[half:]
    keep_ref[h] = jnp.where(core == 0, low, high)
    send_ref[h] = jnp.where(core == 0, high, low)


INDEX, BASE, NEXT_START, LATER_START, NEXT_BEGIN, FADES = range(6)


def fade_rows(hops):
    c, p = ~1, ~3
    ahead = [
        (0, -1, 1, 0, c, 2),
        (1, -1, 1, 0, c, 2),
        (0, c, 2, 0, p, 4),
        (2, c, 2, 0, p, 4),
        (0, p, 0, 0, p, 2),
        (0, c, 0, 0, c, 1),
    ]
    back = [
        (0, -1, 0, 0, c, 0),
        (1, -1, 0, 0, c, 0),
        (0, c, 0, 0, p, 0),
        (2, c, 0, 0, p, 0),
        (0, p, 4, 0, p, 2),
        (0, c, 2, 0, c, 1),
    ]
    ahead += [(0, p, -4 * hop, 0, p, 0) for hop in range(1, hops)]
    back += [(0, p, 4 + 4 * hop, 0, p, 4) for hop in range(1, hops)]
    return ahead, back


def setup_kernel(hops, docs_ref, info_ref, dist_ref, begin_ref):
    tokens = dist_ref.shape[0]
    lanes = begin_ref.shape[1]
    index = lax.axis_index("ctx").astype(jnp.int32)
    base = index * tokens
    ahead, back = fade_rows(hops)
    spot = lambda x, a, d: (((index ^ x) & a) + d) * tokens
    spans = [(spot(*row[:3]), spot(*row[3:])) for row in ahead + back]
    tops = [end - 1 for _, end in spans[: len(ahead)]] + [begin for begin, _ in spans[len(ahead) :]]
    tops.append(base + tokens)
    row = column(tokens, lanes)
    begin_ref[...] = jnp.zeros_like(begin_ref)

    def doc(j, carry):
        start, upper, later, seen = carry
        upper = jnp.where((start >= base) & (start < upper), start, upper)
        later = jnp.where((start > base) & (start < later), start, later)
        seen = tuple(jnp.where(start <= top, start, old) for top, old in zip(tops, seen))

        @pl.when((start > base) & (start < base + tokens))
        def _():
            begin_ref[...] = jnp.where(row >= start - base, start - base, begin_ref[...])

        return start + docs_ref[j], upper, later, seen

    zero = jnp.int32(0)
    far = jnp.int32(APART)
    _, upper, later, seen = lax.fori_loop(
        0, docs_ref.shape[0], doc, (zero, far, far, (zero,) * len(tops))
    )
    info_ref[INDEX] = index
    info_ref[BASE] = base
    info_ref[NEXT_START] = upper
    info_ref[LATER_START] = later
    info_ref[NEXT_BEGIN] = seen[-1]
    for j, ((begin, end), last) in enumerate(zip(spans, seen)):
        forward = j < len(ahead)
        joined = last < begin if forward else last <= end
        info_ref[FADES + j] = jnp.where(joined, end - begin if forward else begin - end, far)

    for low in range(0, tokens, lanes):
        spots = low + lax.broadcasted_iota(jnp.int32, (tokens, lanes), 1)
        allowed = (spots <= row) & (spots >= begin_ref[...])
        dist_ref[:, low : low + lanes] = jnp.where(allowed, (row - spots).astype(F32), F32(FAR))


def fade(rate, distance, shape):
    return jnp.exp(jnp.full(shape, -rate * distance.astype(F32), F32))


def spread(factor, block):
    return (block.reshape(-1, *factor.shape) * factor[None]).reshape(block.shape)


TILE = (8, 128)


def chip_kernel(at, info_ref, rate_ref, keep_ref, came_ref, keep_part_ref, send_part_ref):
    heads, quarter, _ = keep_part_ref.shape
    side = (info_ref[INDEX] >> 1) & 1
    for h in range(heads):
        rate = rate_ref[h]
        mine = fade(rate, info_ref[at], TILE)
        theirs = fade(rate, info_ref[at + 1], TILE)
        chip = spread(mine, keep_ref[h]) + spread(theirs, came_ref[h])
        low, high = chip[:quarter], chip[quarter:]
        keep_part_ref[h] = jnp.where(side == 0, low, high)
        send_part_ref[h] = jnp.where(side == 0, high, low)


def plane_kernel(at, info_ref, rate_ref, keep_ref, came_ref, out_ref):
    for h in range(out_ref.shape[0]):
        rate = rate_ref[h]
        mine = fade(rate, info_ref[at + 2], TILE)
        theirs = fade(rate, info_ref[at + 3], TILE)
        out_ref[h] = spread(mine, keep_ref[h]) + spread(theirs, came_ref[h])


def part_kernel(at, hops, first_side, info_ref, rate_ref, keep_ref, came_ref, *refs):
    moved, (own_ref, send_ref) = refs[:hops], refs[hops:]
    is_first = ((info_ref[INDEX] >> 1) & 1) == first_side
    for h in range(own_ref.shape[0]):
        rate = rate_ref[h]
        total = moved[0][h]
        for hop in range(1, hops):
            total += spread(fade(rate, info_ref[at + 5 + hop], TILE), moved[hop][h])
        earlier = jnp.where(is_first, keep_ref[h], came_ref[h])
        later = spread(fade(rate, info_ref[at + 4], TILE), total) + earlier
        own_ref[h] = jnp.where(is_first, total, later)
        send_ref[h] = jnp.where(is_first, later, total)


def half_kernel(at, first_core, info_ref, rate_ref, keep_ref, came_ref, own_ref, came_part_ref, mine_ref, send_ref):
    heads = own_ref.shape[0]
    index = info_ref[INDEX]
    is_first = (index & 1) == first_core
    low_side = ((index >> 1) & 1) == 0
    for h in range(heads):
        own, came = own_ref[h], came_part_ref[h]
        half = jnp.concatenate(
            [jnp.where(low_side, own, came), jnp.where(low_side, came, own)], axis=0
        )
        earlier = jnp.where(is_first, keep_ref[h], came_ref[h])
        later = spread(fade(rate_ref[h], info_ref[at + 5], TILE), half) + earlier
        mine_ref[h] = jnp.where(is_first, half, later).astype(BF16)
        send_ref[h] = jnp.where(is_first, later, half)


def state_kernel(docs_ref, rate_ref, k_ref, v_ref, kh_ref, vh_ref, send_ref, keep_ref):
    tokens, heads, dim = k_ref.shape
    first = pl.program_id(0) * heads
    index = lax.axis_index("ctx")
    end = (index + 1) * tokens

    def scan(j, carry):
        start, last = carry
        last = jnp.where(start <= end - 1, start, last)
        return (start + docs_ref[j], last)

    _, last = lax.fori_loop(0, docs_ref.shape[0], scan, (jnp.int32(0), jnp.int32(0)))
    row = column(tokens, dim)
    distance = jnp.where(
        row + index * tokens >= last, (tokens - 1 - row).astype(F32), F32(FAR)
    )
    turned_k = jnp.swapaxes(k_ref[...], 0, 1)
    turned_v = jnp.swapaxes(v_ref[...], 0, 1)
    kh_ref[pl.ds(first, heads)] = turned_k
    vh_ref[pl.ds(first, heads)] = turned_v
    core = index & 1
    for h in range(heads):
        tail = jnp.exp(-rate_ref[first + h] * distance)
        faded = (turned_k[h].astype(F32) * tail).astype(BF16)
        split_halves(core, dot(faded, turned_v[h], TN), send_ref, keep_ref, h)


def turn_kernel(q_ref, g_ref, qh_ref, gh_ref):
    heads = q_ref.shape[1]
    here = pl.ds(pl.program_id(0) * heads, heads)
    qh_ref[here] = jnp.swapaxes(q_ref[...], 0, 1)
    gh_ref[here] = jnp.swapaxes(g_ref[...], 0, 1)


def scores_kernel(first, rows, rate_ref, qh_ref, kh_ref, vh_ref, dist_ref, out_ref, probs_ref):
    heads, tokens, _ = out_ref.shape

    def head(h, carry):
        full = first + h
        rate = rate_ref[full]
        for low in range(0, tokens, rows):
            top = low + rows
            scores = dot(qh_ref[full, low:top, :], kh_ref[full, :top, :], NT)
            decay = jnp.exp(-rate * dist_ref[low:top, :top])
            probs = (scores * decay).astype(BF16)
            probs_ref[h, low:top, :top] = probs
            out_ref[h, low:top, :] = dot(probs, vh_ref[full, :top, :], NN).astype(BF16)
        return carry

    lax.fori_loop(0, heads, head, 0)


def attend_kernel(groups, info_ref, rate_ref, qh_ref, gh_ref, gain_ref, mine_ref, other_ref, *refs):
    local_refs, (attn_ref, state_ref, stats_ref) = refs[:groups], refs[groups:]
    heads, tokens, dim = qh_ref.shape
    count = heads // groups
    core = info_ref[INDEX] & 1
    row = column(tokens, dim)
    distance = jnp.where(
        row + info_ref[BASE] < info_ref[NEXT_START], (row + 1).astype(F32), F32(FAR)
    )
    squares = jnp.zeros((tokens, dim), F32)
    cross = jnp.zeros((tokens, dim), F32)
    for h in range(heads):
        put_halves(core, state_ref, h, mine_ref[h], other_ref[h])
        factor = jnp.exp(-rate_ref[h] * distance)
        near = local_refs[h // count][h % count].astype(F32)
        attn = near + factor * dot(qh_ref[h], state_ref[h], NN)
        attn_ref[h] = attn.astype(BF16)
        squares += attn * attn
        cross += gain_ref[h : h + 1, :] * gh_ref[h].astype(F32) * attn
    stats_ref[0:1, :] = jnp.sum(jnp.swapaxes(squares, 0, 1), axis=0, keepdims=True)
    stats_ref[1:2, :] = jnp.sum(jnp.swapaxes(cross, 0, 1), axis=0, keepdims=True)


def norm_kernel(width, parts, info_ref, rate_ref, *refs):
    stats_refs, refs = refs[:parts], refs[parts:]
    attn_ref, gh_ref, qh_ref, gain_ref, grad_ref, send_ref, keep_ref = refs
    heads, tokens, dim = qh_ref.shape
    core = info_ref[INDEX] & 1
    stats = stats_refs[0][...]
    for ref in stats_refs[1:]:
        stats = stats + ref[...]
    squares, cross = stats[0:1, :], stats[1:2, :]
    inverse = 1.0 / jnp.sqrt(squares / width + EPSILON)
    scale = cross * inverse * inverse * inverse / width
    inverse = jnp.swapaxes(jnp.broadcast_to(inverse, (dim, tokens)), 0, 1)
    scale = jnp.swapaxes(jnp.broadcast_to(scale, (dim, tokens)), 0, 1)
    row = column(tokens, dim)
    distance = jnp.where(row + info_ref[BASE] < info_ref[LATER_START], row.astype(F32), F32(FAR))
    for h in range(heads):
        gained = gain_ref[h : h + 1, :] * gh_ref[h].astype(F32)
        grad = (gained * inverse - attn_ref[h].astype(F32) * scale).astype(BF16)
        grad_ref[h] = grad
        lead = jnp.exp(-rate_ref[h] * distance)
        faded = (qh_ref[h].astype(F32) * lead).astype(BF16)
        split_halves(core, dot(faded, grad, TN), send_ref, keep_ref, h)


def grads_kernel(first, rows, info_ref, rate_ref, grad_ref, qh_ref, kh_ref, vh_ref, probs_ref, dist_ref, state_ref, dq_ref, dk_ref, dv_ref):
    heads, tokens, dim = dq_ref.shape
    row = column(tokens, dim)
    distance = jnp.where(
        row + info_ref[BASE] < info_ref[NEXT_START], (row + 1).astype(F32), F32(FAR)
    )

    def head(h, carry):
        full = first + h
        rate = rate_ref[full]
        factor = jnp.exp(-rate * distance)
        dk = dv = None
        for low in range(tokens - rows, -1, -rows):
            top = low + rows
            grad = grad_ref[full, low:top, :]
            raw = dot(grad, vh_ref[full, :top, :], NT)
            weights = (raw * jnp.exp(-rate * dist_ref[low:top, :top])).astype(BF16)
            dq = dot(weights, kh_ref[full, :top, :], NN)
            dq += factor[low:top] * dot(grad, state_ref[full], NT)
            dq_ref[h, low:top, :] = dq.astype(BF16)
            dk_new = dot(weights, qh_ref[full, low:top, :], TN)
            dv_new = dot(probs_ref[h, low:top, :top], grad, TN)
            if dk is not None:
                dk_new += dk[:top]
                dv_new += dv[:top]
            dk, dv = dk_new, dv_new
            dk_ref[h, low:top, :] = dk[low:top].astype(BF16)
            dv_ref[h, low:top, :] = dv[low:top].astype(BF16)
        return carry

    lax.fori_loop(0, heads, head, 0)


def turn_back_kernel(steps, *refs):
    parts, out_ref = refs[:-1], refs[-1]
    each = len(parts) // steps
    for s in range(steps):

        @pl.when(pl.program_id(0) == s)
        def _():
            block = [ref[...] for ref in parts[s * each : (s + 1) * each]]
            out_ref[...] = jnp.swapaxes(jnp.concatenate(block, axis=0), 0, 1)


def finish_kernel(groups, info_ref, rate_ref, kh_ref, vh_ref, mine_ref, other_ref, *refs):
    dk_parts, dv_parts = refs[:groups], refs[groups : 2 * groups]
    dk_ref, dv_ref, dkh_ref, dvh_ref, state_ref = refs[2 * groups :]
    heads, tokens, dim = dkh_ref.shape
    count = dk_parts[0].shape[0]
    core = info_ref[INDEX] & 1
    row = column(tokens, dim)
    distance = jnp.where(
        row + info_ref[BASE] >= info_ref[NEXT_BEGIN], (tokens - row).astype(F32), F32(FAR)
    )
    for s in range(groups * count // heads):

        @pl.when(pl.program_id(0) == s)
        def _():
            for h in range(heads):
                full = s * heads + h
                put_halves(core, state_ref, h, mine_ref[h], other_ref[h])
                factor = jnp.exp(-rate_ref[full] * distance)
                dk = dk_parts[full // count][full % count].astype(F32)
                dv = dv_parts[full // count][full % count].astype(F32)
                dk += factor * dot(vh_ref[full], state_ref[h], NT)
                dv += factor * dot(kh_ref[full], state_ref[h], NN)
                dkh_ref[h] = dk.astype(BF16)
                dvh_ref[h] = dv.astype(BF16)
            dk_ref[...] = jnp.swapaxes(dkh_ref[...], 0, 1)
            dv_ref[...] = jnp.swapaxes(dvh_ref[...], 0, 1)


def send(block, axis, target):
    count = lax.axis_size(axis)
    route = [(i, target(i)) for i in range(count) if 0 <= target(i) < count]
    return lax.ppermute(block, axis, route)


def hop_count(tokens):
    return -(-LONGEST // (4 * tokens))


def entering_state(leave, keep, info, rates, forward, hops):
    heads, rows, dim = keep.shape
    at = FADES + (0 if forward else len(fade_rows(hops)[0]))
    first = 0 if forward else 1
    step = 4 if forward else -4
    part = jax.ShapeDtypeStruct((heads, rows // 2, dim), F32)
    half = jax.ShapeDtypeStruct(keep.shape, F32)

    def combine(kernel, arrays, outs):
        return run(
            kernel,
            [info, rates, *arrays],
            [SMEM, SMEM] + [VMEM] * len(arrays),
            outs,
            [VMEM] * len(outs),
            cost=(0, 4 * heads * rows * dim),
        )

    came_half = send(leave, "ctx", lambda i: i ^ 1)
    keep_part, send_part = combine(partial(chip_kernel, at), [keep, came_half], [part] * 2)
    came_part = send(send_part, "ctx", lambda i: i ^ 2)
    (moving,) = combine(partial(plane_kernel, at), [keep_part, came_part], [part])
    moved = []
    for _ in range(hops):
        moving = send(moving, "ctx", lambda i: i + step)
        moved.append(moving)
    own, send_part = combine(
        partial(part_kernel, at, hops, first), [keep_part, came_part, *moved], [part] * 2
    )
    came = send(send_part, "ctx", lambda i: i ^ 2)
    mine, send_half = combine(
        partial(half_kernel, at, first),
        [keep, came_half, own, came],
        [jax.ShapeDtypeStruct(keep.shape, BF16), half],
    )
    return mine, send(send_half, "ctx", lambda i: i ^ 1)


def head_sum_parts(stats):
    count = lax.axis_size("head")
    if count & (count - 1):
        return [stats] + [
            lax.ppermute(stats, "head", [(i, (i + d) % count) for i in range(count)])
            for d in range(1, count)
        ]
    parts, bit = [stats], 1
    while bit < count:
        stats = parts[0] if len(parts) == 1 else parts[0] + parts[1]
        parts = [stats, send(stats, "head", lambda i: i ^ bit)]
        bit *= 2
    return parts


SMEM = pl.BlockSpec(memory_space=pltpu.SMEM)
VMEM = pl.BlockSpec(memory_space=pltpu.VMEM)


def kept(*arrays):
    return [pltpu.with_memory_space_constraint(a, pltpu.VMEM) for a in arrays]


def streamed(*arrays):
    return [pltpu.with_memory_space_constraint(a, pltpu.HBM) for a in arrays]


def run(kernel, args, specs, outs, out_specs, steps=None, scratch=(), cost=(0, 0)):
    return pl.pallas_call(
        kernel,
        out_shape=outs,
        grid=() if steps is None else (steps,),
        in_specs=specs,
        out_specs=out_specs,
        scratch_shapes=scratch,
        cost_estimate=pl.CostEstimate(flops=cost[0], bytes_accessed=cost[1], transcendentals=0),
        compiler_params=pltpu.CompilerParams(vmem_limit_bytes=16 << 20),
    )(*args)


def body(queries, keys, values, out_grad, gain, rates, docs):
    tokens, heads, dim = queries.shape
    wide = 8 if heads % 8 == 0 else heads
    count = 4 if heads % 4 == 0 else heads
    groups, steps = heads // count, heads // wide
    rows = tokens // 2
    hops = hop_count(tokens)
    width = heads * dim * lax.axis_size("head")
    shape = lambda *s: jax.ShapeDtypeStruct(s, F32)
    major = pltpu.VMEM((heads, tokens, dim), BF16)
    some = pltpu.VMEM((count, tokens, dim), BF16)
    half = shape(heads, dim // 2, dim)
    token_block = pl.BlockSpec((tokens, wide, dim), lambda i: (0, i, 0))
    half_block = pl.BlockSpec((wide, dim // 2, dim), lambda i: (i, 0, 0))
    unit = heads * tokens * dim

    kh, vh, leave, keep = run(
        state_kernel,
        [docs, rates, *streamed(keys, values)],
        [SMEM, SMEM, token_block, token_block],
        [major, major, half, half],
        [VMEM, VMEM, half_block, half_block],
        steps=steps,
        cost=(2 * unit * dim, 8 * unit),
    )

    spans = sum(len(rows) for rows in fade_rows(hops))
    limits, distance = run(
        partial(setup_kernel, hops),
        [docs],
        [SMEM],
        [jax.ShapeDtypeStruct((FADES + spans,), jnp.int32), pltpu.VMEM((tokens, tokens), F32)],
        [SMEM, VMEM],
        scratch=[pltpu.VMEM((tokens, dim), jnp.int32)],
        cost=(0, 2 * tokens * tokens),
    )

    qh, gh = run(
        turn_kernel,
        streamed(queries, out_grad),
        [token_block, token_block],
        [major, major],
        [VMEM, VMEM],
        steps=steps,
        cost=(0, 8 * unit),
    )
    near, probs = [], []
    for g in range(groups):
        n, p = run(
            partial(scores_kernel, g * count, rows),
            [rates, *kept(qh, kh, vh, distance)],
            [SMEM] + [VMEM] * 4,
            [some, pltpu.VMEM((count, tokens, tokens), BF16)],
            [VMEM] * 2,
            cost=(4 * unit * tokens // groups, 0),
        )
        near.append(n), probs.append(p)

    mine, other = entering_state(leave, keep, limits, rates, True, hops)
    attn, states, stats = run(
        partial(attend_kernel, groups),
        [limits, rates, *kept(qh, gh), gain, mine, other, *kept(*near)],
        [SMEM, SMEM] + [VMEM] * (5 + groups),
        [major, pltpu.VMEM((heads, dim, dim), BF16), shape(2, tokens)],
        [VMEM] * 3,
        cost=(2 * unit * dim, 4 * unit),
    )
    parts = head_sum_parts(stats)

    grads, leave, keep = run(
        partial(norm_kernel, width, len(parts)),
        [limits, rates, *parts, *kept(attn, gh, qh), gain],
        [SMEM, SMEM] + [VMEM] * (len(parts) + 4),
        [major, half, half],
        [VMEM] * 3,
        cost=(2 * unit * dim, 4 * unit),
    )

    dqh, dk_part, dv_part = [], [], []
    for g in range(groups):
        a, b, c = run(
            partial(grads_kernel, g * count, rows),
            [limits, rates, *kept(grads, qh, kh, vh, probs[g], distance, states)],
            [SMEM, SMEM] + [VMEM] * 7,
            [some] * 3,
            [VMEM] * 3,
            cost=(8 * unit * tokens // groups, 0),
        )
        dqh.append(a), dk_part.append(b), dv_part.append(c)
    full = jax.ShapeDtypeStruct((tokens, heads, dim), BF16)
    dq = run(
        partial(turn_back_kernel, steps),
        kept(*dqh),
        [VMEM] * groups,
        full,
        token_block,
        steps=steps,
        cost=(0, 2 * unit),
    )

    mine, other = entering_state(leave, keep, limits, rates, False, hops)
    dk, dv = run(
        partial(finish_kernel, groups),
        [limits, rates, *kept(kh, vh), mine, other, *kept(*dk_part, *dv_part)],
        [SMEM, SMEM, VMEM, VMEM, half_block, half_block] + [VMEM] * (2 * groups),
        [full, full],
        [token_block, token_block],
        steps=steps,
        scratch=[pltpu.VMEM((wide, tokens, dim), BF16)] * 2 + [pltpu.VMEM((wide, dim, dim), BF16)],
        cost=(4 * unit * dim, 4 * unit),
    )
    return dq, dk, dv


def solution(mesh):
    token, head = P("ctx", "head", None), P("head")
    return jax.shard_map(
        body,
        mesh=mesh,
        in_specs=(token, token, token, token, P("head", None), head, P()),
        out_specs=(token, token, token),
        check_vma=False,
    )
```

time: 142 us -> 129 us (0.908)
  waiting for transfers between devices: 26.9 us -> 56.7 us
  starting transfers between devices: 32 us -> 15.6 us
  other arithmetic: 11 us -> 0 us
  local copies, waits for them, and re-layouts: 10.4 us -> 1.32 us
  Pallas kernels: 58.2 us -> 52.1 us
    ppermute x25 -> x13, waiting for transfers between devices: 26.9 us -> 56.7 us  [send(): return lax.ppermute(block, axis, route)]
    ppermute x25 -> x13, starting transfers between devices: 32 us -> 15.6 us  [send(): return lax.ppermute(block, axis, route)]
    select_n x14 -> x0, other arithmetic: 6.87 us -> none  [the longest x4 2.92 us: entering_state(): jnp.where(core_first, later_half, half)]
    unnamed x72 -> x10, local copies, waits for them, and re-layouts: 7.61 us -> 1.32 us
    pallas_call x12 -> x23, Pallas kernels: 58.2 us -> 52.1 us  [run(): pl.pallas_call(kernel, out_shape=outs, grid=() if steps is None else (ste...]
    add x9 -> x0, other arithmetic: 2.96 us -> none  [the longest x4 1.61 us: entering_state(): moving = w[2] * keep_part + w[3] * came_part]
    another operation x1 -> x0, local copies, waits for them, and re-layouts: 2.02 us -> none  [local(): jnp.stack([index, base, jnp.min(jnp.where(starts >= base, starts, inf)),...]
  transfers between devices with their start and end apart: 25 -> 13, of which waited for: 13 -> 10; matrix products, arithmetic and copies ran while one was open for 10% -> 0% of each run, Pallas kernels for 35% -> 26%
where the time goes in v2:
time: 129 us; the launch traced here: 127 us
  waiting for transfers between devices  56.7 us (44%)
  Pallas kernels  52.1 us (40%)
  starting transfers between devices  15.6 us (12%)
  local copies, waits for them, and re-layouts  1.32 us (1%)
    ppermute x13, waiting for transfers between devices, send(): return lax.ppermute(block, axis, route)  56.7 us
    pallas_call x23, Pallas kernels, run(): pl.pallas_call(kernel, out_shape=outs, grid=() if steps is None else (ste...  52.1 us
    ppermute x13, starting transfers between devices, send(): return lax.ppermute(block, axis, route)  15.6 us
  transfers between devices with their start and end apart: 13, of which 10 were waited for; matrix products, arithmetic and copies ran while one was open for 0% of the time, Pallas kernels for 26%

profile of v2, /device:TPU:12, one launch (start us, length us, event | category | flops | bytes accessed | tf_op | source)
XLA Modules:
  0.0 126.7 jit_solution(9259997573165824191)
XLA Ops:
  1.9 4.2 %shard_map.96 = (bf16[16,512,128]{2,1,0:T(8,128)(2,1)S(1)}, bf16[16,512,128]{2,1,0:T(8,128)(2,1)S(1)}, f32[16,64,128]{2,1,0:T(8,128)S(1)}, f32[16,64,128]{2,1,0:T(8,128)S(1)}) custom-call(s32[32]{0:T(128)S(1)} %copy-done.3, f32[16]{0:T(128)S(1)} %copy-done, bf16[512,16,128]{2,1,0:T(8,128)(2,1)} %k_ref.1, bf16[512,16,128]{2,1,0:T(8,128)(2,1)} %v_ref.1), custom_call_target="tpu_custom_call" | custom-call | flops 268435456 | bytes 8388608 | tf_op jit(solution)/shard_map/pallas_call | solution.py:426
  6.3 2.3 %shard_map.94 = (s32[19]{0:T(128)S(1)}, f32[512,512]{1,0:T(8,128)S(1)}) custom-call(s32[32]{0:T(128)S(1)} %copy-done.4), custom_call_target="tpu_custom_call" | custom-call | bytes 524288 | tf_op jit(solution)/shard_map/pallas_call | solution.py:426
  9.9 8.1 %collective-permute-done.1.came_ref = f32[16,32,128]{2,1,0:T(8,128)S(1)} collective-permute-done((f32[16,32,128]{2,1,0:T(8,128)S(1)}, f32[16,32,128]{2,1,0:T(8,128)S(1)}, u32[]{:S(2)}, u32[]{:S(2)}) %collective-permute-start.1) | collective-permute-done | bytes 262176 | tf_op jit(solution)/shard_map/ppermute | solution.py:353
  18.6 3.5 %collective-permute-start.2 = (f32[16,32,128]{2,1,0:T(8,128)S(1)}, f32[16,32,128]{2,1,0:T(8,128)S(1)}, u32[]{:S(2)}, u32[]{:S(2)}) collective-permute-start(f32[16,32,128]{2,1,0:T(8,128)S(1)} %shard_map.98), channel_id=1, source_target_pairs={{0,4},{1,5},{2,6},{3,7},{4,8},{5,9},{6,10},{7,11},{8,12},{9,13},{1... | collective-permute-start | bytes 786440 | tf_op jit(solution)/shard_map/ppermute | solution.py:353
  22.1 6.2 %collective-permute-done.2.refs_0_ = f32[16,32,128]{2,1,0:T(8,128)S(1)} collective-permute-done((f32[16,32,128]{2,1,0:T(8,128)S(1)}, f32[16,32,128]{2,1,0:T(8,128)S(1)}, u32[]{:S(2)}, u32[]{:S(2)}) %collective-permute-start.2) | collective-permute-done | bytes 262176 | tf_op jit(solution)/shard_map/ppermute | solution.py:353
  28.4 3.5 %collective-permute-start.3 = (f32[16,32,128]{2,1,0:T(8,128)S(1)}, f32[16,32,128]{2,1,0:T(8,128)S(1)}, u32[]{:S(2)}, u32[]{:S(2)}) collective-permute-start(f32[16,32,128]{2,1,0:T(8,128)S(1)} %collective-permute-done.2.refs_0_), channel_id=1, source_target_pairs={{0,4},{1,5},{2,6},{3,7},{4,8},{5,9},{6,10},{7,11},{8,12},{9,13},{1... | collective-permute-start | bytes 786440 | tf_op jit(solution)/shard_map/ppermute | solution.py:353
  31.8 5.4 %collective-permute-done.3.refs_1_ = f32[16,32,128]{2,1,0:T(8,128)S(1)} collective-permute-done((f32[16,32,128]{2,1,0:T(8,128)S(1)}, f32[16,32,128]{2,1,0:T(8,128)S(1)}, u32[]{:S(2)}, u32[]{:S(2)}) %collective-permute-start.3) | collective-permute-done | bytes 262176 | tf_op jit(solution)/shard_map/ppermute | solution.py:353
  38.5 5.8 %collective-permute-done.4.came_part_ref = f32[16,32,128]{2,1,0:T(8,128)S(1)} collective-permute-done((f32[16,32,128]{2,1,0:T(8,128)S(1)}, f32[16,32,128]{2,1,0:T(8,128)S(1)}, u32[]{:S(2)}, u32[]{:S(2)}) %collective-permute-start.4) | collective-permute-done | bytes 262176 | tf_op jit(solution)/shard_map/ppermute | solution.py:353
  44.3 0.7 shard_map.100
  45.1 2.6 %shard_map.95 = (bf16[16,512,128]{2,1,0:T(8,128)(2,1)S(1)}, bf16[16,512,128]{2,1,0:T(8,128)(2,1)S(1)}) custom-call(bf16[512,16,128]{2,1,0:T(8,128)(2,1)} %q_ref.1, bf16[512,16,128]{2,1,0:T(8,128)(2,1)} %g_ref.1), custom_call_target="tpu_custom_call" | custom-call | bytes 8388608 | tf_op jit(solution)/shard_map/pallas_call | solution.py:426
  47.7 2.8 %shard_map.104 = (bf16[4,512,128]{2,1,0:T(8,128)(2,1)S(1)}, bf16[4,512,512]{2,1,0:T(8,128)(2,1)S(1)}) custom-call(f32[16]{0:T(128)S(1)} %copy-done.1, bf16[16,512,128]{2,1,0:T(8,128)(2,1)S(1)} %get-tuple-element.52.qh_ref.refs_4_, bf16[16,512,128]{2,1,0:T(8,128)(2,1)S(1)} %get-tuple-element.62.kh_ref, bf16[16,512,128]{2,1,0:T(8,128)(2,1)S(1)} %get-tuple-element.63.vh_ref, ...), custom_call_target="tpu_custom_call" | custom-call | flops 536870912 | tf_op jit(solution)/shard_map/pallas_call | solution.py:426
  50.4 2.8 %shard_map.103 = (bf16[4,512,128]{2,1,0:T(8,128)(2,1)S(1)}, bf16[4,512,512]{2,1,0:T(8,128)(2,1)S(1)}) custom-call(f32[16]{0:T(128)S(1)} %copy-done.1, bf16[16,512,128]{2,1,0:T(8,128)(2,1)S(1)} %get-tuple-element.52.qh_ref.refs_4_, bf16[16,512,128]{2,1,0:T(8,128)(2,1)S(1)} %get-tuple-element.62.kh_ref, bf16[16,512,128]{2,1,0:T(8,128)(2,1)S(1)} %get-tuple-element.63.vh_ref, ...), custom_call_target="tpu_custom_call" | custom-call | flops 536870912 | tf_op jit(solution)/shard_map/pallas_call | solution.py:426
  53.2 2.8 %shard_map.102 = (bf16[4,512,128]{2,1,0:T(8,128)(2,1)S(1)}, bf16[4,512,512]{2,1,0:T(8,128)(2,1)S(1)}) custom-call(f32[16]{0:T(128)S(1)} %copy-done.1, bf16[16,512,128]{2,1,0:T(8,128)(2,1)S(1)} %get-tuple-element.52.qh_ref.refs_4_, bf16[16,512,128]{2,1,0:T(8,128)(2,1)S(1)} %get-tuple-element.62.kh_ref, bf16[16,512,128]{2,1,0:T(8,128)(2,1)S(1)} %get-tuple-element.63.vh_ref, ...), custom_call_target="tpu_custom_call" | custom-call | flops 536870912 | tf_op jit(solution)/shard_map/pallas_call | solution.py:426
  56.0 2.8 %shard_map.101 = (bf16[4,512,128]{2,1,0:T(8,128)(2,1)S(1)}, bf16[4,512,512]{2,1,0:T(8,128)(2,1)S(1)}) custom-call(f32[16]{0:T(128)S(1)} %copy-done.1, bf16[16,512,128]{2,1,0:T(8,128)(2,1)S(1)} %get-tuple-element.52.qh_ref.refs_4_, bf16[16,512,128]{2,1,0:T(8,128)(2,1)S(1)} %get-tuple-element.62.kh_ref, bf16[16,512,128]{2,1,0:T(8,128)(2,1)S(1)} %get-tuple-element.63.vh_ref, ...), custom_call_target="tpu_custom_call" | custom-call | flops 536870912 | tf_op jit(solution)/shard_map/pallas_call | solution.py:426
  58.8 2.7 %shard_map.105 = (bf16[16,512,128]{2,1,0:T(8,128)(2,1)S(1)}, bf16[16,128,128]{2,1,0:T(8,128)(2,1)S(1)}, f32[2,512]{1,0:T(2,128)S(1)}) custom-call(s32[19]{0:T(128)S(1)} %get-tuple-element.51.info_ref, f32[16]{0:T(128)S(1)} %copy-done.1, bf16[16,512,128]{2,1,0:T(8,128)(2,1)S(1)} %get-tuple-element.52.qh_ref.refs_4_, ...), custom_call_target="tpu_custom_call" | custom-call | flops 268435456 | bytes 4194304 | tf_op jit(solution)/shard_map/pallas_call | solution.py:426
  61.5 1.6 %collective-permute-start.6 = (f32[2,512]{1,0:T(2,128)S(1)}, f32[2,512]{1,0:T(2,128)S(1)}, u32[]{:S(2)}, u32[]{:S(2)}) collective-permute-start(f32[2,512]{1,0:T(2,128)S(1)} %get-tuple-element.69.refs_0_), channel_id=1, source_target_pairs={{0,16},{16,0},{1,17},{17,1},{2,18},{18,2},{3,19},{19,3},{4,20},{20... | collective-permute-start | bytes 12296 | tf_op jit(solution)/shard_map/ppermute | solution.py:353
  63.0 2.1 %collective-permute-done.6.refs_1_ = f32[2,512]{1,0:T(2,128)S(1)} collective-permute-done((f32[2,512]{1,0:T(2,128)S(1)}, f32[2,512]{1,0:T(2,128)S(1)}, u32[]{:S(2)}, u32[]{:S(2)}) %collective-permute-start.6) | collective-permute-done | bytes 4128 | tf_op jit(solution)/shard_map/ppermute | solution.py:353
  65.2 2.9 %shard_map.106 = (bf16[16,512,128]{2,1,0:T(8,128)(2,1)S(1)}, f32[16,64,128]{2,1,0:T(8,128)S(1)}, f32[16,64,128]{2,1,0:T(8,128)S(1)}) custom-call(s32[19]{0:T(128)S(1)} %get-tuple-element.51.info_ref, f32[16]{0:T(128)S(1)} %copy-done.1, f32[2,512]{1,0:T(2,128)S(1)} %get-tuple-element.69.refs_0_, f32[2,512]{1,0:T(2,128)S(1)} %collective-permute-done.6.refs_1_, ...), custom_call_target="tpu_custom_call" | custom-call | flops 268435456 | bytes 4194304 | tf_op jit(solution)/shard_map/pallas_call | solution.py:426
  68.2 1.9 %collective-permute-done.7.came_ref = f32[16,64,128]{2,1,0:T(8,128)S(1)} collective-permute-done((f32[16,64,128]{2,1,0:T(8,128)S(1)}, f32[16,64,128]{2,1,0:T(8,128)S(1)}, u32[]{:S(2)}, u32[]{:S(2)}) %collective-permute-start.7) | collective-permute-done | bytes 524320 | tf_op jit(solution)/shard_map/ppermute | solution.py:353
  71.3 7.8 %collective-permute-done.8.came_ref = f32[16,32,128]{2,1,0:T(8,128)S(1)} collective-permute-done((f32[16,32,128]{2,1,0:T(8,128)S(1)}, f32[16,32,128]{2,1,0:T(8,128)S(1)}, u32[]{:S(2)}, u32[]{:S(2)}) %collective-permute-start.8) | collective-permute-done | bytes 262176 | tf_op jit(solution)/shard_map/ppermute | solution.py:353
  79.7 1.9 %collective-permute-start.9 = (f32[16,32,128]{2,1,0:T(8,128)S(1)}, f32[16,32,128]{2,1,0:T(8,128)S(1)}, u32[]{:S(2)}, u32[]{:S(2)}) collective-permute-start(f32[16,32,128]{2,1,0:T(8,128)S(1)} %shard_map.113), channel_id=1, source_target_pairs={{4,0},{5,1},{6,2},{7,3},{8,4},{9,5},{10,6},{11,7},{12,8},{13,9},{1... | collective-permute-start | bytes 786440 | tf_op jit(solution)/shard_map/ppermute | solution.py:353
  81.6 7.5 %collective-permute-done.9.refs_0_ = f32[16,32,128]{2,1,0:T(8,128)S(1)} collective-permute-done((f32[16,32,128]{2,1,0:T(8,128)S(1)}, f32[16,32,128]{2,1,0:T(8,128)S(1)}, u32[]{:S(2)}, u32[]{:S(2)}) %collective-permute-start.9) | collective-permute-done | bytes 262176 | tf_op jit(solution)/shard_map/ppermute | solution.py:353
  89.1 2.4 %collective-permute-start.10 = (f32[16,32,128]{2,1,0:T(8,128)S(1)}, f32[16,32,128]{2,1,0:T(8,128)S(1)}, u32[]{:S(2)}, u32[]{:S(2)}) collective-permute-start(f32[16,32,128]{2,1,0:T(8,128)S(1)} %collective-permute-done.9.refs_0_), channel_id=1, source_target_pairs={{4,0},{5,1},{6,2},{7,3},{8,4},{9,5},{10,6},{11,7},{12,8},{13,9},{1... | collective-permute-start | bytes 786440 | tf_op jit(solution)/shard_map/ppermute | solution.py:353
  91.5 6.1 %collective-permute-done.10.refs_1_ = f32[16,32,128]{2,1,0:T(8,128)S(1)} collective-permute-done((f32[16,32,128]{2,1,0:T(8,128)S(1)}, f32[16,32,128]{2,1,0:T(8,128)S(1)}, u32[]{:S(2)}, u32[]{:S(2)}) %collective-permute-start.10) | collective-permute-done | bytes 262176 | tf_op jit(solution)/shard_map/ppermute | solution.py:353
  98.9 5.8 %collective-permute-done.11.came_part_ref = f32[16,32,128]{2,1,0:T(8,128)S(1)} collective-permute-done((f32[16,32,128]{2,1,0:T(8,128)S(1)}, f32[16,32,128]{2,1,0:T(8,128)S(1)}, u32[]{:S(2)}, u32[]{:S(2)}) %collective-permute-start.11) | collective-permute-done | bytes 262176 | tf_op jit(solution)/shard_map/ppermute | solution.py:353
  104.7 0.7 shard_map.115
  105.5 3.8 %shard_map.110 = (bf16[4,512,128]{2,1,0:T(8,128)(2,1)S(1)}, bf16[4,512,128]{2,1,0:T(8,128)(2,1)S(1)}, bf16[4,512,128]{2,1,0:T(8,128)(2,1)S(1)}) custom-call(s32[19]{0:T(128)S(1)} %get-tuple-element.51.info_ref, f32[16]{0:T(128)S(1)} %copy-done.1, bf16[16,512,128]{2,1,0:T(8,128)(2,1)S(1)} %get-tuple-element.71.grad_ref, ...), custom_call_target="tpu_custom_call" | custom-call | flops 1073741824 | tf_op jit(solution)/shard_map/pallas_call | solution.py:426
  109.3 3.9 %shard_map.109 = (bf16[4,512,128]{2,1,0:T(8,128)(2,1)S(1)}, bf16[4,512,128]{2,1,0:T(8,128)(2,1)S(1)}, bf16[4,512,128]{2,1,0:T(8,128)(2,1)S(1)}) custom-call(s32[19]{0:T(128)S(1)} %get-tuple-element.51.info_ref, f32[16]{0:T(128)S(1)} %copy-done.1, bf16[16,512,128]{2,1,0:T(8,128)(2,1)S(1)} %get-tuple-element.71.grad_ref, ...), custom_call_target="tpu_custom_call" | custom-call | flops 1073741824 | tf_op jit(solution)/shard_map/pallas_call | solution.py:426
  113.2 3.9 %shard_map.108 = (bf16[4,512,128]{2,1,0:T(8,128)(2,1)S(1)}, bf16[4,512,128]{2,1,0:T(8,128)(2,1)S(1)}, bf16[4,512,128]{2,1,0:T(8,128)(2,1)S(1)}) custom-call(s32[19]{0:T(128)S(1)} %get-tuple-element.51.info_ref, f32[16]{0:T(128)S(1)} %copy-done.1, bf16[16,512,128]{2,1,0:T(8,128)(2,1)S(1)} %get-tuple-element.71.grad_ref, ...), custom_call_target="tpu_custom_call" | custom-call | flops 1073741824 | tf_op jit(solution)/shard_map/pallas_call | solution.py:426
  117.1 3.9 %shard_map.107 = (bf16[4,512,128]{2,1,0:T(8,128)(2,1)S(1)}, bf16[4,512,128]{2,1,0:T(8,128)(2,1)S(1)}, bf16[4,512,128]{2,1,0:T(8,128)(2,1)S(1)}) custom-call(s32[19]{0:T(128)S(1)} %get-tuple-element.51.info_ref, f32[16]{0:T(128)S(1)} %copy-done.1, bf16[16,512,128]{2,1,0:T(8,128)(2,1)S(1)} %get-tuple-element.71.grad_ref, ...), custom_call_target="tpu_custom_call" | custom-call | flops 1073741824 | tf_op jit(solution)/shard_map/pallas_call | solution.py:426
  120.9 1.5 %shard_map.111 = bf16[512,16,128]{2,1,0:T(8,128)(2,1)} custom-call(bf16[4,512,128]{2,1,0:T(8,128)(2,1)S(1)} %get-tuple-element.74.refs_0_, bf16[4,512,128]{2,1,0:T(8,128)(2,1)S(1)} %get-tuple-element.76.refs_1_, bf16[4,512,128]{2,1,0:T(8,128)(2,1)S(1)} %get-tuple-element.78.refs_2_, bf16[4,512,128]{2,1,0:T(8,128)(2,1)S(1)} %get-tuple-element.80.refs_3_), custom_call_target="tpu_custom_call" | custom-call | bytes 2097152 | tf_op jit(solution)/shard_map/pallas_call | solution.py:426
  122.4 4.3 %shard_map.116 = (bf16[512,16,128]{2,1,0:T(8,128)(2,1)}, bf16[512,16,128]{2,1,0:T(8,128)(2,1)}) custom-call(s32[19]{0:T(128)S(1)} %get-tuple-element.51.info_ref, f32[16]{0:T(128)S(1)} %copy-done.1, bf16[16,512,128]{2,1,0:T(8,128)(2,1)S(1)} %get-tuple-element.62.kh_ref, bf16[16,512,128]{2,1,0:T(8,128)(2,1)S(1)} %get-tuple-element.63.vh_ref, ...), custom_call_target="tpu_custom_call" | custom-call | flops 536870912 | bytes 4194304 | tf_op jit(solution)/shard_map/pallas_call | solution.py:426
  (27 shorter events, 7.9 us)
Async XLA Ops:
  0.6 0.7 copy-start
  1.3 0.7 copy-start.3
  1.9 4.3 %copy-start.4 = (s32[32]{0:T(128)S(1)}, s32[32]{0:T(128)}, u32[]{:S(2)}) copy-start(s32[32]{0:T(128)} %docs_ref.3) | copy-start | bytes 388
  1.9 6.7 %copy-start.1 = (f32[16]{0:T(128)S(1)}, f32[16]{0:T(128)}, u32[]{:S(2)}) copy-start(f32[16]{0:T(128)} %rate_ref.39) | copy-start | bytes 196
  6.2 2.4 %collective-permute-start = (f32[16,64,128]{2,1,0:T(8,128)S(1)}, f32[16,64,128]{2,1,0:T(8,128)S(1)}, u32[]{:S(2)}, u32[]{:S(2)}) collective-permute-start(f32[16,64,128]{2,1,0:T(8,128)S(1)} %get-tuple-element.55), channel_id=1, source_target_pairs={{0,1},{1,0},{2,3},{3,2},{4,5},{5,4},{6,7},{7,6},{8,9},{9,8},{10,11... | collective-permute-start | bytes 1572872 | tf_op jit(solution)/shard_map/ppermute | solution.py:353
  9.3 8.8 %collective-permute-start.1 = (f32[16,32,128]{2,1,0:T(8,128)S(1)}, f32[16,32,128]{2,1,0:T(8,128)S(1)}, u32[]{:S(2)}, u32[]{:S(2)}) collective-permute-start(f32[16,32,128]{2,1,0:T(8,128)S(1)} %get-tuple-element.57), channel_id=1, source_target_pairs={{0,2},{1,3},{2,0},{3,1},{4,6},{5,7},{6,4},{7,5},{8,10},{9,11},{10,... | collective-permute-start | bytes 786440 | tf_op jit(solution)/shard_map/ppermute | solution.py:353
  18.6 9.7 %collective-permute-start.2 = (f32[16,32,128]{2,1,0:T(8,128)S(1)}, f32[16,32,128]{2,1,0:T(8,128)S(1)}, u32[]{:S(2)}, u32[]{:S(2)}) collective-permute-start(f32[16,32,128]{2,1,0:T(8,128)S(1)} %shard_map.98), channel_id=1, source_target_pairs={{0,4},{1,5},{2,6},{3,7},{4,8},{5,9},{6,10},{7,11},{8,12},{9,13},{1... | collective-permute-start | bytes 786440 | tf_op jit(solution)/shard_map/ppermute | solution.py:353
  28.4 8.9 %collective-permute-start.3 = (f32[16,32,128]{2,1,0:T(8,128)S(1)}, f32[16,32,128]{2,1,0:T(8,128)S(1)}, u32[]{:S(2)}, u32[]{:S(2)}) collective-permute-start(f32[16,32,128]{2,1,0:T(8,128)S(1)} %collective-permute-done.2.refs_0_), channel_id=1, source_target_pairs={{0,4},{1,5},{2,6},{3,7},{4,8},{5,9},{6,10},{7,11},{8,12},{9,13},{1... | collective-permute-start | bytes 786440 | tf_op jit(solution)/shard_map/ppermute | solution.py:353
  37.9 6.4 %collective-permute-start.4 = (f32[16,32,128]{2,1,0:T(8,128)S(1)}, f32[16,32,128]{2,1,0:T(8,128)S(1)}, u32[]{:S(2)}, u32[]{:S(2)}) collective-permute-start(f32[16,32,128]{2,1,0:T(8,128)S(1)} %get-tuple-element.59), channel_id=1, source_target_pairs={{0,2},{1,3},{2,0},{3,1},{4,6},{5,7},{6,4},{7,5},{8,10},{9,11},{10,... | collective-permute-start | bytes 786440 | tf_op jit(solution)/shard_map/ppermute | solution.py:353
  45.0 13.8 %collective-permute-start.5 = (f32[16,64,128]{2,1,0:T(8,128)S(1)}, f32[16,64,128]{2,1,0:T(8,128)S(1)}, u32[]{:S(2)}, u32[]{:S(2)}) collective-permute-start(f32[16,64,128]{2,1,0:T(8,128)S(1)} %get-tuple-element.61), channel_id=1, source_target_pairs={{0,1},{1,0},{2,3},{3,2},{4,5},{5,4},{6,7},{7,6},{8,9},{9,8},{10,11... | collective-permute-start | bytes 1572872 | tf_op jit(solution)/shard_map/ppermute | solution.py:353
  56.0 2.8 %copy-start.2 = (f32[16,128]{1,0:T(8,128)S(1)}, f32[16,128]{1,0:T(8,128)}, u32[]{:S(2)}) copy-start(f32[16,128]{1,0:T(8,128)} %refs_5_.1) | copy-start | bytes 24580
  61.5 3.7 %collective-permute-start.6 = (f32[2,512]{1,0:T(2,128)S(1)}, f32[2,512]{1,0:T(2,128)S(1)}, u32[]{:S(2)}, u32[]{:S(2)}) collective-permute-start(f32[2,512]{1,0:T(2,128)S(1)} %get-tuple-element.69.refs_0_), channel_id=1, source_target_pairs={{0,16},{16,0},{1,17},{17,1},{2,18},{18,2},{3,19},{19,3},{4,20},{20... | collective-permute-start | bytes 12296 | tf_op jit(solution)/shard_map/ppermute | solution.py:353
  68.1 2.0 %collective-permute-start.7 = (f32[16,64,128]{2,1,0:T(8,128)S(1)}, f32[16,64,128]{2,1,0:T(8,128)S(1)}, u32[]{:S(2)}, u32[]{:S(2)}) collective-permute-start(f32[16,64,128]{2,1,0:T(8,128)S(1)} %get-tuple-element.82), channel_id=1, source_target_pairs={{0,1},{1,0},{2,3},{3,2},{4,5},{5,4},{6,7},{7,6},{8,9},{9,8},{10,11... | collective-permute-start | bytes 1572872 | tf_op jit(solution)/shard_map/ppermute | solution.py:353
  70.7 8.4 %collective-permute-start.8 = (f32[16,32,128]{2,1,0:T(8,128)S(1)}, f32[16,32,128]{2,1,0:T(8,128)S(1)}, u32[]{:S(2)}, u32[]{:S(2)}) collective-permute-start(f32[16,32,128]{2,1,0:T(8,128)S(1)} %get-tuple-element.84), channel_id=1, source_target_pairs={{0,2},{1,3},{2,0},{3,1},{4,6},{5,7},{6,4},{7,5},{8,10},{9,11},{10,... | collective-permute-start | bytes 786440 | tf_op jit(solution)/shard_map/ppermute | solution.py:353
  79.7 9.4 %collective-permute-start.9 = (f32[16,32,128]{2,1,0:T(8,128)S(1)}, f32[16,32,128]{2,1,0:T(8,128)S(1)}, u32[]{:S(2)}, u32[]{:S(2)}) collective-permute-start(f32[16,32,128]{2,1,0:T(8,128)S(1)} %shard_map.113), channel_id=1, source_target_pairs={{4,0},{5,1},{6,2},{7,3},{8,4},{9,5},{10,6},{11,7},{12,8},{13,9},{1... | collective-permute-start | bytes 786440 | tf_op jit(solution)/shard_map/ppermute | solution.py:353
  89.1 8.5 %collective-permute-start.10 = (f32[16,32,128]{2,1,0:T(8,128)S(1)}, f32[16,32,128]{2,1,0:T(8,128)S(1)}, u32[]{:S(2)}, u32[]{:S(2)}) collective-permute-start(f32[16,32,128]{2,1,0:T(8,128)S(1)} %collective-permute-done.9.refs_0_), channel_id=1, source_target_pairs={{4,0},{5,1},{6,2},{7,3},{8,4},{9,5},{10,6},{11,7},{12,8},{13,9},{1... | collective-permute-start | bytes 786440 | tf_op jit(solution)/shard_map/ppermute | solution.py:353
  98.3 6.4 %collective-permute-start.11 = (f32[16,32,128]{2,1,0:T(8,128)S(1)}, f32[16,32,128]{2,1,0:T(8,128)S(1)}, u32[]{:S(2)}, u32[]{:S(2)}) collective-permute-start(f32[16,32,128]{2,1,0:T(8,128)S(1)} %get-tuple-element.86), channel_id=1, source_target_pairs={{0,2},{1,3},{2,0},{3,1},{4,6},{5,7},{6,4},{7,5},{8,10},{9,11},{10,... | collective-permute-start | bytes 786440 | tf_op jit(solution)/shard_map/ppermute | solution.py:353
  105.4 17.0 %collective-permute-start.12 = (f32[16,64,128]{2,1,0:T(8,128)S(1)}, f32[16,64,128]{2,1,0:T(8,128)S(1)}, u32[]{:S(2)}, u32[]{:S(2)}) collective-permute-start(f32[16,64,128]{2,1,0:T(8,128)S(1)} %get-tuple-element.88), channel_id=1, source_target_pairs={{0,1},{1,0},{2,3},{3,2},{4,5},{5,4},{6,7},{7,6},{8,9},{9,8},{10,11... | collective-permute-start | bytes 1572872 | tf_op jit(solution)/shard_map/ppermute | solution.py:353

commit v3 on v2

--- a/solution.py
+++ b/solution.py
@@ -12,6 +12,7 @@
 LONGEST = 4096
 FAR = 1e30
 APART = 1 << 30
+CHUNKS = 1
 F32 = jnp.float32
 BF16 = jnp.bfloat16
 
@@ -68,9 +69,9 @@
     return ahead, back
 
 
-def setup_kernel(hops, docs_ref, info_ref, dist_ref, begin_ref):
-    tokens = dist_ref.shape[0]
-    lanes = begin_ref.shape[1]
+def setup_kernel(hops, tokens, docs_ref, rate_in_ref, info_ref, rate_ref):
+    for h in range(rate_ref.shape[0]):
+        rate_ref[h] = rate_in_ref[h]
     index = lax.axis_index("ctx").astype(jnp.int32)
     base = index * tokens
     ahead, back = fade_rows(hops)
@@ -78,19 +79,12 @@
     spans = [(spot(*row[:3]), spot(*row[3:])) for row in ahead + back]
     tops = [end - 1 for _, end in spans[: len(ahead)]] + [begin for begin, _ in spans[len(ahead) :]]
     tops.append(base + tokens)
-    row = column(tokens, lanes)
-    begin_ref[...] = jnp.zeros_like(begin_ref)
 
     def doc(j, carry):
         start, upper, later, seen = carry
         upper = jnp.where((start >= base) & (start < upper), start, upper)
         later = jnp.where((start > base) & (start < later), start, later)
         seen = tuple(jnp.where(start <= top, start, old) for top, old in zip(tops, seen))
-
-        @pl.when((start > base) & (start < base + tokens))
-        def _():
-            begin_ref[...] = jnp.where(row >= start - base, start - base, begin_ref[...])
-
         return start + docs_ref[j], upper, later, seen
 
     zero = jnp.int32(0)
@@ -108,6 +102,21 @@
         joined = last < begin if forward else last <= end
         info_ref[FADES + j] = jnp.where(joined, end - begin if forward else begin - end, far)
 
+
+def mask_kernel(docs_ref, dist_ref, begin_ref):
+    tokens, lanes = begin_ref.shape
+    base = lax.axis_index("ctx").astype(jnp.int32) * tokens
+    row = column(tokens, lanes)
+    begin_ref[...] = jnp.zeros_like(begin_ref)
+
+    def doc(j, start):
+        @pl.when((start > base) & (start < base + tokens))
+        def _():
+            begin_ref[...] = jnp.where(row >= start - base, start - base, begin_ref[...])
+
+        return start + docs_ref[j]
+
+    lax.fori_loop(0, docs_ref.shape[0], doc, jnp.int32(0))
     for low in range(0, tokens, lanes):
         spots = low + lax.broadcasted_iota(jnp.int32, (tokens, lanes), 1)
         allowed = (spots <= row) & (spots >= begin_ref[...])
@@ -125,11 +134,11 @@
 TILE = (8, 128)
 
 
-def chip_kernel(at, info_ref, rate_ref, keep_ref, came_ref, keep_part_ref, send_part_ref):
+def chip_kernel(at, base, info_ref, rate_ref, keep_ref, came_ref, keep_part_ref, send_part_ref):
     heads, quarter, _ = keep_part_ref.shape
     side = (info_ref[INDEX] >> 1) & 1
     for h in range(heads):
-        rate = rate_ref[h]
+        rate = rate_ref[base + h]
         mine = fade(rate, info_ref[at], TILE)
         theirs = fade(rate, info_ref[at + 1], TILE)
         chip = spread(mine, keep_ref[h]) + spread(theirs, came_ref[h])
@@ -138,19 +147,19 @@
         send_part_ref[h] = jnp.where(side == 0, high, low)
 
 
-def plane_kernel(at, info_ref, rate_ref, keep_ref, came_ref, out_ref):
+def plane_kernel(at, base, info_ref, rate_ref, keep_ref, came_ref, out_ref):
     for h in range(out_ref.shape[0]):
-        rate = rate_ref[h]
+        rate = rate_ref[base + h]
         mine = fade(rate, info_ref[at + 2], TILE)
         theirs = fade(rate, info_ref[at + 3], TILE)
         out_ref[h] = spread(mine, keep_ref[h]) + spread(theirs, came_ref[h])
 
 
-def part_kernel(at, hops, first_side, info_ref, rate_ref, keep_ref, came_ref, *refs):
+def part_kernel(at, base, hops, first_side, info_ref, rate_ref, keep_ref, came_ref, *refs):
     moved, (own_ref, send_ref) = refs[:hops], refs[hops:]
     is_first = ((info_ref[INDEX] >> 1) & 1) == first_side
     for h in range(own_ref.shape[0]):
-        rate = rate_ref[h]
+        rate = rate_ref[base + h]
         total = moved[0][h]
         for hop in range(1, hops):
             total += spread(fade(rate, info_ref[at + 5 + hop], TILE), moved[hop][h])
@@ -160,7 +169,7 @@
         send_ref[h] = jnp.where(is_first, later, total)
 
 
-def half_kernel(at, first_core, info_ref, rate_ref, keep_ref, came_ref, own_ref, came_part_ref, mine_ref, send_ref):
+def half_kernel(at, base, first_core, info_ref, rate_ref, keep_ref, came_ref, own_ref, came_part_ref, mine_ref, send_ref):
     heads = own_ref.shape[0]
     index = info_ref[INDEX]
     is_first = (index & 1) == first_core
@@ -171,7 +180,7 @@
             [jnp.where(low_side, own, came), jnp.where(low_side, came, own)], axis=0
         )
         earlier = jnp.where(is_first, keep_ref[h], came_ref[h])
-        later = spread(fade(rate_ref[h], info_ref[at + 5], TILE), half) + earlier
+        later = spread(fade(rate_ref[base + h], info_ref[at + 5], TILE), half) + earlier
         mine_ref[h] = jnp.where(is_first, half, later).astype(BF16)
         send_ref[h] = jnp.where(is_first, later, half)
 
@@ -200,7 +209,7 @@
     for h in range(heads):
         tail = jnp.exp(-rate_ref[first + h] * distance)
         faded = (turned_k[h].astype(F32) * tail).astype(BF16)
-        split_halves(core, dot(faded, turned_v[h], TN), send_ref, keep_ref, h)
+        split_halves(core, dot(faded, turned_v[h], TN), send_ref, keep_ref, first + h)
 
 
 def turn_kernel(q_ref, g_ref, qh_ref, gh_ref):
@@ -228,33 +237,44 @@
     lax.fori_loop(0, heads, head, 0)
 
 
-def attend_kernel(groups, info_ref, rate_ref, qh_ref, gh_ref, gain_ref, mine_ref, other_ref, *refs):
-    local_refs, (attn_ref, state_ref, stats_ref) = refs[:groups], refs[groups:]
-    heads, tokens, dim = qh_ref.shape
+def attend_kernel(base, groups, begin, final, info_ref, rate_ref, qh_ref, gh_ref, gain_ref, mine_ref, other_ref, *refs):
+    local_refs, refs = refs[:groups], refs[groups:]
+    if not begin:
+        sums_ref, refs = refs[0], refs[1:]
+    attn_ref, state_ref, stats_ref = refs
+    heads, tokens, dim = attn_ref.shape
     count = heads // groups
     core = info_ref[INDEX] & 1
     row = column(tokens, dim)
     distance = jnp.where(
         row + info_ref[BASE] < info_ref[NEXT_START], (row + 1).astype(F32), F32(FAR)
     )
-    squares = jnp.zeros((tokens, dim), F32)
-    cross = jnp.zeros((tokens, dim), F32)
+    if begin:
+        squares = jnp.zeros((tokens, dim), F32)
+        cross = jnp.zeros((tokens, dim), F32)
+    else:
+        squares, cross = sums_ref[0], sums_ref[1]
     for h in range(heads):
+        full = base + h
         put_halves(core, state_ref, h, mine_ref[h], other_ref[h])
-        factor = jnp.exp(-rate_ref[h] * distance)
+        factor = jnp.exp(-rate_ref[full] * distance)
         near = local_refs[h // count][h % count].astype(F32)
-        attn = near + factor * dot(qh_ref[h], state_ref[h], NN)
+        attn = near + factor * dot(qh_ref[full], state_ref[h], NN)
         attn_ref[h] = attn.astype(BF16)
         squares += attn * attn
-        cross += gain_ref[h : h + 1, :] * gh_ref[h].astype(F32) * attn
-    stats_ref[0:1, :] = jnp.sum(jnp.swapaxes(squares, 0, 1), axis=0, keepdims=True)
-    stats_ref[1:2, :] = jnp.sum(jnp.swapaxes(cross, 0, 1), axis=0, keepdims=True)
-
-
-def norm_kernel(width, parts, info_ref, rate_ref, *refs):
+        cross += gain_ref[full : full + 1, :] * gh_ref[full].astype(F32) * attn
+    if final:
+        stats_ref[0:1, :] = jnp.sum(jnp.swapaxes(squares, 0, 1), axis=0, keepdims=True)
+        stats_ref[1:2, :] = jnp.sum(jnp.swapaxes(cross, 0, 1), axis=0, keepdims=True)
+    else:
+        stats_ref[0] = squares
+        stats_ref[1] = cross
+
+
+def norm_kernel(base, width, parts, info_ref, rate_ref, *refs):
     stats_refs, refs = refs[:parts], refs[parts:]
     attn_ref, gh_ref, qh_ref, gain_ref, grad_ref, send_ref, keep_ref = refs
-    heads, tokens, dim = qh_ref.shape
+    heads, tokens, dim = grad_ref.shape
     core = info_ref[INDEX] & 1
     stats = stats_refs[0][...]
     for ref in stats_refs[1:]:
@@ -267,15 +287,16 @@
     row = column(tokens, dim)
     distance = jnp.where(row + info_ref[BASE] < info_ref[LATER_START], row.astype(F32), F32(FAR))
     for h in range(heads):
-        gained = gain_ref[h : h + 1, :] * gh_ref[h].astype(F32)
+        full = base + h
+        gained = gain_ref[full : full + 1, :] * gh_ref[full].astype(F32)
         grad = (gained * inverse - attn_ref[h].astype(F32) * scale).astype(BF16)
         grad_ref[h] = grad
-        lead = jnp.exp(-rate_ref[h] * distance)
-        faded = (qh_ref[h].astype(F32) * lead).astype(BF16)
+        lead = jnp.exp(-rate_ref[full] * distance)
+        faded = (qh_ref[full].astype(F32) * lead).astype(BF16)
         split_halves(core, dot(faded, grad, TN), send_ref, keep_ref, h)
 
 
-def grads_kernel(first, rows, info_ref, rate_ref, grad_ref, qh_ref, kh_ref, vh_ref, probs_ref, dist_ref, state_ref, dq_ref, dk_ref, dv_ref):
+def grads_kernel(base, first, rows, info_ref, rate_ref, grad_ref, qh_ref, kh_ref, vh_ref, probs_ref, dist_ref, state_ref, dq_ref, dk_ref, dv_ref):
     heads, tokens, dim = dq_ref.shape
     row = column(tokens, dim)
     distance = jnp.where(
@@ -283,17 +304,18 @@
     )
 
     def head(h, carry):
-        full = first + h
+        near = first + h
+        full = base + near
         rate = rate_ref[full]
         factor = jnp.exp(-rate * distance)
         dk = dv = None
         for low in range(tokens - rows, -1, -rows):
             top = low + rows
-            grad = grad_ref[full, low:top, :]
+            grad = grad_ref[near, low:top, :]
             raw = dot(grad, vh_ref[full, :top, :], NT)
             weights = (raw * jnp.exp(-rate * dist_ref[low:top, :top])).astype(BF16)
             dq = dot(weights, kh_ref[full, :top, :], NN)
-            dq += factor[low:top] * dot(grad, state_ref[full], NT)
+            dq += factor[low:top] * dot(grad, state_ref[near], NT)
             dq_ref[h, low:top, :] = dq.astype(BF16)
             dk_new = dot(weights, qh_ref[full, low:top, :], TN)
             dv_new = dot(probs_ref[h, low:top, :top], grad, TN)
@@ -319,32 +341,37 @@
             out_ref[...] = jnp.swapaxes(jnp.concatenate(block, axis=0), 0, 1)
 
 
-def finish_kernel(groups, info_ref, rate_ref, kh_ref, vh_ref, mine_ref, other_ref, *refs):
-    dk_parts, dv_parts = refs[:groups], refs[groups : 2 * groups]
-    dk_ref, dv_ref, dkh_ref, dvh_ref, state_ref = refs[2 * groups :]
-    heads, tokens, dim = dkh_ref.shape
-    count = dk_parts[0].shape[0]
+def finish_kernel(base, groups, steps, info_ref, rate_ref, kh_ref, vh_ref, mine_ref, other_ref, *refs):
+    dk_parts, dv_parts = refs[: groups * steps], refs[groups * steps : 2 * groups * steps]
+    dk_ref, dv_ref, state_ref = refs[-3:]
+    heads = mine_ref.shape[0]
+    count, tokens, dim = dk_parts[0].shape
     core = info_ref[INDEX] & 1
     row = column(tokens, dim)
     distance = jnp.where(
         row + info_ref[BASE] >= info_ref[NEXT_BEGIN], (tokens - row).astype(F32), F32(FAR)
     )
-    for s in range(groups * count // heads):
-
-        @pl.when(pl.program_id(0) == s)
-        def _():
-            for h in range(heads):
-                full = s * heads + h
-                put_halves(core, state_ref, h, mine_ref[h], other_ref[h])
-                factor = jnp.exp(-rate_ref[full] * distance)
-                dk = dk_parts[full // count][full % count].astype(F32)
-                dv = dv_parts[full // count][full % count].astype(F32)
-                dk += factor * dot(vh_ref[full], state_ref[h], NT)
-                dv += factor * dot(kh_ref[full], state_ref[h], NN)
-                dkh_ref[h] = dk.astype(BF16)
-                dvh_ref[h] = dv.astype(BF16)
-            dk_ref[...] = jnp.swapaxes(dkh_ref[...], 0, 1)
-            dv_ref[...] = jnp.swapaxes(dvh_ref[...], 0, 1)
+
+    def block(first, dk_parts, dv_parts):
+        dks, dvs = [], []
+        for h in range(heads):
+            full = first + h
+            put_halves(core, state_ref, h, mine_ref[h], other_ref[h])
+            factor = jnp.exp(-rate_ref[full] * distance)
+            dk = dk_parts[h // count][h % count].astype(F32)
+            dv = dv_parts[h // count][h % count].astype(F32)
+            dk += factor * dot(vh_ref[full], state_ref[h], NT)
+            dv += factor * dot(kh_ref[full], state_ref[h], NN)
+            dks.append(dk.astype(BF16))
+            dvs.append(dv.astype(BF16))
+        dk_ref[...] = jnp.swapaxes(jnp.stack(dks), 0, 1)
+        dv_ref[...] = jnp.swapaxes(jnp.stack(dvs), 0, 1)
+
+    if base is not None:
+        return block(base, dk_parts, dv_parts)
+    for s in range(steps):
+        here = slice(s * groups, (s + 1) * groups)
+        pl.when(pl.program_id(0) == s)(partial(block, s * heads, dk_parts[here], dv_parts[here]))
 
 
 def send(block, axis, target):
@@ -357,7 +384,7 @@
     return -(-LONGEST // (4 * tokens))
 
 
-def entering_state(leave, keep, info, rates, forward, hops):
+def entering_state(leave, keep, info, rates, base, forward, hops):
     heads, rows, dim = keep.shape
     at = FADES + (0 if forward else len(fade_rows(hops)[0]))
     first = 0 if forward else 1
@@ -376,19 +403,19 @@
         )
 
     came_half = send(leave, "ctx", lambda i: i ^ 1)
-    keep_part, send_part = combine(partial(chip_kernel, at), [keep, came_half], [part] * 2)
+    keep_part, send_part = combine(partial(chip_kernel, at, base), [keep, came_half], [part] * 2)
     came_part = send(send_part, "ctx", lambda i: i ^ 2)
-    (moving,) = combine(partial(plane_kernel, at), [keep_part, came_part], [part])
+    (moving,) = combine(partial(plane_kernel, at, base), [keep_part, came_part], [part])
     moved = []
     for _ in range(hops):
         moving = send(moving, "ctx", lambda i: i + step)
         moved.append(moving)
     own, send_part = combine(
-        partial(part_kernel, at, hops, first), [keep_part, came_part, *moved], [part] * 2
+        partial(part_kernel, at, base, hops, first), [keep_part, came_part, *moved], [part] * 2
     )
     came = send(send_part, "ctx", lambda i: i ^ 2)
     mine, send_half = combine(
-        partial(half_kernel, at, first),
+        partial(half_kernel, at, base, first),
         [keep, came_half, own, came],
         [jax.ShapeDtypeStruct(keep.shape, BF16), half],
     )
@@ -418,11 +445,15 @@
     return [pltpu.with_memory_space_constraint(a, pltpu.VMEM) for a in arrays]
 
 
+def at_hand(*arrays):
+    return [pltpu.with_memory_space_constraint(a, pltpu.SMEM) for a in arrays]
+
+
 def streamed(*arrays):
     return [pltpu.with_memory_space_constraint(a, pltpu.HBM) for a in arrays]
 
 
-def run(kernel, args, specs, outs, out_specs, steps=None, scratch=(), cost=(0, 0)):
+def run(kernel, args, specs, outs, out_specs, steps=None, scratch=(), alias=None, cost=(0, 0)):
     return pl.pallas_call(
         kernel,
         out_shape=outs,
@@ -430,6 +461,7 @@
         in_specs=specs,
         out_specs=out_specs,
         scratch_shapes=scratch,
+        input_output_aliases=alias or {},
         cost_estimate=pl.CostEstimate(flops=cost[0], bytes_accessed=cost[1], transcendentals=0),
         compiler_params=pltpu.CompilerParams(vmem_limit_bytes=16 << 20),
     )(*args)
@@ -438,36 +470,51 @@
 def body(queries, keys, values, out_grad, gain, rates, docs):
     tokens, heads, dim = queries.shape
     wide = 8 if heads % 8 == 0 else heads
-    count = 4 if heads % 4 == 0 else heads
-    groups, steps = heads // count, heads // wide
+    count = 4 if wide % 4 == 0 else wide
+    span = heads // (CHUNKS if heads % (CHUNKS * count) == 0 else 1)
+    steps, groups = heads // wide, span // count
+    total_groups = heads // count
     rows = tokens // 2
     hops = hop_count(tokens)
     width = heads * dim * lax.axis_size("head")
+    chunks = range(heads // span)
+    last = heads // span - 1
     shape = lambda *s: jax.ShapeDtypeStruct(s, F32)
     major = pltpu.VMEM((heads, tokens, dim), BF16)
+    chunk = pltpu.VMEM((span, tokens, dim), BF16)
     some = pltpu.VMEM((count, tokens, dim), BF16)
-    half = shape(heads, dim // 2, dim)
+    half = shape(span, dim // 2, dim)
     token_block = pl.BlockSpec((tokens, wide, dim), lambda i: (0, i, 0))
-    half_block = pl.BlockSpec((wide, dim // 2, dim), lambda i: (i, 0, 0))
     unit = heads * tokens * dim
+    rates, docs, gain = streamed(rates, docs, gain)
 
     kh, vh, leave, keep = run(
         state_kernel,
         [docs, rates, *streamed(keys, values)],
         [SMEM, SMEM, token_block, token_block],
-        [major, major, half, half],
-        [VMEM, VMEM, half_block, half_block],
+        [major, major] + [shape(heads, dim // 2, dim)] * 2,
+        [VMEM] * 4,
         steps=steps,
         cost=(2 * unit * dim, 8 * unit),
     )
 
+    halves = [x[c * span : (c + 1) * span] for c in chunks for x in (leave, keep)]
+
     spans = sum(len(rows) for rows in fade_rows(hops))
-    limits, distance = run(
-        partial(setup_kernel, hops),
+    info, rates = run(
+        partial(setup_kernel, hops, tokens),
+        [docs, rates],
+        [SMEM] * 2,
+        [pltpu.SMEM((FADES + spans,), jnp.int32), pltpu.SMEM((heads,), F32)],
+        [SMEM] * 2,
+    )
+    info, rates = at_hand(info, rates)
+    distance = run(
+        mask_kernel,
         [docs],
         [SMEM],
-        [jax.ShapeDtypeStruct((FADES + spans,), jnp.int32), pltpu.VMEM((tokens, tokens), F32)],
-        [SMEM, VMEM],
+        pltpu.VMEM((tokens, tokens), F32),
+        VMEM,
         scratch=[pltpu.VMEM((tokens, dim), jnp.int32)],
         cost=(0, 2 * tokens * tokens),
     )
@@ -482,71 +529,113 @@
         cost=(0, 8 * unit),
     )
     near, probs = [], []
-    for g in range(groups):
+    for g in range(total_groups):
         n, p = run(
             partial(scores_kernel, g * count, rows),
             [rates, *kept(qh, kh, vh, distance)],
             [SMEM] + [VMEM] * 4,
             [some, pltpu.VMEM((count, tokens, tokens), BF16)],
             [VMEM] * 2,
-            cost=(4 * unit * tokens // groups, 0),
+            cost=(4 * unit * tokens // total_groups, 0),
         )
         near.append(n), probs.append(p)
 
-    mine, other = entering_state(leave, keep, limits, rates, True, hops)
-    attn, states, stats = run(
-        partial(attend_kernel, groups),
-        [limits, rates, *kept(qh, gh), gain, mine, other, *kept(*near)],
-        [SMEM, SMEM] + [VMEM] * (5 + groups),
-        [major, pltpu.VMEM((heads, dim, dim), BF16), shape(2, tokens)],
-        [VMEM] * 3,
-        cost=(2 * unit * dim, 4 * unit),
-    )
+    attn, states, stats = [], [], None
+    for c in chunks:
+        mine, other = entering_state(*halves[2 * c : 2 * c + 2], info, rates, c * span, True, hops)
+        begin, final = c == 0, c == last
+        args = [info, rates, *kept(qh, gh), gain, mine, other, *kept(*near[c * groups : (c + 1) * groups])]
+        if not begin:
+            args += kept(stats)
+        a, s, stats = run(
+            partial(attend_kernel, c * span, groups, begin, final),
+            args,
+            [SMEM, SMEM] + [VMEM] * (len(args) - 2),
+            [
+                chunk,
+                pltpu.VMEM((span, dim, dim), BF16),
+                shape(2, tokens) if final else pltpu.VMEM((2, tokens, dim), F32),
+            ],
+            [VMEM] * 3,
+            cost=(2 * unit * dim // len(chunks), 0),
+        )
+        attn.append(a), states.append(s)
     parts = head_sum_parts(stats)
 
-    grads, leave, keep = run(
-        partial(norm_kernel, width, len(parts)),
-        [limits, rates, *parts, *kept(attn, gh, qh), gain],
-        [SMEM, SMEM] + [VMEM] * (len(parts) + 4),
-        [major, half, half],
-        [VMEM] * 3,
-        cost=(2 * unit * dim, 4 * unit),
-    )
+    grads, halves = [], []
+    for c in chunks:
+        g, *pair = run(
+            partial(norm_kernel, c * span, width, len(parts)),
+            [info, rates, *parts, *kept(attn[c], gh, qh), gain],
+            [SMEM, SMEM] + [VMEM] * (len(parts) + 4),
+            [chunk, half, half],
+            [VMEM] * 3,
+            cost=(2 * unit * dim // len(chunks), 0),
+        )
+        grads.append(g), halves.extend(pair)
 
     dqh, dk_part, dv_part = [], [], []
-    for g in range(groups):
-        a, b, c = run(
-            partial(grads_kernel, g * count, rows),
-            [limits, rates, *kept(grads, qh, kh, vh, probs[g], distance, states)],
+    for g in range(total_groups):
+        c, at = divmod(g, groups)
+        parts = run(
+            partial(grads_kernel, c * span, at * count, rows),
+            [info, rates, *kept(grads[c], qh, kh, vh, probs[g], distance, states[c])],
             [SMEM, SMEM] + [VMEM] * 7,
             [some] * 3,
             [VMEM] * 3,
-            cost=(8 * unit * tokens // groups, 0),
-        )
-        dqh.append(a), dk_part.append(b), dv_part.append(c)
+            cost=(8 * unit * tokens // total_groups, 0),
+        )
+        for kind, part in zip((dqh, dk_part, dv_part), parts):
+            kind.append(part)
     full = jax.ShapeDtypeStruct((tokens, heads, dim), BF16)
     dq = run(
         partial(turn_back_kernel, steps),
         kept(*dqh),
-        [VMEM] * groups,
+        [VMEM] * total_groups,
         full,
         token_block,
         steps=steps,
         cost=(0, 2 * unit),
     )
 
-    mine, other = entering_state(leave, keep, limits, rates, False, hops)
-    dk, dv = run(
-        partial(finish_kernel, groups),
-        [limits, rates, *kept(kh, vh), mine, other, *kept(*dk_part, *dv_part)],
-        [SMEM, SMEM, VMEM, VMEM, half_block, half_block] + [VMEM] * (2 * groups),
-        [full, full],
-        [token_block, token_block],
-        steps=steps,
-        scratch=[pltpu.VMEM((wide, tokens, dim), BF16)] * 2 + [pltpu.VMEM((wide, dim, dim), BF16)],
-        cost=(4 * unit * dim, 4 * unit),
-    )
-    return dq, dk, dv
+    entered = [
+        entering_state(*halves[2 * c : 2 * c + 2], info, rates, c * span, False, hops)
+        for c in chunks
+    ]
+    made = []
+    if len(chunks) == 1:
+        ((mine, other),) = entered
+        half_block = pl.BlockSpec((wide, dim // 2, dim), lambda i: (i, 0, 0))
+        made = run(
+            partial(finish_kernel, None, total_groups // steps, steps),
+            [info, rates, *kept(kh, vh), mine, other, *kept(*dk_part, *dv_part)],
+            [SMEM, SMEM, VMEM, VMEM, half_block, half_block] + [VMEM] * (2 * total_groups),
+            [full, full],
+            [token_block, token_block],
+            steps=steps,
+            scratch=[pltpu.VMEM((wide, dim, dim), BF16)],
+            cost=(4 * unit * dim, 4 * unit),
+        )
+        return dq, *made
+    for c in chunks:
+        mine, other = entered[c]
+        here = slice(c * groups, (c + 1) * groups)
+        args = [info, rates, *kept(kh, vh), mine, other, *kept(*dk_part[here], *dv_part[here])]
+        specs = [SMEM, SMEM] + [VMEM] * (4 + 2 * groups)
+        alias = {len(args) + j: j for j in range(len(made))}
+        block = pl.BlockSpec((tokens, wide, dim), lambda i, c=c: (0, c, 0))
+        made = run(
+            partial(finish_kernel, c * span, groups, 1),
+            args + list(made),
+            specs + [pl.BlockSpec(memory_space=pl.ANY)] * len(made),
+            [full, full],
+            [block, block],
+            steps=1,
+            scratch=[pltpu.VMEM((wide, dim, dim), BF16)],
+            alias=alias,
+            cost=(4 * unit * dim // len(chunks), 4 * unit // len(chunks)),
+        )
+    return dq, *made
 
 
 def solution(mesh):

time: 129 us -> 118 us (0.915)
  Pallas kernels: 52.1 us -> 43.2 us
  local copies, waits for them, and re-layouts: 1.32 us -> 0 us
    pallas_call x23 -> x24, Pallas kernels: 52.1 us -> 43.2 us  [run(): pl.pallas_call(kernel, out_shape=outs, grid=() if steps is None else (ste...]
    unnamed x10 -> x0, local copies, waits for them, and re-layouts: 1.32 us -> none
  transfers between devices with their start and end apart: 13 -> 13, of which waited for: 10 -> 11; matrix products, arithmetic and copies ran while one was open for 0% -> 0% of each run, Pallas kernels for 26% -> 25%
where the time goes in v3:
time: 118 us; the launch traced here: 116 us
  waiting for transfers between devices  56.6 us (48%)
  Pallas kernels  43.2 us (37%)
  starting transfers between devices  15.5 us (13%)
    ppermute x13, waiting for transfers between devices, send(): return lax.ppermute(block, axis, route)  56.6 us
    pallas_call x24, Pallas kernels, run(): pl.pallas_call(kernel, out_shape=outs, grid=() if steps is None else (ste...  43.2 us
    ppermute x13, starting transfers between devices, send(): return lax.ppermute(block, axis, route)  15.5 us
  transfers between devices with their start and end apart: 13, of which 11 were waited for; matrix products, arithmetic and copies ran while one was open for 0% of the time, Pallas kernels for 25%

profile of v3, /device:TPU:12, one launch (start us, length us, event | category | flops | bytes accessed | tf_op | source)
XLA Modules:
  0.0 116.2 jit_solution(15748449080934541196)
XLA Ops:
  0.6 4.2 %shard_map.96 = (bf16[16,512,128]{2,1,0:T(8,128)(2,1)S(1)}, bf16[16,512,128]{2,1,0:T(8,128)(2,1)S(1)}, f32[16,64,128]{2,1,0:T(8,128)S(1)}, f32[16,64,128]{2,1,0:T(8,128)S(1)}) custom-call(s32[32]{0:T(128)} %docs_ref.5, f32[16]{0:T(128)} %rate_ref.1, bf16[512,16,128]{2,1,0:T(8,128)(2,1)} %k_ref.1, bf16[512,16,128]{2,1,0:T(8,128)(2,1)} %v_ref.1), custom_call_target="tpu_custom_call" | custom-call | flops 268435456 | bytes 8388608 | tf_op jit(solution)/shard_map/pallas_call | solution.py:457
  4.9 1.7 %shard_map.94 = (s32[19]{0:T(128)S(4)}, f32[16]{0:T(128)S(4)}) custom-call(s32[32]{0:T(128)} %docs_ref.5, f32[16]{0:T(128)} %rate_ref.1), custom_call_target="tpu_custom_call" | custom-call | tf_op jit(solution)/shard_map/pallas_call | solution.py:457
  7.5 8.1 %collective-permute-done.1.came_ref = f32[16,32,128]{2,1,0:T(8,128)S(1)} collective-permute-done((f32[16,32,128]{2,1,0:T(8,128)S(1)}, f32[16,32,128]{2,1,0:T(8,128)S(1)}, u32[]{:S(2)}, u32[]{:S(2)}) %collective-permute-start.1) | collective-permute-done | bytes 262176 | tf_op jit(solution)/shard_map/ppermute | solution.py:380
  15.6 3.5 %collective-permute-start.2 = (f32[16,32,128]{2,1,0:T(8,128)S(1)}, f32[16,32,128]{2,1,0:T(8,128)S(1)}, u32[]{:S(2)}, u32[]{:S(2)}) collective-permute-start(f32[16,32,128]{2,1,0:T(8,128)S(1)} %shard_map.98), channel_id=1, source_target_pairs={{0,4},{1,5},{2,6},{3,7},{4,8},{5,9},{6,10},{7,11},{8,12},{9,13},{1... | collective-permute-start | bytes 786440 | tf_op jit(solution)/shard_map/ppermute | solution.py:380
  19.1 6.1 %collective-permute-done.2.refs_0_ = f32[16,32,128]{2,1,0:T(8,128)S(1)} collective-permute-done((f32[16,32,128]{2,1,0:T(8,128)S(1)}, f32[16,32,128]{2,1,0:T(8,128)S(1)}, u32[]{:S(2)}, u32[]{:S(2)}) %collective-permute-start.2) | collective-permute-done | bytes 262176 | tf_op jit(solution)/shard_map/ppermute | solution.py:380
  25.2 3.5 %collective-permute-start.3 = (f32[16,32,128]{2,1,0:T(8,128)S(1)}, f32[16,32,128]{2,1,0:T(8,128)S(1)}, u32[]{:S(2)}, u32[]{:S(2)}) collective-permute-start(f32[16,32,128]{2,1,0:T(8,128)S(1)} %collective-permute-done.2.refs_0_), channel_id=1, source_target_pairs={{0,4},{1,5},{2,6},{3,7},{4,8},{5,9},{6,10},{7,11},{8,12},{9,13},{1... | collective-permute-start | bytes 786440 | tf_op jit(solution)/shard_map/ppermute | solution.py:380
  28.7 5.3 %collective-permute-done.3.refs_1_ = f32[16,32,128]{2,1,0:T(8,128)S(1)} collective-permute-done((f32[16,32,128]{2,1,0:T(8,128)S(1)}, f32[16,32,128]{2,1,0:T(8,128)S(1)}, u32[]{:S(2)}, u32[]{:S(2)}) %collective-permute-start.3) | collective-permute-done | bytes 262176 | tf_op jit(solution)/shard_map/ppermute | solution.py:380
  34.7 5.9 %collective-permute-done.4.came_part_ref = f32[16,32,128]{2,1,0:T(8,128)S(1)} collective-permute-done((f32[16,32,128]{2,1,0:T(8,128)S(1)}, f32[16,32,128]{2,1,0:T(8,128)S(1)}, u32[]{:S(2)}, u32[]{:S(2)}) %collective-permute-start.4) | collective-permute-done | bytes 262176 | tf_op jit(solution)/shard_map/ppermute | solution.py:380
  40.7 1.2 %shard_map.101.dist_ref = f32[512,512]{1,0:T(8,128)S(1)} custom-call(s32[32]{0:T(128)} %docs_ref.5), custom_call_target="tpu_custom_call" | custom-call | bytes 524288 | tf_op jit(solution)/shard_map/pallas_call | solution.py:457
  42.0 2.6 %shard_map.95 = (bf16[16,512,128]{2,1,0:T(8,128)(2,1)S(1)}, bf16[16,512,128]{2,1,0:T(8,128)(2,1)S(1)}) custom-call(bf16[512,16,128]{2,1,0:T(8,128)(2,1)} %q_ref.1, bf16[512,16,128]{2,1,0:T(8,128)(2,1)} %g_ref.1), custom_call_target="tpu_custom_call" | custom-call | bytes 8388608 | tf_op jit(solution)/shard_map/pallas_call | solution.py:457
  44.6 2.2 %shard_map.105 = (bf16[4,512,128]{2,1,0:T(8,128)(2,1)S(1)}, bf16[4,512,512]{2,1,0:T(8,128)(2,1)S(1)}) custom-call(f32[16]{0:T(128)S(4)} %get-tuple-element.52.rate_ref, bf16[16,512,128]{2,1,0:T(8,128)(2,1)S(1)} %get-tuple-element.53.qh_ref.refs_4_, bf16[16,512,128]{2,1,0:T(8,128)(2,1)S(1)} %get-tuple-element.63.kh_ref, ...), custom_call_target="tpu_custom_call" | custom-call | flops 536870912 | tf_op jit(solution)/shard_map/pallas_call | solution.py:457
  46.8 2.2 %shard_map.104 = (bf16[4,512,128]{2,1,0:T(8,128)(2,1)S(1)}, bf16[4,512,512]{2,1,0:T(8,128)(2,1)S(1)}) custom-call(f32[16]{0:T(128)S(4)} %get-tuple-element.52.rate_ref, bf16[16,512,128]{2,1,0:T(8,128)(2,1)S(1)} %get-tuple-element.53.qh_ref.refs_4_, bf16[16,512,128]{2,1,0:T(8,128)(2,1)S(1)} %get-tuple-element.63.kh_ref, ...), custom_call_target="tpu_custom_call" | custom-call | flops 536870912 | tf_op jit(solution)/shard_map/pallas_call | solution.py:457
  49.0 2.2 %shard_map.103 = (bf16[4,512,128]{2,1,0:T(8,128)(2,1)S(1)}, bf16[4,512,512]{2,1,0:T(8,128)(2,1)S(1)}) custom-call(f32[16]{0:T(128)S(4)} %get-tuple-element.52.rate_ref, bf16[16,512,128]{2,1,0:T(8,128)(2,1)S(1)} %get-tuple-element.53.qh_ref.refs_4_, bf16[16,512,128]{2,1,0:T(8,128)(2,1)S(1)} %get-tuple-element.63.kh_ref, ...), custom_call_target="tpu_custom_call" | custom-call | flops 536870912 | tf_op jit(solution)/shard_map/pallas_call | solution.py:457
  51.3 2.2 %shard_map.102 = (bf16[4,512,128]{2,1,0:T(8,128)(2,1)S(1)}, bf16[4,512,512]{2,1,0:T(8,128)(2,1)S(1)}) custom-call(f32[16]{0:T(128)S(4)} %get-tuple-element.52.rate_ref, bf16[16,512,128]{2,1,0:T(8,128)(2,1)S(1)} %get-tuple-element.53.qh_ref.refs_4_, bf16[16,512,128]{2,1,0:T(8,128)(2,1)S(1)} %get-tuple-element.63.kh_ref, ...), custom_call_target="tpu_custom_call" | custom-call | flops 536870912 | tf_op jit(solution)/shard_map/pallas_call | solution.py:457
  53.5 2.7 %shard_map.106 = (bf16[16,512,128]{2,1,0:T(8,128)(2,1)S(1)}, bf16[16,128,128]{2,1,0:T(8,128)(2,1)S(1)}, f32[2,512]{1,0:T(2,128)S(1)}) custom-call(s32[19]{0:T(128)S(4)} %get-tuple-element.51.info_ref, f32[16]{0:T(128)S(4)} %get-tuple-element.52.rate_ref, bf16[16,512,128]{2,1,0:T(8,128)(2,1)S(1)} %get-tuple-element.53.qh_ref.refs_4_, ...), custom_call_target="tpu_custom_call" | custom-call | flops 268435456 | tf_op jit(solution)/shard_map/pallas_call | solution.py:457
  56.2 1.6 %collective-permute-start.6 = (f32[2,512]{1,0:T(2,128)S(1)}, f32[2,512]{1,0:T(2,128)S(1)}, u32[]{:S(2)}, u32[]{:S(2)}) collective-permute-start(f32[2,512]{1,0:T(2,128)S(1)} %get-tuple-element.69.refs_0_), channel_id=1, source_target_pairs={{0,16},{16,0},{1,17},{17,1},{2,18},{18,2},{3,19},{19,3},{4,20},{20... | collective-permute-start | bytes 12296 | tf_op jit(solution)/shard_map/ppermute | solution.py:380
  57.8 2.1 %collective-permute-done.6.refs_1_ = f32[2,512]{1,0:T(2,128)S(1)} collective-permute-done((f32[2,512]{1,0:T(2,128)S(1)}, f32[2,512]{1,0:T(2,128)S(1)}, u32[]{:S(2)}, u32[]{:S(2)}) %collective-permute-start.6) | collective-permute-done | bytes 4128 | tf_op jit(solution)/shard_map/ppermute | solution.py:380
  59.9 2.9 %shard_map.107 = (bf16[16,512,128]{2,1,0:T(8,128)(2,1)S(1)}, f32[16,64,128]{2,1,0:T(8,128)S(1)}, f32[16,64,128]{2,1,0:T(8,128)S(1)}) custom-call(s32[19]{0:T(128)S(4)} %get-tuple-element.51.info_ref, f32[16]{0:T(128)S(4)} %get-tuple-element.52.rate_ref, f32[2,512]{1,0:T(2,128)S(1)} %get-tuple-element.69.refs_0_, ...), custom_call_target="tpu_custom_call" | custom-call | flops 268435456 | tf_op jit(solution)/shard_map/pallas_call | solution.py:457
  62.9 1.9 %collective-permute-done.7.came_ref = f32[16,64,128]{2,1,0:T(8,128)S(1)} collective-permute-done((f32[16,64,128]{2,1,0:T(8,128)S(1)}, f32[16,64,128]{2,1,0:T(8,128)S(1)}, u32[]{:S(2)}, u32[]{:S(2)}) %collective-permute-start.7) | collective-permute-done | bytes 524320 | tf_op jit(solution)/shard_map/ppermute | solution.py:380
  64.9 0.7 collective-permute-start.8
  65.5 7.8 %collective-permute-done.8.came_ref = f32[16,32,128]{2,1,0:T(8,128)S(1)} collective-permute-done((f32[16,32,128]{2,1,0:T(8,128)S(1)}, f32[16,32,128]{2,1,0:T(8,128)S(1)}, u32[]{:S(2)}, u32[]{:S(2)}) %collective-permute-start.8) | collective-permute-done | bytes 262176 | tf_op jit(solution)/shard_map/ppermute | solution.py:380
  73.4 1.9 %collective-permute-start.9 = (f32[16,32,128]{2,1,0:T(8,128)S(1)}, f32[16,32,128]{2,1,0:T(8,128)S(1)}, u32[]{:S(2)}, u32[]{:S(2)}) collective-permute-start(f32[16,32,128]{2,1,0:T(8,128)S(1)} %shard_map.114), channel_id=1, source_target_pairs={{4,0},{5,1},{6,2},{7,3},{8,4},{9,5},{10,6},{11,7},{12,8},{13,9},{1... | collective-permute-start | bytes 786440 | tf_op jit(solution)/shard_map/ppermute | solution.py:380
  75.3 7.5 %collective-permute-done.9.refs_0_ = f32[16,32,128]{2,1,0:T(8,128)S(1)} collective-permute-done((f32[16,32,128]{2,1,0:T(8,128)S(1)}, f32[16,32,128]{2,1,0:T(8,128)S(1)}, u32[]{:S(2)}, u32[]{:S(2)}) %collective-permute-start.9) | collective-permute-done | bytes 262176 | tf_op jit(solution)/shard_map/ppermute | solution.py:380
  82.7 2.4 %collective-permute-start.10 = (f32[16,32,128]{2,1,0:T(8,128)S(1)}, f32[16,32,128]{2,1,0:T(8,128)S(1)}, u32[]{:S(2)}, u32[]{:S(2)}) collective-permute-start(f32[16,32,128]{2,1,0:T(8,128)S(1)} %collective-permute-done.9.refs_0_), channel_id=1, source_target_pairs={{4,0},{5,1},{6,2},{7,3},{8,4},{9,5},{10,6},{11,7},{12,8},{13,9},{1... | collective-permute-start | bytes 786440 | tf_op jit(solution)/shard_map/ppermute | solution.py:380
  85.1 6.1 %collective-permute-done.10.refs_1_ = f32[16,32,128]{2,1,0:T(8,128)S(1)} collective-permute-done((f32[16,32,128]{2,1,0:T(8,128)S(1)}, f32[16,32,128]{2,1,0:T(8,128)S(1)}, u32[]{:S(2)}, u32[]{:S(2)}) %collective-permute-start.10) | collective-permute-done | bytes 262176 | tf_op jit(solution)/shard_map/ppermute | solution.py:380
  92.0 5.8 %collective-permute-done.11.came_part_ref = f32[16,32,128]{2,1,0:T(8,128)S(1)} collective-permute-done((f32[16,32,128]{2,1,0:T(8,128)S(1)}, f32[16,32,128]{2,1,0:T(8,128)S(1)}, u32[]{:S(2)}, u32[]{:S(2)}) %collective-permute-start.11) | collective-permute-done | bytes 262176 | tf_op jit(solution)/shard_map/ppermute | solution.py:380
  98.0 3.3 %shard_map.111 = (bf16[4,512,128]{2,1,0:T(8,128)(2,1)S(1)}, bf16[4,512,128]{2,1,0:T(8,128)(2,1)S(1)}, bf16[4,512,128]{2,1,0:T(8,128)(2,1)S(1)}) custom-call(s32[19]{0:T(128)S(4)} %get-tuple-element.51.info_ref, f32[16]{0:T(128)S(4)} %get-tuple-element.52.rate_ref, bf16[16,512,128]{2,1,0:T(8,128)(2,1)S(1)} %get-tuple-element.71.grad_ref, ...), custom_call_target="tpu_custom_call" | custom-call | flops 1073741824 | tf_op jit(solution)/shard_map/pallas_call | solution.py:457
  101.4 3.3 %shard_map.110 = (bf16[4,512,128]{2,1,0:T(8,128)(2,1)S(1)}, bf16[4,512,128]{2,1,0:T(8,128)(2,1)S(1)}, bf16[4,512,128]{2,1,0:T(8,128)(2,1)S(1)}) custom-call(s32[19]{0:T(128)S(4)} %get-tuple-element.51.info_ref, f32[16]{0:T(128)S(4)} %get-tuple-element.52.rate_ref, bf16[16,512,128]{2,1,0:T(8,128)(2,1)S(1)} %get-tuple-element.71.grad_ref, ...), custom_call_target="tpu_custom_call" | custom-call | flops 1073741824 | tf_op jit(solution)/shard_map/pallas_call | solution.py:457
  104.7 3.3 %shard_map.109 = (bf16[4,512,128]{2,1,0:T(8,128)(2,1)S(1)}, bf16[4,512,128]{2,1,0:T(8,128)(2,1)S(1)}, bf16[4,512,128]{2,1,0:T(8,128)(2,1)S(1)}) custom-call(s32[19]{0:T(128)S(4)} %get-tuple-element.51.info_ref, f32[16]{0:T(128)S(4)} %get-tuple-element.52.rate_ref, bf16[16,512,128]{2,1,0:T(8,128)(2,1)S(1)} %get-tuple-element.71.grad_ref, ...), custom_call_target="tpu_custom_call" | custom-call | flops 1073741824 | tf_op jit(solution)/shard_map/pallas_call | solution.py:457
  108.1 3.3 %shard_map.108 = (bf16[4,512,128]{2,1,0:T(8,128)(2,1)S(1)}, bf16[4,512,128]{2,1,0:T(8,128)(2,1)S(1)}, bf16[4,512,128]{2,1,0:T(8,128)(2,1)S(1)}) custom-call(s32[19]{0:T(128)S(4)} %get-tuple-element.51.info_ref, f32[16]{0:T(128)S(4)} %get-tuple-element.52.rate_ref, bf16[16,512,128]{2,1,0:T(8,128)(2,1)S(1)} %get-tuple-element.71.grad_ref, ...), custom_call_target="tpu_custom_call" | custom-call | flops 1073741824 | tf_op jit(solution)/shard_map/pallas_call | solution.py:457
  111.4 1.5 %shard_map.112 = bf16[512,16,128]{2,1,0:T(8,128)(2,1)} custom-call(bf16[4,512,128]{2,1,0:T(8,128)(2,1)S(1)} %get-tuple-element.74.refs_0_, bf16[4,512,128]{2,1,0:T(8,128)(2,1)S(1)} %get-tuple-element.76.refs_1_, bf16[4,512,128]{2,1,0:T(8,128)(2,1)S(1)} %get-tuple-element.78.refs_2_, bf16[4,512,128]{2,1,0:T(8,128)(2,1)S(1)} %get-tuple-element.80.refs_3_), custom_call_target="tpu_custom_call" | custom-call | bytes 2097152 | tf_op jit(solution)/shard_map/pallas_call | solution.py:457
  112.9 3.3 %shard_map.117 = (bf16[512,16,128]{2,1,0:T(8,128)(2,1)}, bf16[512,16,128]{2,1,0:T(8,128)(2,1)}) custom-call(s32[19]{0:T(128)S(4)} %get-tuple-element.51.info_ref, f32[16]{0:T(128)S(4)} %get-tuple-element.52.rate_ref, bf16[16,512,128]{2,1,0:T(8,128)(2,1)S(1)} %get-tuple-element.63.kh_ref, bf16[16,512,128]{2,1,0:T(8,128)(2,1)S(1)} %get-tuple-element.64.vh_ref, ...), custom_call_target="tpu_custom_call" | custom-call | flops 536870912 | bytes 4194304 | tf_op jit(solution)/shard_map/pallas_call | solution.py:457
  (18 shorter events, 3.1 us)
Async XLA Ops:
  4.9 2.0 %collective-permute-start = (f32[16,64,128]{2,1,0:T(8,128)S(1)}, f32[16,64,128]{2,1,0:T(8,128)S(1)}, u32[]{:S(2)}, u32[]{:S(2)}) collective-permute-start(f32[16,64,128]{2,1,0:T(8,128)S(1)} %get-tuple-element.56), channel_id=1, source_target_pairs={{0,1},{1,0},{2,3},{3,2},{4,5},{5,4},{6,7},{7,6},{8,9},{9,8},{10,11... | collective-permute-start | bytes 1572872 | tf_op jit(solution)/shard_map/ppermute | solution.py:380
  6.9 8.6 %collective-permute-start.1 = (f32[16,32,128]{2,1,0:T(8,128)S(1)}, f32[16,32,128]{2,1,0:T(8,128)S(1)}, u32[]{:S(2)}, u32[]{:S(2)}) collective-permute-start(f32[16,32,128]{2,1,0:T(8,128)S(1)} %get-tuple-element.58), channel_id=1, source_target_pairs={{0,2},{1,3},{2,0},{3,1},{4,6},{5,7},{6,4},{7,5},{8,10},{9,11},{10,... | collective-permute-start | bytes 786440 | tf_op jit(solution)/shard_map/ppermute | solution.py:380
  15.6 9.6 %collective-permute-start.2 = (f32[16,32,128]{2,1,0:T(8,128)S(1)}, f32[16,32,128]{2,1,0:T(8,128)S(1)}, u32[]{:S(2)}, u32[]{:S(2)}) collective-permute-start(f32[16,32,128]{2,1,0:T(8,128)S(1)} %shard_map.98), channel_id=1, source_target_pairs={{0,4},{1,5},{2,6},{3,7},{4,8},{5,9},{6,10},{7,11},{8,12},{9,13},{1... | collective-permute-start | bytes 786440 | tf_op jit(solution)/shard_map/ppermute | solution.py:380
  25.2 8.7 %collective-permute-start.3 = (f32[16,32,128]{2,1,0:T(8,128)S(1)}, f32[16,32,128]{2,1,0:T(8,128)S(1)}, u32[]{:S(2)}, u32[]{:S(2)}) collective-permute-start(f32[16,32,128]{2,1,0:T(8,128)S(1)} %collective-permute-done.2.refs_0_), channel_id=1, source_target_pairs={{0,4},{1,5},{2,6},{3,7},{4,8},{5,9},{6,10},{7,11},{8,12},{9,13},{1... | collective-permute-start | bytes 786440 | tf_op jit(solution)/shard_map/ppermute | solution.py:380
  34.1 6.4 %collective-permute-start.4 = (f32[16,32,128]{2,1,0:T(8,128)S(1)}, f32[16,32,128]{2,1,0:T(8,128)S(1)}, u32[]{:S(2)}, u32[]{:S(2)}) collective-permute-start(f32[16,32,128]{2,1,0:T(8,128)S(1)} %get-tuple-element.60), channel_id=1, source_target_pairs={{0,2},{1,3},{2,0},{3,1},{4,6},{5,7},{6,4},{7,5},{8,10},{9,11},{10,... | collective-permute-start | bytes 786440 | tf_op jit(solution)/shard_map/ppermute | solution.py:380
  40.7 12.8 %collective-permute-start.5 = (f32[16,64,128]{2,1,0:T(8,128)S(1)}, f32[16,64,128]{2,1,0:T(8,128)S(1)}, u32[]{:S(2)}, u32[]{:S(2)}) collective-permute-start(f32[16,64,128]{2,1,0:T(8,128)S(1)} %get-tuple-element.62), channel_id=1, source_target_pairs={{0,1},{1,0},{2,3},{3,2},{4,5},{5,4},{6,7},{7,6},{8,9},{9,8},{10,11... | collective-permute-start | bytes 1572872 | tf_op jit(solution)/shard_map/ppermute | solution.py:380
  56.2 3.7 %collective-permute-start.6 = (f32[2,512]{1,0:T(2,128)S(1)}, f32[2,512]{1,0:T(2,128)S(1)}, u32[]{:S(2)}, u32[]{:S(2)}) collective-permute-start(f32[2,512]{1,0:T(2,128)S(1)} %get-tuple-element.69.refs_0_), channel_id=1, source_target_pairs={{0,16},{16,0},{1,17},{17,1},{2,18},{18,2},{3,19},{19,3},{4,20},{20... | collective-permute-start | bytes 12296 | tf_op jit(solution)/shard_map/ppermute | solution.py:380
  62.8 2.0 %collective-permute-start.7 = (f32[16,64,128]{2,1,0:T(8,128)S(1)}, f32[16,64,128]{2,1,0:T(8,128)S(1)}, u32[]{:S(2)}, u32[]{:S(2)}) collective-permute-start(f32[16,64,128]{2,1,0:T(8,128)S(1)} %get-tuple-element.82), channel_id=1, source_target_pairs={{0,1},{1,0},{2,3},{3,2},{4,5},{5,4},{6,7},{7,6},{8,9},{9,8},{10,11... | collective-permute-start | bytes 1572872 | tf_op jit(solution)/shard_map/ppermute | solution.py:380
  64.9 8.4 %collective-permute-start.8 = (f32[16,32,128]{2,1,0:T(8,128)S(1)}, f32[16,32,128]{2,1,0:T(8,128)S(1)}, u32[]{:S(2)}, u32[]{:S(2)}) collective-permute-start(f32[16,32,128]{2,1,0:T(8,128)S(1)} %get-tuple-element.84), channel_id=1, source_target_pairs={{0,2},{1,3},{2,0},{3,1},{4,6},{5,7},{6,4},{7,5},{8,10},{9,11},{10,... | collective-permute-start | bytes 786440 | tf_op jit(solution)/shard_map/ppermute | solution.py:380
  73.4 9.4 %collective-permute-start.9 = (f32[16,32,128]{2,1,0:T(8,128)S(1)}, f32[16,32,128]{2,1,0:T(8,128)S(1)}, u32[]{:S(2)}, u32[]{:S(2)}) collective-permute-start(f32[16,32,128]{2,1,0:T(8,128)S(1)} %shard_map.114), channel_id=1, source_target_pairs={{4,0},{5,1},{6,2},{7,3},{8,4},{9,5},{10,6},{11,7},{12,8},{13,9},{1... | collective-permute-start | bytes 786440 | tf_op jit(solution)/shard_map/ppermute | solution.py:380
  82.7 8.5 %collective-permute-start.10 = (f32[16,32,128]{2,1,0:T(8,128)S(1)}, f32[16,32,128]{2,1,0:T(8,128)S(1)}, u32[]{:S(2)}, u32[]{:S(2)}) collective-permute-start(f32[16,32,128]{2,1,0:T(8,128)S(1)} %collective-permute-done.9.refs_0_), channel_id=1, source_target_pairs={{4,0},{5,1},{6,2},{7,3},{8,4},{9,5},{10,6},{11,7},{12,8},{13,9},{1... | collective-permute-start | bytes 786440 | tf_op jit(solution)/shard_map/ppermute | solution.py:380
  91.4 6.4 %collective-permute-start.11 = (f32[16,32,128]{2,1,0:T(8,128)S(1)}, f32[16,32,128]{2,1,0:T(8,128)S(1)}, u32[]{:S(2)}, u32[]{:S(2)}) collective-permute-start(f32[16,32,128]{2,1,0:T(8,128)S(1)} %get-tuple-element.86), channel_id=1, source_target_pairs={{0,2},{1,3},{2,0},{3,1},{4,6},{5,7},{6,4},{7,5},{8,10},{9,11},{10,... | collective-permute-start | bytes 786440 | tf_op jit(solution)/shard_map/ppermute | solution.py:380
  98.0 14.9 %collective-permute-start.12 = (f32[16,64,128]{2,1,0:T(8,128)S(1)}, f32[16,64,128]{2,1,0:T(8,128)S(1)}, u32[]{:S(2)}, u32[]{:S(2)}) collective-permute-start(f32[16,64,128]{2,1,0:T(8,128)S(1)} %get-tuple-element.88), channel_id=1, source_target_pairs={{0,1},{1,0},{2,3},{3,2},{4,5},{5,4},{6,7},{7,6},{8,9},{9,8},{10,11... | collective-permute-start | bytes 1572872 | tf_op jit(solution)/shard_map/ppermute | solution.py:380

commit v4 on v3

--- a/solution.py
+++ b/solution.py
@@ -12,7 +12,7 @@
 LONGEST = 4096
 FAR = 1e30
 APART = 1 << 30
-CHUNKS = 1
+CHUNKS = 2
 F32 = jnp.float32
 BF16 = jnp.bfloat16
 
@@ -43,7 +43,8 @@
     send_ref[h] = jnp.where(core == 0, high, low)
 
 
-INDEX, BASE, NEXT_START, LATER_START, NEXT_BEGIN, FADES = range(6)
+INDEX, BASE, NEXT_START, LATER_START, NEXT_BEGIN = range(5)
+MID_NEXT, MID_LATER, MID_BEGIN, MID_AHEAD, MID_OWN, MID_BACK, FADES = range(5, 12)
 
 
 def fade_rows(hops):
@@ -78,25 +79,35 @@
     spot = lambda x, a, d: (((index ^ x) & a) + d) * tokens
     spans = [(spot(*row[:3]), spot(*row[3:])) for row in ahead + back]
     tops = [end - 1 for _, end in spans[: len(ahead)]] + [begin for begin, _ in spans[len(ahead) :]]
-    tops.append(base + tokens)
+    mid, top = base + tokens // 2, base + tokens
+    tops += [mid, top]
 
     def doc(j, carry):
-        start, upper, later, seen = carry
+        start, upper, later, mid_next, mid_later, seen = carry
         upper = jnp.where((start >= base) & (start < upper), start, upper)
         later = jnp.where((start > base) & (start < later), start, later)
+        mid_next = jnp.where((start >= mid) & (start < mid_next), start, mid_next)
+        mid_later = jnp.where((start > mid) & (start < mid_later), start, mid_later)
         seen = tuple(jnp.where(start <= top, start, old) for top, old in zip(tops, seen))
-        return start + docs_ref[j], upper, later, seen
+        return start + docs_ref[j], upper, later, mid_next, mid_later, seen
 
     zero = jnp.int32(0)
     far = jnp.int32(APART)
-    _, upper, later, seen = lax.fori_loop(
-        0, docs_ref.shape[0], doc, (zero, far, far, (zero,) * len(tops))
+    _, upper, later, mid_next, mid_later, seen = lax.fori_loop(
+        0, docs_ref.shape[0], doc, (zero, far, far, far, far, (zero,) * len(tops))
     )
     info_ref[INDEX] = index
     info_ref[BASE] = base
     info_ref[NEXT_START] = upper
     info_ref[LATER_START] = later
     info_ref[NEXT_BEGIN] = seen[-1]
+    info_ref[MID_NEXT] = mid_next
+    info_ref[MID_LATER] = mid_later
+    info_ref[MID_BEGIN] = seen[-2]
+    across = jnp.int32(tokens // 2)
+    info_ref[MID_AHEAD] = jnp.where(upper >= mid, across, far)
+    info_ref[MID_OWN] = jnp.where(later > mid, across, far)
+    info_ref[MID_BACK] = jnp.where(mid_later > top, across, far)
     for j, ((begin, end), last) in enumerate(zip(spans, seen)):
         forward = j < len(ahead)
         joined = last < begin if forward else last <= end
@@ -117,8 +128,10 @@
         return start + docs_ref[j]
 
     lax.fori_loop(0, docs_ref.shape[0], doc, jnp.int32(0))
-    for low in range(0, tokens, lanes):
-        spots = low + lax.broadcasted_iota(jnp.int32, (tokens, lanes), 1)
+    side = tokens // 2
+    across = jnp.where(row >= side, side, 0)
+    for low in range(0, side, lanes):
+        spots = across + low + lax.broadcasted_iota(jnp.int32, (tokens, lanes), 1)
         allowed = (spots <= row) & (spots >= begin_ref[...])
         dist_ref[:, low : low + lanes] = jnp.where(allowed, (row - spots).astype(F32), F32(FAR))
 
@@ -185,21 +198,31 @@
         send_ref[h] = jnp.where(is_first, later, half)
 
 
-def state_kernel(docs_ref, rate_ref, k_ref, v_ref, kh_ref, vh_ref, send_ref, keep_ref):
+def by_side(row, first, second):
+    return jnp.where(row < row.shape[0] // 2, first, second)
+
+
+def state_kernel(docs_ref, rate_ref, k_ref, v_ref, kh_ref, vh_ref, send_ref, keep_ref, half_ref):
     tokens, heads, dim = k_ref.shape
+    side = tokens // 2
     first = pl.program_id(0) * heads
     index = lax.axis_index("ctx")
-    end = (index + 1) * tokens
+    base = index * tokens
+    mid, end = base + side, base + tokens
 
     def scan(j, carry):
-        start, last = carry
+        start, mid_last, last = carry
+        mid_last = jnp.where(start <= mid - 1, start, mid_last)
         last = jnp.where(start <= end - 1, start, last)
-        return (start + docs_ref[j], last)
-
-    _, last = lax.fori_loop(0, docs_ref.shape[0], scan, (jnp.int32(0), jnp.int32(0)))
+        return (start + docs_ref[j], mid_last, last)
+
+    _, mid_last, last = lax.fori_loop(0, docs_ref.shape[0], scan, (jnp.int32(0),) * 3)
+    across = jnp.where(last < mid, jnp.int32(side), jnp.int32(APART))
     row = column(tokens, dim)
     distance = jnp.where(
-        row + index * tokens >= last, (tokens - 1 - row).astype(F32), F32(FAR)
+        row + base >= by_side(row, mid_last, last),
+        (by_side(row, side, tokens) - 1 - row).astype(F32),
+        F32(FAR),
     )
     turned_k = jnp.swapaxes(k_ref[...], 0, 1)
     turned_v = jnp.swapaxes(v_ref[...], 0, 1)
@@ -207,9 +230,13 @@
     vh_ref[pl.ds(first, heads)] = turned_v
     core = index & 1
     for h in range(heads):
-        tail = jnp.exp(-rate_ref[first + h] * distance)
+        rate = rate_ref[first + h]
+        tail = jnp.exp(-rate * distance)
         faded = (turned_k[h].astype(F32) * tail).astype(BF16)
-        split_halves(core, dot(faded, turned_v[h], TN), send_ref, keep_ref, first + h)
+        near = dot(faded[:side], turned_v[h, :side], TN)
+        half_ref[first + h] = near
+        state = spread(fade(rate, across, TILE), near) + dot(faded[side:], turned_v[h, side:], TN)
+        split_halves(core, state, send_ref, keep_ref, first + h)
 
 
 def turn_kernel(q_ref, g_ref, qh_ref, gh_ref):
@@ -226,54 +253,55 @@
         full = first + h
         rate = rate_ref[full]
         for low in range(0, tokens, rows):
-            top = low + rows
-            scores = dot(qh_ref[full, low:top, :], kh_ref[full, :top, :], NT)
-            decay = jnp.exp(-rate * dist_ref[low:top, :top])
-            probs = (scores * decay).astype(BF16)
-            probs_ref[h, low:top, :top] = probs
-            out_ref[h, low:top, :] = dot(probs, vh_ref[full, :top, :], NN).astype(BF16)
+            here = slice(low, low + rows)
+            scores = dot(qh_ref[full, here, :], kh_ref[full, here, :], NT)
+            probs = (scores * jnp.exp(-rate * dist_ref[here, :])).astype(BF16)
+            probs_ref[h, here, :] = probs
+            out_ref[h, here, :] = dot(probs, vh_ref[full, here, :], NN).astype(BF16)
         return carry
 
-    lax.fori_loop(0, heads, head, 0)
-
-
-def attend_kernel(base, groups, begin, final, info_ref, rate_ref, qh_ref, gh_ref, gain_ref, mine_ref, other_ref, *refs):
-    local_refs, refs = refs[:groups], refs[groups:]
-    if not begin:
-        sums_ref, refs = refs[0], refs[1:]
-    attn_ref, state_ref, stats_ref = refs
+    lax.fori_loop(0, heads, head, 0, unroll=2 if heads % 2 == 0 else 1)
+
+
+def entry_distance(info_ref, row):
+    side = row.shape[0] // 2
+    return jnp.where(
+        row + info_ref[BASE] < by_side(row, info_ref[NEXT_START], info_ref[MID_NEXT]),
+        (row + 1 - by_side(row, 0, side)).astype(F32),
+        F32(FAR),
+    )
+
+
+def attend_kernel(groups, info_ref, rate_ref, qh_ref, gh_ref, gain_ref, mine_ref, other_ref, half_ref, *refs):
+    local_refs, (attn_ref, state_ref, mid_ref, stats_ref) = refs[:groups], refs[groups:]
     heads, tokens, dim = attn_ref.shape
+    side = tokens // 2
     count = heads // groups
     core = info_ref[INDEX] & 1
-    row = column(tokens, dim)
-    distance = jnp.where(
-        row + info_ref[BASE] < info_ref[NEXT_START], (row + 1).astype(F32), F32(FAR)
-    )
-    if begin:
-        squares = jnp.zeros((tokens, dim), F32)
-        cross = jnp.zeros((tokens, dim), F32)
-    else:
-        squares, cross = sums_ref[0], sums_ref[1]
+    distance = entry_distance(info_ref, column(tokens, dim))
+    squares = jnp.zeros((tokens, dim), F32)
+    cross = jnp.zeros((tokens, dim), F32)
     for h in range(heads):
-        full = base + h
+        rate = rate_ref[h]
         put_halves(core, state_ref, h, mine_ref[h], other_ref[h])
-        factor = jnp.exp(-rate_ref[full] * distance)
+        state = state_ref[h]
+        mid = (spread(fade(rate, info_ref[MID_AHEAD], TILE), state.astype(F32)) + half_ref[h]).astype(BF16)
+        mid_ref[h] = mid
+        far = jnp.concatenate(
+            [dot(qh_ref[h, :side, :], state, NN), dot(qh_ref[h, side:, :], mid, NN)], axis=0
+        )
         near = local_refs[h // count][h % count].astype(F32)
-        attn = near + factor * dot(qh_ref[full], state_ref[h], NN)
+        attn = near + jnp.exp(-rate * distance) * far
         attn_ref[h] = attn.astype(BF16)
         squares += attn * attn
-        cross += gain_ref[full : full + 1, :] * gh_ref[full].astype(F32) * attn
-    if final:
-        stats_ref[0:1, :] = jnp.sum(jnp.swapaxes(squares, 0, 1), axis=0, keepdims=True)
-        stats_ref[1:2, :] = jnp.sum(jnp.swapaxes(cross, 0, 1), axis=0, keepdims=True)
-    else:
-        stats_ref[0] = squares
-        stats_ref[1] = cross
+        cross += gain_ref[h : h + 1, :] * gh_ref[h].astype(F32) * attn
+    stats_ref[0:1, :] = jnp.sum(jnp.swapaxes(squares, 0, 1), axis=0, keepdims=True)
+    stats_ref[1:2, :] = jnp.sum(jnp.swapaxes(cross, 0, 1), axis=0, keepdims=True)
 
 
 def norm_kernel(base, width, parts, info_ref, rate_ref, *refs):
     stats_refs, refs = refs[:parts], refs[parts:]
-    attn_ref, gh_ref, qh_ref, gain_ref, grad_ref, send_ref, keep_ref = refs
+    attn_ref, gh_ref, qh_ref, gain_ref, grad_ref, send_ref, keep_ref, half_ref = refs
     heads, tokens, dim = grad_ref.shape
     core = info_ref[INDEX] & 1
     stats = stats_refs[0][...]
@@ -285,49 +313,48 @@
     inverse = jnp.swapaxes(jnp.broadcast_to(inverse, (dim, tokens)), 0, 1)
     scale = jnp.swapaxes(jnp.broadcast_to(scale, (dim, tokens)), 0, 1)
     row = column(tokens, dim)
-    distance = jnp.where(row + info_ref[BASE] < info_ref[LATER_START], row.astype(F32), F32(FAR))
+    side = tokens // 2
+    distance = jnp.where(
+        row + info_ref[BASE] < by_side(row, info_ref[LATER_START], info_ref[MID_LATER]),
+        (row - by_side(row, 0, side)).astype(F32),
+        F32(FAR),
+    )
     for h in range(heads):
         full = base + h
         gained = gain_ref[full : full + 1, :] * gh_ref[full].astype(F32)
-        grad = (gained * inverse - attn_ref[h].astype(F32) * scale).astype(BF16)
+        grad = (gained * inverse - attn_ref[full].astype(F32) * scale).astype(BF16)
         grad_ref[h] = grad
         lead = jnp.exp(-rate_ref[full] * distance)
         faded = (qh_ref[full].astype(F32) * lead).astype(BF16)
-        split_halves(core, dot(faded, grad, TN), send_ref, keep_ref, h)
-
-
-def grads_kernel(base, first, rows, info_ref, rate_ref, grad_ref, qh_ref, kh_ref, vh_ref, probs_ref, dist_ref, state_ref, dq_ref, dk_ref, dv_ref):
+        near = dot(faded[side:], grad[side:], TN)
+        half_ref[h] = near
+        state = dot(faded[:side], grad[:side], TN)
+        state += spread(fade(rate_ref[full], info_ref[MID_OWN], TILE), near)
+        split_halves(core, state, send_ref, keep_ref, h)
+
+
+def grads_kernel(base, first, rows, info_ref, rate_ref, grad_ref, qh_ref, kh_ref, vh_ref, probs_ref, dist_ref, state_ref, mid_ref, dq_ref, dk_ref, dv_ref):
     heads, tokens, dim = dq_ref.shape
-    row = column(tokens, dim)
-    distance = jnp.where(
-        row + info_ref[BASE] < info_ref[NEXT_START], (row + 1).astype(F32), F32(FAR)
-    )
+    distance = entry_distance(info_ref, column(tokens, dim))
 
     def head(h, carry):
         near = first + h
         full = base + near
         rate = rate_ref[full]
         factor = jnp.exp(-rate * distance)
-        dk = dv = None
-        for low in range(tokens - rows, -1, -rows):
-            top = low + rows
-            grad = grad_ref[near, low:top, :]
-            raw = dot(grad, vh_ref[full, :top, :], NT)
-            weights = (raw * jnp.exp(-rate * dist_ref[low:top, :top])).astype(BF16)
-            dq = dot(weights, kh_ref[full, :top, :], NN)
-            dq += factor[low:top] * dot(grad, state_ref[near], NT)
-            dq_ref[h, low:top, :] = dq.astype(BF16)
-            dk_new = dot(weights, qh_ref[full, low:top, :], TN)
-            dv_new = dot(probs_ref[h, low:top, :top], grad, TN)
-            if dk is not None:
-                dk_new += dk[:top]
-                dv_new += dv[:top]
-            dk, dv = dk_new, dv_new
-            dk_ref[h, low:top, :] = dk[low:top].astype(BF16)
-            dv_ref[h, low:top, :] = dv[low:top].astype(BF16)
+        for low, entry_ref in ((0, state_ref), (rows, mid_ref)):
+            here = slice(low, low + rows)
+            grad = grad_ref[near, here, :]
+            raw = dot(grad, vh_ref[full, here, :], NT)
+            weights = (raw * jnp.exp(-rate * dist_ref[here, :])).astype(BF16)
+            dq = dot(weights, kh_ref[full, here, :], NN)
+            dq += factor[here] * dot(grad, entry_ref[full], NT)
+            dq_ref[h, here, :] = dq.astype(BF16)
+            dk_ref[h, here, :] = dot(weights, qh_ref[full, here, :], TN).astype(BF16)
+            dv_ref[h, here, :] = dot(probs_ref[h, here, :], grad, TN).astype(BF16)
         return carry
 
-    lax.fori_loop(0, heads, head, 0)
+    lax.fori_loop(0, heads, head, 0, unroll=2 if heads % 2 == 0 else 1)
 
 
 def turn_back_kernel(steps, *refs):
@@ -341,15 +368,18 @@
             out_ref[...] = jnp.swapaxes(jnp.concatenate(block, axis=0), 0, 1)
 
 
-def finish_kernel(base, groups, steps, info_ref, rate_ref, kh_ref, vh_ref, mine_ref, other_ref, *refs):
+def finish_kernel(base, groups, steps, info_ref, rate_ref, kh_ref, vh_ref, mine_ref, other_ref, half_ref, *refs):
     dk_parts, dv_parts = refs[: groups * steps], refs[groups * steps : 2 * groups * steps]
     dk_ref, dv_ref, state_ref = refs[-3:]
     heads = mine_ref.shape[0]
     count, tokens, dim = dk_parts[0].shape
     core = info_ref[INDEX] & 1
     row = column(tokens, dim)
+    side = tokens // 2
     distance = jnp.where(
-        row + info_ref[BASE] >= info_ref[NEXT_BEGIN], (tokens - row).astype(F32), F32(FAR)
+        row + info_ref[BASE] >= by_side(row, info_ref[MID_BEGIN], info_ref[NEXT_BEGIN]),
+        (by_side(row, side, tokens) - row).astype(F32),
+        F32(FAR),
     )
 
     def block(first, dk_parts, dv_parts):
@@ -360,8 +390,12 @@
             factor = jnp.exp(-rate_ref[full] * distance)
             dk = dk_parts[h // count][h % count].astype(F32)
             dv = dv_parts[h // count][h % count].astype(F32)
-            dk += factor * dot(vh_ref[full], state_ref[h], NT)
-            dv += factor * dot(kh_ref[full], state_ref[h], NN)
+            state = state_ref[h]
+            faded = spread(fade(rate_ref[full], info_ref[MID_BACK], TILE), state.astype(F32))
+            mid = (faded + half_ref[h]).astype(BF16)
+            v, k = vh_ref[full], kh_ref[full]
+            dk += factor * jnp.concatenate([dot(v[:side], mid, NT), dot(v[side:], state, NT)], axis=0)
+            dv += factor * jnp.concatenate([dot(k[:side], mid, NN), dot(k[side:], state, NN)], axis=0)
             dks.append(dk.astype(BF16))
             dvs.append(dv.astype(BF16))
         dk_ref[...] = jnp.swapaxes(jnp.stack(dks), 0, 1)
@@ -410,9 +444,7 @@
     for _ in range(hops):
         moving = send(moving, "ctx", lambda i: i + step)
         moved.append(moving)
-    own, send_part = combine(
-        partial(part_kernel, at, base, hops, first), [keep_part, came_part, *moved], [part] * 2
-    )
+    own, send_part = combine(partial(part_kernel, at, base, hops, first), [keep_part, came_part, *moved], [part] * 2)
     came = send(send_part, "ctx", lambda i: i ^ 2)
     mine, send_half = combine(
         partial(half_kernel, at, base, first),
@@ -478,7 +510,6 @@
     hops = hop_count(tokens)
     width = heads * dim * lax.axis_size("head")
     chunks = range(heads // span)
-    last = heads // span - 1
     shape = lambda *s: jax.ShapeDtypeStruct(s, F32)
     major = pltpu.VMEM((heads, tokens, dim), BF16)
     chunk = pltpu.VMEM((span, tokens, dim), BF16)
@@ -488,17 +519,15 @@
     unit = heads * tokens * dim
     rates, docs, gain = streamed(rates, docs, gain)
 
-    kh, vh, leave, keep = run(
+    kh, vh, leave, keep, early = run(
         state_kernel,
         [docs, rates, *streamed(keys, values)],
         [SMEM, SMEM, token_block, token_block],
-        [major, major] + [shape(heads, dim // 2, dim)] * 2,
-        [VMEM] * 4,
+        [major, major] + [shape(heads, dim // 2, dim)] * 2 + [pltpu.VMEM((heads, dim, dim), F32)],
+        [VMEM] * 5,
         steps=steps,
         cost=(2 * unit * dim, 8 * unit),
     )
-
-    halves = [x[c * span : (c + 1) * span] for c in chunks for x in (leave, keep)]
 
     spans = sum(len(rows) for rows in fade_rows(hops))
     info, rates = run(
@@ -513,7 +542,7 @@
         mask_kernel,
         [docs],
         [SMEM],
-        pltpu.VMEM((tokens, tokens), F32),
+        pltpu.VMEM((tokens, rows), F32),
         VMEM,
         scratch=[pltpu.VMEM((tokens, dim), jnp.int32)],
         cost=(0, 2 * tokens * tokens),
@@ -534,53 +563,43 @@
             partial(scores_kernel, g * count, rows),
             [rates, *kept(qh, kh, vh, distance)],
             [SMEM] + [VMEM] * 4,
-            [some, pltpu.VMEM((count, tokens, tokens), BF16)],
+            [some, pltpu.VMEM((count, tokens, rows), BF16)],
             [VMEM] * 2,
             cost=(4 * unit * tokens // total_groups, 0),
         )
         near.append(n), probs.append(p)
 
-    attn, states, stats = [], [], None
+    mine, other = entering_state(leave, keep, info, rates, 0, True, hops)
+    states = pltpu.VMEM((heads, dim, dim), BF16)
+    attn, states, mids, stats = run(
+        partial(attend_kernel, total_groups),
+        [info, rates, *kept(qh, gh), gain, mine, other, *kept(early, *near)],
+        [SMEM, SMEM] + [VMEM] * (6 + total_groups),
+        [major, states, states, shape(2, tokens)],
+        [VMEM] * 4,
+        cost=(2 * unit * dim, 0),
+    )
+    parts = head_sum_parts(stats)
+
+    grads, halves, late = [], [], []
     for c in chunks:
-        mine, other = entering_state(*halves[2 * c : 2 * c + 2], info, rates, c * span, True, hops)
-        begin, final = c == 0, c == last
-        args = [info, rates, *kept(qh, gh), gain, mine, other, *kept(*near[c * groups : (c + 1) * groups])]
-        if not begin:
-            args += kept(stats)
-        a, s, stats = run(
-            partial(attend_kernel, c * span, groups, begin, final),
-            args,
-            [SMEM, SMEM] + [VMEM] * (len(args) - 2),
-            [
-                chunk,
-                pltpu.VMEM((span, dim, dim), BF16),
-                shape(2, tokens) if final else pltpu.VMEM((2, tokens, dim), F32),
-            ],
-            [VMEM] * 3,
+        g, *pair, n = run(
+            partial(norm_kernel, c * span, width, len(parts)),
+            [info, rates, *parts, *kept(attn, gh, qh), gain],
+            [SMEM, SMEM] + [VMEM] * (len(parts) + 4),
+            [chunk, half, half, pltpu.VMEM((span, dim, dim), F32)],
+            [VMEM] * 4,
             cost=(2 * unit * dim // len(chunks), 0),
         )
-        attn.append(a), states.append(s)
-    parts = head_sum_parts(stats)
-
-    grads, halves = [], []
-    for c in chunks:
-        g, *pair = run(
-            partial(norm_kernel, c * span, width, len(parts)),
-            [info, rates, *parts, *kept(attn[c], gh, qh), gain],
-            [SMEM, SMEM] + [VMEM] * (len(parts) + 4),
-            [chunk, half, half],
-            [VMEM] * 3,
-            cost=(2 * unit * dim // len(chunks), 0),
-        )
-        grads.append(g), halves.extend(pair)
+        grads.append(g), halves.extend(pair), late.append(n)
 
     dqh, dk_part, dv_part = [], [], []
     for g in range(total_groups):
         c, at = divmod(g, groups)
         parts = run(
             partial(grads_kernel, c * span, at * count, rows),
-            [info, rates, *kept(grads[c], qh, kh, vh, probs[g], distance, states[c])],
-            [SMEM, SMEM] + [VMEM] * 7,
+            [info, rates, *kept(grads[c], qh, kh, vh, probs[g], distance, states, mids)],
+            [SMEM, SMEM] + [VMEM] * 8,
             [some] * 3,
             [VMEM] * 3,
             cost=(8 * unit * tokens // total_groups, 0),
@@ -598,18 +617,16 @@
         cost=(0, 2 * unit),
     )
 
-    entered = [
-        entering_state(*halves[2 * c : 2 * c + 2], info, rates, c * span, False, hops)
-        for c in chunks
-    ]
+    entered = [entering_state(*halves[2 * c : 2 * c + 2], info, rates, c * span, False, hops) for c in chunks]
     made = []
     if len(chunks) == 1:
         ((mine, other),) = entered
         half_block = pl.BlockSpec((wide, dim // 2, dim), lambda i: (i, 0, 0))
+        full_block = pl.BlockSpec((wide, dim, dim), lambda i: (i, 0, 0))
         made = run(
             partial(finish_kernel, None, total_groups // steps, steps),
-            [info, rates, *kept(kh, vh), mine, other, *kept(*dk_part, *dv_part)],
-            [SMEM, SMEM, VMEM, VMEM, half_block, half_block] + [VMEM] * (2 * total_groups),
+            [info, rates, *kept(kh, vh), mine, other, late[0], *kept(*dk_part, *dv_part)],
+            [SMEM, SMEM, VMEM, VMEM, half_block, half_block, full_block] + [VMEM] * (2 * total_groups),
             [full, full],
             [token_block, token_block],
             steps=steps,
@@ -620,8 +637,8 @@
     for c in chunks:
         mine, other = entered[c]
         here = slice(c * groups, (c + 1) * groups)
-        args = [info, rates, *kept(kh, vh), mine, other, *kept(*dk_part[here], *dv_part[here])]
-        specs = [SMEM, SMEM] + [VMEM] * (4 + 2 * groups)
+        args = [info, rates, *kept(kh, vh), mine, other, *kept(late[c], *dk_part[here], *dv_part[here])]
+        specs = [SMEM, SMEM] + [VMEM] * (5 + 2 * groups)
         alias = {len(args) + j: j for j in range(len(made))}
         block = pl.BlockSpec((tokens, wide, dim), lambda i, c=c: (0, c, 0))
         made = run(

time: 118 us -> 107 us (0.907)
  waiting for transfers between devices: 56.6 us -> 43.1 us
  starting transfers between devices: 15.5 us -> 21.4 us
  Pallas kernels: 43.2 us -> 39.9 us
    ppermute x13 -> x19, waiting for transfers between devices: 56.6 us -> 43.1 us  [send(): return lax.ppermute(block, axis, route)]
    ppermute x13 -> x19, starting transfers between devices: 15.5 us -> 21.4 us  [send(): return lax.ppermute(block, axis, route)]
    pallas_call x24 -> x30, Pallas kernels: 43.2 us -> 39.9 us  [run(): pl.pallas_call(kernel, out_shape=outs, grid=() if steps is None else (ste...]
  transfers between devices with their start and end apart: 13 -> 19, of which waited for: 11 -> 12; matrix products, arithmetic and copies ran while one was open for 0% -> 0% of each run, Pallas kernels for 25% -> 27%
where the time goes in v4:
time: 107 us; the launch traced here: 105 us
  waiting for transfers between devices  43.1 us (40%)
  Pallas kernels  39.9 us (37%)
  starting transfers between devices  21.4 us (20%)
    ppermute x19, waiting for transfers between devices, send(): return lax.ppermute(block, axis, route)  43.1 us
    pallas_call x30, Pallas kernels, run(): pl.pallas_call(kernel, out_shape=outs, grid=() if steps is None else (ste...  39.9 us
    ppermute x19, starting transfers between devices, send(): return lax.ppermute(block, axis, route)  21.4 us
  transfers between devices with their start and end apart: 19, of which 12 were waited for; matrix products, arithmetic and copies ran while one was open for 0% of the time, Pallas kernels for 27%

profile of v4, /device:TPU:12, one launch (start us, length us, event | category | flops | bytes accessed | tf_op | source)
XLA Modules:
  0.0 105.4 jit_solution(2802859813308227614)
XLA Ops:
  0.6 4.1 %shard_map.96 = (bf16[16,512,128]{2,1,0:T(8,128)(2,1)S(1)}, bf16[16,512,128]{2,1,0:T(8,128)(2,1)S(1)}, f32[16,64,128]{2,1,0:T(8,128)S(1)}, f32[16,64,128]{2,1,0:T(8,128)S(1)}, f32[16,128,128]{2,1,0:T(8,128)S(1)}) custom-call(s32[32]{0:T(128)} %docs_ref.5, f32[16]{0:T(128)} %rate_ref.1, bf16[512,16,128]{2,1,0:T(8,128)(2,1)} %k_ref.1, bf16[512,16,128]{2,1,0:T(8,128)(2,1)} %v_ref.1), custom_call_target="tpu_custom_call" | custom-call | flops 268435456 | bytes 8388608 | tf_op jit(solution)/shard_map/pallas_call | solution.py:489
  4.8 1.9 %shard_map.94 = (s32[25]{0:T(128)S(4)}, f32[16]{0:T(128)S(4)}) custom-call(s32[32]{0:T(128)} %docs_ref.5, f32[16]{0:T(128)} %rate_ref.1), custom_call_target="tpu_custom_call" | custom-call | tf_op jit(solution)/shard_map/pallas_call | solution.py:489
  7.5 8.2 %collective-permute-done.1.came_ref = f32[16,32,128]{2,1,0:T(8,128)S(1)} collective-permute-done((f32[16,32,128]{2,1,0:T(8,128)S(1)}, f32[16,32,128]{2,1,0:T(8,128)S(1)}, u32[]{:S(2)}, u32[]{:S(2)}) %collective-permute-start.1) | collective-permute-done | bytes 262176 | tf_op jit(solution)/shard_map/ppermute | solution.py:414
  15.7 3.5 %collective-permute-start.2 = (f32[16,32,128]{2,1,0:T(8,128)S(1)}, f32[16,32,128]{2,1,0:T(8,128)S(1)}, u32[]{:S(2)}, u32[]{:S(2)}) collective-permute-start(f32[16,32,128]{2,1,0:T(8,128)S(1)} %shard_map.98), channel_id=1, source_target_pairs={{0,4},{1,5},{2,6},{3,7},{4,8},{5,9},{6,10},{7,11},{8,12},{9,13},{1... | collective-permute-start | bytes 786440 | tf_op jit(solution)/shard_map/ppermute | solution.py:414
  19.2 6.3 %collective-permute-done.2.refs_0_ = f32[16,32,128]{2,1,0:T(8,128)S(1)} collective-permute-done((f32[16,32,128]{2,1,0:T(8,128)S(1)}, f32[16,32,128]{2,1,0:T(8,128)S(1)}, u32[]{:S(2)}, u32[]{:S(2)}) %collective-permute-start.2) | collective-permute-done | bytes 262176 | tf_op jit(solution)/shard_map/ppermute | solution.py:414
  25.5 3.5 %collective-permute-start.3 = (f32[16,32,128]{2,1,0:T(8,128)S(1)}, f32[16,32,128]{2,1,0:T(8,128)S(1)}, u32[]{:S(2)}, u32[]{:S(2)}) collective-permute-start(f32[16,32,128]{2,1,0:T(8,128)S(1)} %collective-permute-done.2.refs_0_), channel_id=1, source_target_pairs={{0,4},{1,5},{2,6},{3,7},{4,8},{5,9},{6,10},{7,11},{8,12},{9,13},{1... | collective-permute-start | bytes 786440 | tf_op jit(solution)/shard_map/ppermute | solution.py:414
  28.9 5.4 %collective-permute-done.3.refs_1_ = f32[16,32,128]{2,1,0:T(8,128)S(1)} collective-permute-done((f32[16,32,128]{2,1,0:T(8,128)S(1)}, f32[16,32,128]{2,1,0:T(8,128)S(1)}, u32[]{:S(2)}, u32[]{:S(2)}) %collective-permute-start.3) | collective-permute-done | bytes 262176 | tf_op jit(solution)/shard_map/ppermute | solution.py:414
  35.0 5.9 %collective-permute-done.4.came_part_ref = f32[16,32,128]{2,1,0:T(8,128)S(1)} collective-permute-done((f32[16,32,128]{2,1,0:T(8,128)S(1)}, f32[16,32,128]{2,1,0:T(8,128)S(1)}, u32[]{:S(2)}, u32[]{:S(2)}) %collective-permute-start.4) | collective-permute-done | bytes 262176 | tf_op jit(solution)/shard_map/ppermute | solution.py:414
  42.2 2.6 %shard_map.95 = (bf16[16,512,128]{2,1,0:T(8,128)(2,1)S(1)}, bf16[16,512,128]{2,1,0:T(8,128)(2,1)S(1)}) custom-call(bf16[512,16,128]{2,1,0:T(8,128)(2,1)} %q_ref.1, bf16[512,16,128]{2,1,0:T(8,128)(2,1)} %g_ref.1), custom_call_target="tpu_custom_call" | custom-call | bytes 8388608 | tf_op jit(solution)/shard_map/pallas_call | solution.py:489
  44.9 1.3 %shard_map.105 = (bf16[4,512,128]{2,1,0:T(8,128)(2,1)S(1)}, bf16[4,512,256]{2,1,0:T(8,128)(2,1)S(1)}) custom-call(f32[16]{0:T(128)S(4)} %get-tuple-element.67.rate_ref, bf16[16,512,128]{2,1,0:T(8,128)(2,1)S(1)} %get-tuple-element.68.qh_ref.refs_4_, bf16[16,512,128]{2,1,0:T(8,128)(2,1)S(1)} %get-tuple-element.79.kh_ref, ...), custom_call_target="tpu_custom_call" | custom-call | flops 536870912 | tf_op jit(solution)/shard_map/pallas_call | solution.py:489
  46.2 1.3 %shard_map.104 = (bf16[4,512,128]{2,1,0:T(8,128)(2,1)S(1)}, bf16[4,512,256]{2,1,0:T(8,128)(2,1)S(1)}) custom-call(f32[16]{0:T(128)S(4)} %get-tuple-element.67.rate_ref, bf16[16,512,128]{2,1,0:T(8,128)(2,1)S(1)} %get-tuple-element.68.qh_ref.refs_4_, bf16[16,512,128]{2,1,0:T(8,128)(2,1)S(1)} %get-tuple-element.79.kh_ref, ...), custom_call_target="tpu_custom_call" | custom-call | flops 536870912 | tf_op jit(solution)/shard_map/pallas_call | solution.py:489
  47.5 1.3 %shard_map.103 = (bf16[4,512,128]{2,1,0:T(8,128)(2,1)S(1)}, bf16[4,512,256]{2,1,0:T(8,128)(2,1)S(1)}) custom-call(f32[16]{0:T(128)S(4)} %get-tuple-element.67.rate_ref, bf16[16,512,128]{2,1,0:T(8,128)(2,1)S(1)} %get-tuple-element.68.qh_ref.refs_4_, bf16[16,512,128]{2,1,0:T(8,128)(2,1)S(1)} %get-tuple-element.79.kh_ref, ...), custom_call_target="tpu_custom_call" | custom-call | flops 536870912 | tf_op jit(solution)/shard_map/pallas_call | solution.py:489
  50.2 2.9 %shard_map.106 = (bf16[16,512,128]{2,1,0:T(8,128)(2,1)S(1)}, bf16[16,128,128]{2,1,0:T(8,128)(2,1)S(1)}, bf16[16,128,128]{2,1,0:T(8,128)(2,1)S(1)}, f32[2,512]{1,0:T(2,128)S(1)}) custom-call(s32[25]{0:T(128)S(4)} %get-tuple-element.66.info_ref, f32[16]{0:T(128)S(4)} %get-tuple-element.67.rate_ref, bf16[16,512,128]{2,1,0:T(8,128)(2,1)S(1)} %get-tuple-element.68.qh_ref.refs_4_, ...), custom_call_target="tpu_custom_call" | custom-call | flops 268435456 | tf_op jit(solution)/shard_map/pallas_call | solution.py:489
  53.1 1.6 %collective-permute-start.6 = (f32[2,512]{1,0:T(2,128)S(1)}, f32[2,512]{1,0:T(2,128)S(1)}, u32[]{:S(2)}, u32[]{:S(2)}) collective-permute-start(f32[2,512]{1,0:T(2,128)S(1)} %get-tuple-element.85.refs_0_), channel_id=1, source_target_pairs={{0,16},{16,0},{1,17},{17,1},{2,18},{18,2},{3,19},{19,3},{4,20},{20... | collective-permute-start | bytes 12296 | tf_op jit(solution)/shard_map/ppermute | solution.py:414
  54.6 2.1 %collective-permute-done.6.refs_1_ = f32[2,512]{1,0:T(2,128)S(1)} collective-permute-done((f32[2,512]{1,0:T(2,128)S(1)}, f32[2,512]{1,0:T(2,128)S(1)}, u32[]{:S(2)}, u32[]{:S(2)}) %collective-permute-start.6) | collective-permute-done | bytes 4128 | tf_op jit(solution)/shard_map/ppermute | solution.py:414
  56.8 1.9 %shard_map.110 = (bf16[8,512,128]{2,1,0:T(8,128)(2,1)S(1)}, f32[8,64,128]{2,1,0:T(8,128)S(1)}, f32[8,64,128]{2,1,0:T(8,128)S(1)}, f32[8,128,128]{2,1,0:T(8,128)S(1)}) custom-call(s32[25]{0:T(128)S(4)} %get-tuple-element.66.info_ref, f32[16]{0:T(128)S(4)} %get-tuple-element.67.rate_ref, f32[2,512]{1,0:T(2,128)S(1)} %get-tuple-element.85.refs_0_, ...), custom_call_target="tpu_custom_call" | custom-call | flops 134217728 | tf_op jit(solution)/shard_map/pallas_call | solution.py:489
  58.7 1.9 %shard_map.107 = (bf16[8,512,128]{2,1,0:T(8,128)(2,1)S(1)}, f32[8,64,128]{2,1,0:T(8,128)S(1)}, f32[8,64,128]{2,1,0:T(8,128)S(1)}, f32[8,128,128]{2,1,0:T(8,128)S(1)}) custom-call(s32[25]{0:T(128)S(4)} %get-tuple-element.66.info_ref, f32[16]{0:T(128)S(4)} %get-tuple-element.67.rate_ref, f32[2,512]{1,0:T(2,128)S(1)} %get-tuple-element.85.refs_0_, ...), custom_call_target="tpu_custom_call" | custom-call | flops 134217728 | tf_op jit(solution)/shard_map/pallas_call | solution.py:489
  63.5 4.2 %collective-permute-done.8.came_ref = f32[8,32,128]{2,1,0:T(8,128)S(1)} collective-permute-done((f32[8,32,128]{2,1,0:T(8,128)S(1)}, f32[8,32,128]{2,1,0:T(8,128)S(1)}, u32[]{:S(2)}, u32[]{:S(2)}) %collective-permute-start.8) | collective-permute-done | bytes 131104 | tf_op jit(solution)/shard_map/ppermute | solution.py:414
  67.7 1.9 %collective-permute-start.9 = (f32[8,32,128]{2,1,0:T(8,128)S(1)}, f32[8,32,128]{2,1,0:T(8,128)S(1)}, u32[]{:S(2)}, u32[]{:S(2)}) collective-permute-start(f32[8,32,128]{2,1,0:T(8,128)S(1)} %shard_map.115), channel_id=1, source_target_pairs={{4,0},{5,1},{6,2},{7,3},{8,4},{9,5},{10,6},{11,7},{12,8},{13,9},{1... | collective-permute-start | bytes 393224 | tf_op jit(solution)/shard_map/ppermute | solution.py:414
  69.7 1.9 %collective-permute-start.15 = (f32[8,32,128]{2,1,0:T(8,128)S(1)}, f32[8,32,128]{2,1,0:T(8,128)S(1)}, u32[]{:S(2)}, u32[]{:S(2)}) collective-permute-start(f32[8,32,128]{2,1,0:T(8,128)S(1)} %shard_map.119), channel_id=1, source_target_pairs={{4,0},{5,1},{6,2},{7,3},{8,4},{9,5},{10,6},{11,7},{12,8},{13,9},{1... | collective-permute-start | bytes 393224 | tf_op jit(solution)/shard_map/ppermute | solution.py:414
  71.6 4.3 %collective-permute-done.9.refs_0_ = f32[8,32,128]{2,1,0:T(8,128)S(1)} collective-permute-done((f32[8,32,128]{2,1,0:T(8,128)S(1)}, f32[8,32,128]{2,1,0:T(8,128)S(1)}, u32[]{:S(2)}, u32[]{:S(2)}) %collective-permute-start.9) | collective-permute-done | bytes 131104 | tf_op jit(solution)/shard_map/ppermute | solution.py:414
  75.9 1.9 %collective-permute-start.10 = (f32[8,32,128]{2,1,0:T(8,128)S(1)}, f32[8,32,128]{2,1,0:T(8,128)S(1)}, u32[]{:S(2)}, u32[]{:S(2)}) collective-permute-start(f32[8,32,128]{2,1,0:T(8,128)S(1)} %collective-permute-done.9.refs_0_), channel_id=1, source_target_pairs={{4,0},{5,1},{6,2},{7,3},{8,4},{9,5},{10,6},{11,7},{12,8},{13,9},{1... | collective-permute-start | bytes 393224 | tf_op jit(solution)/shard_map/ppermute | solution.py:414
  78.6 2.1 %collective-permute-start.16 = (f32[8,32,128]{2,1,0:T(8,128)S(1)}, f32[8,32,128]{2,1,0:T(8,128)S(1)}, u32[]{:S(2)}, u32[]{:S(2)}) collective-permute-start(f32[8,32,128]{2,1,0:T(8,128)S(1)} %collective-permute-done.15.refs_0_), channel_id=1, source_target_pairs={{4,0},{5,1},{6,2},{7,3},{8,4},{9,5},{10,6},{11,7},{12,8},{13,9},{1... | collective-permute-start | bytes 393224 | tf_op jit(solution)/shard_map/ppermute | solution.py:414
  80.7 2.7 %collective-permute-done.10.refs_1_ = f32[8,32,128]{2,1,0:T(8,128)S(1)} collective-permute-done((f32[8,32,128]{2,1,0:T(8,128)S(1)}, f32[8,32,128]{2,1,0:T(8,128)S(1)}, u32[]{:S(2)}, u32[]{:S(2)}) %collective-permute-start.10) | collective-permute-done | bytes 131104 | tf_op jit(solution)/shard_map/ppermute | solution.py:414
  86.2 2.7 %shard_map.112 = (bf16[4,512,128]{2,1,0:T(8,128)(2,1)S(1)}, bf16[4,512,128]{2,1,0:T(8,128)(2,1)S(1)}, bf16[4,512,128]{2,1,0:T(8,128)(2,1)S(1)}) custom-call(s32[25]{0:T(128)S(4)} %get-tuple-element.66.info_ref, f32[16]{0:T(128)S(4)} %get-tuple-element.67.rate_ref, bf16[8,512,128]{2,1,0:T(8,128)(2,1)S(1)} %get-tuple-element.94.grad_ref, ...), custom_call_target="tpu_custom_call" | custom-call | flops 1073741824 | tf_op jit(solution)/shard_map/pallas_call | solution.py:489
  89.1 1.5 %collective-permute-done.17.came_part_ref = f32[8,32,128]{2,1,0:T(8,128)S(1)} collective-permute-done((f32[8,32,128]{2,1,0:T(8,128)S(1)}, f32[8,32,128]{2,1,0:T(8,128)S(1)}, u32[]{:S(2)}, u32[]{:S(2)}) %collective-permute-start.17) | collective-permute-done | bytes 131104 | tf_op jit(solution)/shard_map/ppermute | solution.py:414
  90.7 2.7 %shard_map.111 = (bf16[4,512,128]{2,1,0:T(8,128)(2,1)S(1)}, bf16[4,512,128]{2,1,0:T(8,128)(2,1)S(1)}, bf16[4,512,128]{2,1,0:T(8,128)(2,1)S(1)}) custom-call(s32[25]{0:T(128)S(4)} %get-tuple-element.66.info_ref, f32[16]{0:T(128)S(4)} %get-tuple-element.67.rate_ref, bf16[8,512,128]{2,1,0:T(8,128)(2,1)S(1)} %get-tuple-element.94.grad_ref, ...), custom_call_target="tpu_custom_call" | custom-call | flops 1073741824 | tf_op jit(solution)/shard_map/pallas_call | solution.py:489
  93.5 2.7 %shard_map.109 = (bf16[4,512,128]{2,1,0:T(8,128)(2,1)S(1)}, bf16[4,512,128]{2,1,0:T(8,128)(2,1)S(1)}, bf16[4,512,128]{2,1,0:T(8,128)(2,1)S(1)}) custom-call(s32[25]{0:T(128)S(4)} %get-tuple-element.66.info_ref, f32[16]{0:T(128)S(4)} %get-tuple-element.67.rate_ref, bf16[8,512,128]{2,1,0:T(8,128)(2,1)S(1)} %get-tuple-element.87.grad_ref, ...), custom_call_target="tpu_custom_call" | custom-call | flops 1073741824 | tf_op jit(solution)/shard_map/pallas_call | solution.py:489
  96.2 2.7 %shard_map.108 = (bf16[4,512,128]{2,1,0:T(8,128)(2,1)S(1)}, bf16[4,512,128]{2,1,0:T(8,128)(2,1)S(1)}, bf16[4,512,128]{2,1,0:T(8,128)(2,1)S(1)}) custom-call(s32[25]{0:T(128)S(4)} %get-tuple-element.66.info_ref, f32[16]{0:T(128)S(4)} %get-tuple-element.67.rate_ref, bf16[8,512,128]{2,1,0:T(8,128)(2,1)S(1)} %get-tuple-element.87.grad_ref, ...), custom_call_target="tpu_custom_call" | custom-call | flops 1073741824 | tf_op jit(solution)/shard_map/pallas_call | solution.py:489
  99.0 1.5 %shard_map.113 = bf16[512,16,128]{2,1,0:T(8,128)(2,1)} custom-call(bf16[4,512,128]{2,1,0:T(8,128)(2,1)S(1)} %get-tuple-element.91.refs_0_, bf16[4,512,128]{2,1,0:T(8,128)(2,1)S(1)} %get-tuple-element.93.refs_1_, bf16[4,512,128]{2,1,0:T(8,128)(2,1)S(1)} %get-tuple-element.96.refs_2_, bf16[4,512,128]{2,1,0:T(8,128)(2,1)S(1)} %get-tuple-element.98.refs_3_), custom_call_target="tpu_custom_call" | custom-call | bytes 2097152 | tf_op jit(solution)/shard_map/pallas_call | solution.py:489
  100.5 2.4 %shard_map.122 = (bf16[512,16,128]{2,1,0:T(8,128)(2,1)}, bf16[512,16,128]{2,1,0:T(8,128)(2,1)}) custom-call(s32[25]{0:T(128)S(4)} %get-tuple-element.66.info_ref, f32[16]{0:T(128)S(4)} %get-tuple-element.67.rate_ref, bf16[16,512,128]{2,1,0:T(8,128)(2,1)S(1)} %get-tuple-element.79.kh_ref, bf16[16,512,128]{2,1,0:T(8,128)(2,1)S(1)} %get-tuple-element.80.vh_ref, ...), custom_call_target="tpu_custom_call" | custom-call | flops 268435456 | bytes 2097152 | tf_op jit(solution)/shard_map/pallas_call | solution.py:489
  102.9 2.5 %shard_map.123 = (bf16[512,16,128]{2,1,0:T(8,128)(2,1)}, bf16[512,16,128]{2,1,0:T(8,128)(2,1)}) custom-call(s32[25]{0:T(128)S(4)} %get-tuple-element.66.info_ref, f32[16]{0:T(128)S(4)} %get-tuple-element.67.rate_ref, bf16[16,512,128]{2,1,0:T(8,128)(2,1)S(1)} %get-tuple-element.79.kh_ref, ...), custom_call_target="tpu_custom_call", output_to_operand_aliasing={{0}: (11, {}), {1}: (12, {})} | custom-call | flops 268435456 | bytes 2097152 | tf_op jit(solution)/shard_map/pallas_call | solution.py:489
  (36 shorter events, 11.0 us)
Async XLA Ops:
  4.8 2.0 %collective-permute-start = (f32[16,64,128]{2,1,0:T(8,128)S(1)}, f32[16,64,128]{2,1,0:T(8,128)S(1)}, u32[]{:S(2)}, u32[]{:S(2)}) collective-permute-start(f32[16,64,128]{2,1,0:T(8,128)S(1)} %get-tuple-element.71), channel_id=1, source_target_pairs={{0,1},{1,0},{2,3},{3,2},{4,5},{5,4},{6,7},{7,6},{8,9},{9,8},{10,11... | collective-permute-start | bytes 1572872 | tf_op jit(solution)/shard_map/ppermute | solution.py:414
  6.9 8.8 %collective-permute-start.1 = (f32[16,32,128]{2,1,0:T(8,128)S(1)}, f32[16,32,128]{2,1,0:T(8,128)S(1)}, u32[]{:S(2)}, u32[]{:S(2)}) collective-permute-start(f32[16,32,128]{2,1,0:T(8,128)S(1)} %get-tuple-element.73), channel_id=1, source_target_pairs={{0,2},{1,3},{2,0},{3,1},{4,6},{5,7},{6,4},{7,5},{8,10},{9,11},{10,... | collective-permute-start | bytes 786440 | tf_op jit(solution)/shard_map/ppermute | solution.py:414
  15.7 9.7 %collective-permute-start.2 = (f32[16,32,128]{2,1,0:T(8,128)S(1)}, f32[16,32,128]{2,1,0:T(8,128)S(1)}, u32[]{:S(2)}, u32[]{:S(2)}) collective-permute-start(f32[16,32,128]{2,1,0:T(8,128)S(1)} %shard_map.98), channel_id=1, source_target_pairs={{0,4},{1,5},{2,6},{3,7},{4,8},{5,9},{6,10},{7,11},{8,12},{9,13},{1... | collective-permute-start | bytes 786440 | tf_op jit(solution)/shard_map/ppermute | solution.py:414
  25.5 8.9 %collective-permute-start.3 = (f32[16,32,128]{2,1,0:T(8,128)S(1)}, f32[16,32,128]{2,1,0:T(8,128)S(1)}, u32[]{:S(2)}, u32[]{:S(2)}) collective-permute-start(f32[16,32,128]{2,1,0:T(8,128)S(1)} %collective-permute-done.2.refs_0_), channel_id=1, source_target_pairs={{0,4},{1,5},{2,6},{3,7},{4,8},{5,9},{6,10},{7,11},{8,12},{9,13},{1... | collective-permute-start | bytes 786440 | tf_op jit(solution)/shard_map/ppermute | solution.py:414
  34.4 6.4 %collective-permute-start.4 = (f32[16,32,128]{2,1,0:T(8,128)S(1)}, f32[16,32,128]{2,1,0:T(8,128)S(1)}, u32[]{:S(2)}, u32[]{:S(2)}) collective-permute-start(f32[16,32,128]{2,1,0:T(8,128)S(1)} %get-tuple-element.75), channel_id=1, source_target_pairs={{0,2},{1,3},{2,0},{3,1},{4,6},{5,7},{6,4},{7,5},{8,10},{9,11},{10,... | collective-permute-start | bytes 786440 | tf_op jit(solution)/shard_map/ppermute | solution.py:414
  41.0 9.2 %collective-permute-start.5 = (f32[16,64,128]{2,1,0:T(8,128)S(1)}, f32[16,64,128]{2,1,0:T(8,128)S(1)}, u32[]{:S(2)}, u32[]{:S(2)}) collective-permute-start(f32[16,64,128]{2,1,0:T(8,128)S(1)} %get-tuple-element.77), channel_id=1, source_target_pairs={{0,1},{1,0},{2,3},{3,2},{4,5},{5,4},{6,7},{7,6},{8,9},{9,8},{10,11... | collective-permute-start | bytes 1572872 | tf_op jit(solution)/shard_map/ppermute | solution.py:414
  53.1 3.7 %collective-permute-start.6 = (f32[2,512]{1,0:T(2,128)S(1)}, f32[2,512]{1,0:T(2,128)S(1)}, u32[]{:S(2)}, u32[]{:S(2)}) collective-permute-start(f32[2,512]{1,0:T(2,128)S(1)} %get-tuple-element.85.refs_0_), channel_id=1, source_target_pairs={{0,16},{16,0},{1,17},{17,1},{2,18},{18,2},{3,19},{19,3},{4,20},{20... | collective-permute-start | bytes 12296 | tf_op jit(solution)/shard_map/ppermute | solution.py:414
  58.6 2.5 %collective-permute-start.7 = (f32[8,64,128]{2,1,0:T(8,128)S(1)}, f32[8,64,128]{2,1,0:T(8,128)S(1)}, u32[]{:S(2)}, u32[]{:S(2)}) collective-permute-start(f32[8,64,128]{2,1,0:T(8,128)S(1)} %get-tuple-element.100), channel_id=1, source_target_pairs={{0,1},{1,0},{2,3},{3,2},{4,5},{5,4},{6,7},{7,6},{8,9},{9,8},{10,11... | collective-permute-start | bytes 786440 | tf_op jit(solution)/shard_map/ppermute | solution.py:414
  60.6 1.7 %collective-permute-start.13 = (f32[8,64,128]{2,1,0:T(8,128)S(1)}, f32[8,64,128]{2,1,0:T(8,128)S(1)}, u32[]{:S(2)}, u32[]{:S(2)}) collective-permute-start(f32[8,64,128]{2,1,0:T(8,128)S(1)} %get-tuple-element.113), channel_id=1, source_target_pairs={{0,1},{1,0},{2,3},{3,2},{4,5},{5,4},{6,7},{7,6},{8,9},{9,8},{10,11... | collective-permute-start | bytes 786440 | tf_op jit(solution)/shard_map/ppermute | solution.py:414
  61.2 6.4 %collective-permute-start.8 = (f32[8,32,128]{2,1,0:T(8,128)S(1)}, f32[8,32,128]{2,1,0:T(8,128)S(1)}, u32[]{:S(2)}, u32[]{:S(2)}) collective-permute-start(f32[8,32,128]{2,1,0:T(8,128)S(1)} %get-tuple-element.102), channel_id=1, source_target_pairs={{0,2},{1,3},{2,0},{3,1},{4,6},{5,7},{6,4},{7,5},{8,10},{9,11},{10,... | collective-permute-start | bytes 393224 | tf_op jit(solution)/shard_map/ppermute | solution.py:414
  62.4 7.2 %collective-permute-start.14 = (f32[8,32,128]{2,1,0:T(8,128)S(1)}, f32[8,32,128]{2,1,0:T(8,128)S(1)}, u32[]{:S(2)}, u32[]{:S(2)}) collective-permute-start(f32[8,32,128]{2,1,0:T(8,128)S(1)} %get-tuple-element.115), channel_id=1, source_target_pairs={{0,2},{1,3},{2,0},{3,1},{4,6},{5,7},{6,4},{7,5},{8,10},{9,11},{10,... | collective-permute-start | bytes 393224 | tf_op jit(solution)/shard_map/ppermute | solution.py:414
  67.7 8.2 %collective-permute-start.9 = (f32[8,32,128]{2,1,0:T(8,128)S(1)}, f32[8,32,128]{2,1,0:T(8,128)S(1)}, u32[]{:S(2)}, u32[]{:S(2)}) collective-permute-start(f32[8,32,128]{2,1,0:T(8,128)S(1)} %shard_map.115), channel_id=1, source_target_pairs={{4,0},{5,1},{6,2},{7,3},{8,4},{9,5},{10,6},{11,7},{12,8},{13,9},{1... | collective-permute-start | bytes 393224 | tf_op jit(solution)/shard_map/ppermute | solution.py:414
  69.7 8.9 %collective-permute-start.15 = (f32[8,32,128]{2,1,0:T(8,128)S(1)}, f32[8,32,128]{2,1,0:T(8,128)S(1)}, u32[]{:S(2)}, u32[]{:S(2)}) collective-permute-start(f32[8,32,128]{2,1,0:T(8,128)S(1)} %shard_map.119), channel_id=1, source_target_pairs={{4,0},{5,1},{6,2},{7,3},{8,4},{9,5},{10,6},{11,7},{12,8},{13,9},{1... | collective-permute-start | bytes 393224 | tf_op jit(solution)/shard_map/ppermute | solution.py:414
  75.9 7.5 %collective-permute-start.10 = (f32[8,32,128]{2,1,0:T(8,128)S(1)}, f32[8,32,128]{2,1,0:T(8,128)S(1)}, u32[]{:S(2)}, u32[]{:S(2)}) collective-permute-start(f32[8,32,128]{2,1,0:T(8,128)S(1)} %collective-permute-done.9.refs_0_), channel_id=1, source_target_pairs={{4,0},{5,1},{6,2},{7,3},{8,4},{9,5},{10,6},{11,7},{12,8},{13,9},{1... | collective-permute-start | bytes 393224 | tf_op jit(solution)/shard_map/ppermute | solution.py:414
  78.6 6.8 %collective-permute-start.16 = (f32[8,32,128]{2,1,0:T(8,128)S(1)}, f32[8,32,128]{2,1,0:T(8,128)S(1)}, u32[]{:S(2)}, u32[]{:S(2)}) collective-permute-start(f32[8,32,128]{2,1,0:T(8,128)S(1)} %collective-permute-done.15.refs_0_), channel_id=1, source_target_pairs={{4,0},{5,1},{6,2},{7,3},{8,4},{9,5},{10,6},{11,7},{12,8},{13,9},{1... | collective-permute-start | bytes 393224 | tf_op jit(solution)/shard_map/ppermute | solution.py:414
  83.5 5.4 %collective-permute-start.11 = (f32[8,32,128]{2,1,0:T(8,128)S(1)}, f32[8,32,128]{2,1,0:T(8,128)S(1)}, u32[]{:S(2)}, u32[]{:S(2)}) collective-permute-start(f32[8,32,128]{2,1,0:T(8,128)S(1)} %get-tuple-element.104), channel_id=1, source_target_pairs={{0,2},{1,3},{2,0},{3,1},{4,6},{5,7},{6,4},{7,5},{8,10},{9,11},{10,... | collective-permute-start | bytes 393224 | tf_op jit(solution)/shard_map/ppermute | solution.py:414
  85.5 5.0 %collective-permute-start.17 = (f32[8,32,128]{2,1,0:T(8,128)S(1)}, f32[8,32,128]{2,1,0:T(8,128)S(1)}, u32[]{:S(2)}, u32[]{:S(2)}) collective-permute-start(f32[8,32,128]{2,1,0:T(8,128)S(1)} %get-tuple-element.117), channel_id=1, source_target_pairs={{0,2},{1,3},{2,0},{3,1},{4,6},{5,7},{6,4},{7,5},{8,10},{9,11},{10,... | collective-permute-start | bytes 393224 | tf_op jit(solution)/shard_map/ppermute | solution.py:414
  89.0 13.9 %collective-permute-start.12 = (f32[8,64,128]{2,1,0:T(8,128)S(1)}, f32[8,64,128]{2,1,0:T(8,128)S(1)}, u32[]{:S(2)}, u32[]{:S(2)}) collective-permute-start(f32[8,64,128]{2,1,0:T(8,128)S(1)} %get-tuple-element.106), channel_id=1, source_target_pairs={{0,1},{1,0},{2,3},{3,2},{4,5},{5,4},{6,7},{7,6},{8,9},{9,8},{10,11... | collective-permute-start | bytes 786440 | tf_op jit(solution)/shard_map/ppermute | solution.py:414
  90.7 9.8 %collective-permute-start.18 = (f32[8,64,128]{2,1,0:T(8,128)S(1)}, f32[8,64,128]{2,1,0:T(8,128)S(1)}, u32[]{:S(2)}, u32[]{:S(2)}) collective-permute-start(f32[8,64,128]{2,1,0:T(8,128)S(1)} %get-tuple-element.119), channel_id=1, source_target_pairs={{0,1},{1,0},{2,3},{3,2},{4,5},{5,4},{6,7},{7,6},{8,9},{9,8},{10,11... | collective-permute-start | bytes 786440 | tf_op jit(solution)/shard_map/ppermute | solution.py:414

commit v5 on v4

--- a/solution.py
+++ b/solution.py
@@ -12,7 +12,6 @@
 LONGEST = 4096
 FAR = 1e30
 APART = 1 << 30
-CHUNKS = 2
 F32 = jnp.float32
 BF16 = jnp.bfloat16
 
@@ -272,13 +271,20 @@
     )
 
 
-def attend_kernel(groups, info_ref, rate_ref, qh_ref, gh_ref, gain_ref, mine_ref, other_ref, half_ref, *refs):
+def reach_kernel(info_ref, rate_ref, qh_ref, gh_ref, gain_ref, far_ref, gained_ref):
+    heads, tokens, dim = qh_ref.shape
+    distance = entry_distance(info_ref, column(tokens, dim))
+    for h in range(heads):
+        far_ref[h] = (qh_ref[h].astype(F32) * jnp.exp(-rate_ref[h] * distance)).astype(BF16)
+        gained_ref[h] = gain_ref[h : h + 1, :] * gh_ref[h].astype(F32)
+
+
+def attend_kernel(groups, info_ref, rate_ref, far_ref, gained_ref, mine_ref, other_ref, half_ref, *refs):
     local_refs, (attn_ref, state_ref, mid_ref, stats_ref) = refs[:groups], refs[groups:]
     heads, tokens, dim = attn_ref.shape
     side = tokens // 2
     count = heads // groups
     core = info_ref[INDEX] & 1
-    distance = entry_distance(info_ref, column(tokens, dim))
     squares = jnp.zeros((tokens, dim), F32)
     cross = jnp.zeros((tokens, dim), F32)
     for h in range(heads):
@@ -288,20 +294,33 @@
         mid = (spread(fade(rate, info_ref[MID_AHEAD], TILE), state.astype(F32)) + half_ref[h]).astype(BF16)
         mid_ref[h] = mid
         far = jnp.concatenate(
-            [dot(qh_ref[h, :side, :], state, NN), dot(qh_ref[h, side:, :], mid, NN)], axis=0
+            [dot(far_ref[h, :side, :], state, NN), dot(far_ref[h, side:, :], mid, NN)], axis=0
         )
         near = local_refs[h // count][h % count].astype(F32)
-        attn = near + jnp.exp(-rate * distance) * far
+        attn = near + far
         attn_ref[h] = attn.astype(BF16)
         squares += attn * attn
-        cross += gain_ref[h : h + 1, :] * gh_ref[h].astype(F32) * attn
+        cross += gained_ref[h] * attn
     stats_ref[0:1, :] = jnp.sum(jnp.swapaxes(squares, 0, 1), axis=0, keepdims=True)
     stats_ref[1:2, :] = jnp.sum(jnp.swapaxes(cross, 0, 1), axis=0, keepdims=True)
 
 
+def lead_kernel(info_ref, rate_ref, qh_ref, faded_ref):
+    heads, tokens, dim = qh_ref.shape
+    row = column(tokens, dim)
+    side = tokens // 2
+    distance = jnp.where(
+        row + info_ref[BASE] < by_side(row, info_ref[LATER_START], info_ref[MID_LATER]),
+        (row - by_side(row, 0, side)).astype(F32),
+        F32(FAR),
+    )
+    for h in range(heads):
+        faded_ref[h] = (qh_ref[h].astype(F32) * jnp.exp(-rate_ref[h] * distance)).astype(BF16)
+
+
 def norm_kernel(base, width, parts, info_ref, rate_ref, *refs):
     stats_refs, refs = refs[:parts], refs[parts:]
-    attn_ref, gh_ref, qh_ref, gain_ref, grad_ref, send_ref, keep_ref, half_ref = refs
+    attn_ref, gained_ref, faded_ref, grad_ref, send_ref, keep_ref, half_ref = refs
     heads, tokens, dim = grad_ref.shape
     core = info_ref[INDEX] & 1
     stats = stats_refs[0][...]
@@ -312,20 +331,12 @@
     scale = cross * inverse * inverse * inverse / width
     inverse = jnp.swapaxes(jnp.broadcast_to(inverse, (dim, tokens)), 0, 1)
     scale = jnp.swapaxes(jnp.broadcast_to(scale, (dim, tokens)), 0, 1)
-    row = column(tokens, dim)
     side = tokens // 2
-    distance = jnp.where(
-        row + info_ref[BASE] < by_side(row, info_ref[LATER_START], info_ref[MID_LATER]),
-        (row - by_side(row, 0, side)).astype(F32),
-        F32(FAR),
-    )
     for h in range(heads):
         full = base + h
-        gained = gain_ref[full : full + 1, :] * gh_ref[full].astype(F32)
-        grad = (gained * inverse - attn_ref[full].astype(F32) * scale).astype(BF16)
+        grad = (gained_ref[full] * inverse - attn_ref[full].astype(F32) * scale).astype(BF16)
         grad_ref[h] = grad
-        lead = jnp.exp(-rate_ref[full] * distance)
-        faded = (qh_ref[full].astype(F32) * lead).astype(BF16)
+        faded = faded_ref[full]
         near = dot(faded[side:], grad[side:], TN)
         half_ref[h] = near
         state = dot(faded[:side], grad[:side], TN)
@@ -368,44 +379,50 @@
             out_ref[...] = jnp.swapaxes(jnp.concatenate(block, axis=0), 0, 1)
 
 
-def finish_kernel(base, groups, steps, info_ref, rate_ref, kh_ref, vh_ref, mine_ref, other_ref, half_ref, *refs):
-    dk_parts, dv_parts = refs[: groups * steps], refs[groups * steps : 2 * groups * steps]
+def return_kernel(info_ref, rate_ref, kh_ref, vh_ref, far_k_ref, far_v_ref):
+    heads, tokens, dim = kh_ref.shape
+    row = column(tokens, dim)
+    distance = jnp.where(
+        row + info_ref[BASE] >= by_side(row, info_ref[MID_BEGIN], info_ref[NEXT_BEGIN]),
+        (by_side(row, tokens // 2, tokens) - row).astype(F32),
+        F32(FAR),
+    )
+    for h in range(heads):
+        factor = jnp.exp(-rate_ref[h] * distance)
+        far_k_ref[h] = (kh_ref[h].astype(F32) * factor).astype(BF16)
+        far_v_ref[h] = (vh_ref[h].astype(F32) * factor).astype(BF16)
+
+
+def finish_kernel(base, groups, info_ref, rate_ref, far_k_ref, far_v_ref, mine_ref, other_ref, half_ref, *refs):
+    dk_parts, dv_parts = refs[:groups], refs[groups : 2 * groups]
     dk_ref, dv_ref, state_ref = refs[-3:]
     heads = mine_ref.shape[0]
-    count, tokens, dim = dk_parts[0].shape
+    count, tokens, _ = dk_parts[0].shape
+    side = tokens // 2
     core = info_ref[INDEX] & 1
-    row = column(tokens, dim)
-    side = tokens // 2
-    distance = jnp.where(
-        row + info_ref[BASE] >= by_side(row, info_ref[MID_BEGIN], info_ref[NEXT_BEGIN]),
-        (by_side(row, side, tokens) - row).astype(F32),
-        F32(FAR),
-    )
-
-    def block(first, dk_parts, dv_parts):
+
+    def block(low):
+        here = slice(low, low + side)
         dks, dvs = [], []
         for h in range(heads):
-            full = first + h
-            put_halves(core, state_ref, h, mine_ref[h], other_ref[h])
-            factor = jnp.exp(-rate_ref[full] * distance)
-            dk = dk_parts[h // count][h % count].astype(F32)
-            dv = dv_parts[h // count][h % count].astype(F32)
+            full = base + h
+            if low == 0:
+                put_halves(core, state_ref, h, mine_ref[h], other_ref[h])
             state = state_ref[h]
-            faded = spread(fade(rate_ref[full], info_ref[MID_BACK], TILE), state.astype(F32))
-            mid = (faded + half_ref[h]).astype(BF16)
-            v, k = vh_ref[full], kh_ref[full]
-            dk += factor * jnp.concatenate([dot(v[:side], mid, NT), dot(v[side:], state, NT)], axis=0)
-            dv += factor * jnp.concatenate([dot(k[:side], mid, NN), dot(k[side:], state, NN)], axis=0)
+            if low == 0:
+                faded = spread(fade(rate_ref[full], info_ref[MID_BACK], TILE), state.astype(F32))
+                state = (faded + half_ref[h]).astype(BF16)
+            dk = dk_parts[h // count][h % count, here, :].astype(F32)
+            dv = dv_parts[h // count][h % count, here, :].astype(F32)
+            dk += dot(far_v_ref[full, here, :], state, NT)
+            dv += dot(far_k_ref[full, here, :], state, NN)
             dks.append(dk.astype(BF16))
             dvs.append(dv.astype(BF16))
         dk_ref[...] = jnp.swapaxes(jnp.stack(dks), 0, 1)
         dv_ref[...] = jnp.swapaxes(jnp.stack(dvs), 0, 1)
 
-    if base is not None:
-        return block(base, dk_parts, dv_parts)
-    for s in range(steps):
-        here = slice(s * groups, (s + 1) * groups)
-        pl.when(pl.program_id(0) == s)(partial(block, s * heads, dk_parts[here], dv_parts[here]))
+    for s in range(2):
+        pl.when(pl.program_id(0) == s)(partial(block, s * side))
 
 
 def send(block, axis, target):
@@ -444,7 +461,9 @@
     for _ in range(hops):
         moving = send(moving, "ctx", lambda i: i + step)
         moved.append(moving)
-    own, send_part = combine(partial(part_kernel, at, base, hops, first), [keep_part, came_part, *moved], [part] * 2)
+    own, send_part = combine(
+        partial(part_kernel, at, base, hops, first), [keep_part, came_part, *moved], [part] * 2
+    )
     came = send(send_part, "ctx", lambda i: i ^ 2)
     mine, send_half = combine(
         partial(half_kernel, at, base, first),
@@ -502,8 +521,8 @@
 def body(queries, keys, values, out_grad, gain, rates, docs):
     tokens, heads, dim = queries.shape
     wide = 8 if heads % 8 == 0 else heads
-    count = 4 if wide % 4 == 0 else wide
-    span = heads // (CHUNKS if heads % (CHUNKS * count) == 0 else 1)
+    count = 2 if wide % 2 == 0 else wide
+    span = wide
     steps, groups = heads // wide, span // count
     total_groups = heads // count
     rows = tokens // 2
@@ -569,24 +588,36 @@
         )
         near.append(n), probs.append(p)
 
+    far, gained = run(
+        reach_kernel,
+        [info, rates, *kept(qh, gh), gain],
+        [SMEM, SMEM] + [VMEM] * 3,
+        [major, pltpu.VMEM((heads, tokens, dim), F32)],
+        [VMEM] * 2,
+        cost=(4 * unit, 0),
+    )
+
     mine, other = entering_state(leave, keep, info, rates, 0, True, hops)
     states = pltpu.VMEM((heads, dim, dim), BF16)
     attn, states, mids, stats = run(
         partial(attend_kernel, total_groups),
-        [info, rates, *kept(qh, gh), gain, mine, other, *kept(early, *near)],
-        [SMEM, SMEM] + [VMEM] * (6 + total_groups),
+        [info, rates, *kept(far, gained), mine, other, *kept(early, *near)],
+        [SMEM, SMEM] + [VMEM] * (5 + total_groups),
         [major, states, states, shape(2, tokens)],
         [VMEM] * 4,
         cost=(2 * unit * dim, 0),
     )
     parts = head_sum_parts(stats)
 
+    faded = run(
+        lead_kernel, [info, rates, *kept(qh)], [SMEM, SMEM, VMEM], major, VMEM, cost=(2 * unit, 0)
+    )
     grads, halves, late = [], [], []
     for c in chunks:
         g, *pair, n = run(
             partial(norm_kernel, c * span, width, len(parts)),
-            [info, rates, *parts, *kept(attn, gh, qh), gain],
-            [SMEM, SMEM] + [VMEM] * (len(parts) + 4),
+            [info, rates, *parts, *kept(attn, gained, faded)],
+            [SMEM, SMEM] + [VMEM] * (len(parts) + 3),
             [chunk, half, half, pltpu.VMEM((span, dim, dim), F32)],
             [VMEM] * 4,
             cost=(2 * unit * dim // len(chunks), 0),
@@ -617,37 +648,33 @@
         cost=(0, 2 * unit),
     )
 
-    entered = [entering_state(*halves[2 * c : 2 * c + 2], info, rates, c * span, False, hops) for c in chunks]
+    far_k, far_v = run(
+        return_kernel,
+        [info, rates, *kept(kh, vh)],
+        [SMEM, SMEM] + [VMEM] * 2,
+        [major] * 2,
+        [VMEM] * 2,
+        cost=(4 * unit, 0),
+    )
+    entered = [
+        entering_state(*halves[2 * c : 2 * c + 2], info, rates, c * span, False, hops)
+        for c in chunks
+    ]
     made = []
-    if len(chunks) == 1:
-        ((mine, other),) = entered
-        half_block = pl.BlockSpec((wide, dim // 2, dim), lambda i: (i, 0, 0))
-        full_block = pl.BlockSpec((wide, dim, dim), lambda i: (i, 0, 0))
-        made = run(
-            partial(finish_kernel, None, total_groups // steps, steps),
-            [info, rates, *kept(kh, vh), mine, other, late[0], *kept(*dk_part, *dv_part)],
-            [SMEM, SMEM, VMEM, VMEM, half_block, half_block, full_block] + [VMEM] * (2 * total_groups),
-            [full, full],
-            [token_block, token_block],
-            steps=steps,
-            scratch=[pltpu.VMEM((wide, dim, dim), BF16)],
-            cost=(4 * unit * dim, 4 * unit),
-        )
-        return dq, *made
     for c in chunks:
         mine, other = entered[c]
         here = slice(c * groups, (c + 1) * groups)
-        args = [info, rates, *kept(kh, vh), mine, other, *kept(late[c], *dk_part[here], *dv_part[here])]
+        args = [info, rates, *kept(far_k, far_v), mine, other, *kept(late[c], *dk_part[here], *dv_part[here])]
         specs = [SMEM, SMEM] + [VMEM] * (5 + 2 * groups)
         alias = {len(args) + j: j for j in range(len(made))}
-        block = pl.BlockSpec((tokens, wide, dim), lambda i, c=c: (0, c, 0))
+        block = pl.BlockSpec((rows, wide, dim), lambda i, c=c: (i, c, 0))
         made = run(
-            partial(finish_kernel, c * span, groups, 1),
+            partial(finish_kernel, c * span, groups),
             args + list(made),
             specs + [pl.BlockSpec(memory_space=pl.ANY)] * len(made),
             [full, full],
             [block, block],
-            steps=1,
+            steps=2,
             scratch=[pltpu.VMEM((wide, dim, dim), BF16)],
             alias=alias,
             cost=(4 * unit * dim // len(chunks), 4 * unit // len(chunks)),

time: 107 us -> 104 us (0.972)
  waiting for transfers between devices: 43.1 us -> 39.7 us
  starting transfers between devices: 21.4 us -> 22.9 us
    ppermute x19, waiting for transfers between devices: 43.1 us -> 39.7 us  [send(): return lax.ppermute(block, axis, route)]
    ppermute x19, starting transfers between devices: 21.4 us -> 22.9 us  [send(): return lax.ppermute(block, axis, route)]
    pallas_call x30 -> x41, Pallas kernels: 39.9 us -> 39.2 us  [run(): pl.pallas_call(kernel, out_shape=outs, grid=() if steps is None else (ste...]
  transfers between devices with their start and end apart: 19 -> 19, of which waited for: 12 -> 11; matrix products, arithmetic and copies ran while one was open for 0% -> 0% of each run, Pallas kernels for 27% -> 29%
where the time goes in v5:
time: 104 us; the launch traced here: 103 us
  waiting for transfers between devices  39.7 us (38%)
  Pallas kernels  39.2 us (38%)
  starting transfers between devices  22.9 us (22%)
    ppermute x19, waiting for transfers between devices, send(): return lax.ppermute(block, axis, route)  39.7 us
    pallas_call x41, Pallas kernels, run(): pl.pallas_call(kernel, out_shape=outs, grid=() if steps is None else (ste...  39.2 us
    ppermute x19, starting transfers between devices, send(): return lax.ppermute(block, axis, route)  22.9 us
  transfers between devices with their start and end apart: 19, of which 11 were waited for; matrix products, arithmetic and copies ran while one was open for 0% of the time, Pallas kernels for 29%

profile of v5, /device:TPU:12, one launch (start us, length us, event | category | flops | bytes accessed | tf_op | source)
XLA Modules:
  0.0 102.8 jit_solution(14252886411498488358)
XLA Ops:
  0.6 4.1 %shard_map.97 = (bf16[16,512,128]{2,1,0:T(8,128)(2,1)S(1)}, bf16[16,512,128]{2,1,0:T(8,128)(2,1)S(1)}, f32[16,64,128]{2,1,0:T(8,128)S(1)}, f32[16,64,128]{2,1,0:T(8,128)S(1)}, f32[16,128,128]{2,1,0:T(8,128)S(1)}) custom-call(s32[32]{0:T(128)} %docs_ref.5, f32[16]{0:T(128)} %rate_ref.1, bf16[512,16,128]{2,1,0:T(8,128)(2,1)} %k_ref.1, bf16[512,16,128]{2,1,0:T(8,128)(2,1)} %v_ref.1), custom_call_target="tpu_custom_call" | custom-call | flops 268435456 | bytes 8388608 | tf_op jit(solution)/shard_map/pallas_call | solution.py:508
  4.8 1.9 %shard_map.94 = (s32[25]{0:T(128)S(4)}, f32[16]{0:T(128)S(4)}) custom-call(s32[32]{0:T(128)} %docs_ref.5, f32[16]{0:T(128)} %rate_ref.1), custom_call_target="tpu_custom_call" | custom-call | tf_op jit(solution)/shard_map/pallas_call | solution.py:508
  7.5 8.2 %collective-permute-done.1.came_ref = f32[16,32,128]{2,1,0:T(8,128)S(1)} collective-permute-done((f32[16,32,128]{2,1,0:T(8,128)S(1)}, f32[16,32,128]{2,1,0:T(8,128)S(1)}, u32[]{:S(2)}, u32[]{:S(2)}) %collective-permute-start.1) | collective-permute-done | bytes 262176 | tf_op jit(solution)/shard_map/ppermute | solution.py:431
  15.7 3.5 %collective-permute-start.2 = (f32[16,32,128]{2,1,0:T(8,128)S(1)}, f32[16,32,128]{2,1,0:T(8,128)S(1)}, u32[]{:S(2)}, u32[]{:S(2)}) collective-permute-start(f32[16,32,128]{2,1,0:T(8,128)S(1)} %shard_map.99), channel_id=1, source_target_pairs={{0,4},{1,5},{2,6},{3,7},{4,8},{5,9},{6,10},{7,11},{8,12},{9,13},{1... | collective-permute-start | bytes 786440 | tf_op jit(solution)/shard_map/ppermute | solution.py:431
  19.2 6.3 %collective-permute-done.2.refs_0_ = f32[16,32,128]{2,1,0:T(8,128)S(1)} collective-permute-done((f32[16,32,128]{2,1,0:T(8,128)S(1)}, f32[16,32,128]{2,1,0:T(8,128)S(1)}, u32[]{:S(2)}, u32[]{:S(2)}) %collective-permute-start.2) | collective-permute-done | bytes 262176 | tf_op jit(solution)/shard_map/ppermute | solution.py:431
  25.5 3.5 %collective-permute-start.3 = (f32[16,32,128]{2,1,0:T(8,128)S(1)}, f32[16,32,128]{2,1,0:T(8,128)S(1)}, u32[]{:S(2)}, u32[]{:S(2)}) collective-permute-start(f32[16,32,128]{2,1,0:T(8,128)S(1)} %collective-permute-done.2.refs_0_), channel_id=1, source_target_pairs={{0,4},{1,5},{2,6},{3,7},{4,8},{5,9},{6,10},{7,11},{8,12},{9,13},{1... | collective-permute-start | bytes 786440 | tf_op jit(solution)/shard_map/ppermute | solution.py:431
  28.9 5.4 %collective-permute-done.3.refs_1_ = f32[16,32,128]{2,1,0:T(8,128)S(1)} collective-permute-done((f32[16,32,128]{2,1,0:T(8,128)S(1)}, f32[16,32,128]{2,1,0:T(8,128)S(1)}, u32[]{:S(2)}, u32[]{:S(2)}) %collective-permute-start.3) | collective-permute-done | bytes 262176 | tf_op jit(solution)/shard_map/ppermute | solution.py:431
  35.0 5.9 %collective-permute-done.4.came_part_ref = f32[16,32,128]{2,1,0:T(8,128)S(1)} collective-permute-done((f32[16,32,128]{2,1,0:T(8,128)S(1)}, f32[16,32,128]{2,1,0:T(8,128)S(1)}, u32[]{:S(2)}, u32[]{:S(2)}) %collective-permute-start.4) | collective-permute-done | bytes 262176 | tf_op jit(solution)/shard_map/ppermute | solution.py:431
  42.2 2.6 %shard_map.95 = (bf16[16,512,128]{2,1,0:T(8,128)(2,1)S(1)}, bf16[16,512,128]{2,1,0:T(8,128)(2,1)S(1)}) custom-call(bf16[512,16,128]{2,1,0:T(8,128)(2,1)} %q_ref.1, bf16[512,16,128]{2,1,0:T(8,128)(2,1)} %g_ref.1), custom_call_target="tpu_custom_call" | custom-call | bytes 8388608 | tf_op jit(solution)/shard_map/pallas_call | solution.py:508
  44.9 1.8 %shard_map.96 = (bf16[16,512,128]{2,1,0:T(8,128)(2,1)S(1)}, f32[16,512,128]{2,1,0:T(8,128)S(1)}) custom-call(s32[25]{0:T(128)S(4)} %get-tuple-element.90.info_ref, f32[16]{0:T(128)S(4)} %get-tuple-element.91.rate_ref, bf16[16,512,128]{2,1,0:T(8,128)(2,1)S(1)} %get-tuple-element.92.qh_ref, bf16[16,512,128]{2,1,0:T(8,128)(2,1)S(1)} %get-tuple-element.93.gh_ref, ...), custom_call_target="tpu_custom_call" | custom-call | flops 4194304 | tf_op jit(solution)/shard_map/pallas_call | solution.py:508
  52.0 1.7 %shard_map.111 = (bf16[16,512,128]{2,1,0:T(8,128)(2,1)S(1)}, bf16[16,128,128]{2,1,0:T(8,128)(2,1)S(1)}, bf16[16,128,128]{2,1,0:T(8,128)(2,1)S(1)}, f32[2,512]{1,0:T(2,128)S(1)}) custom-call(s32[25]{0:T(128)S(4)} %get-tuple-element.90.info_ref, f32[16]{0:T(128)S(4)} %get-tuple-element.91.rate_ref, bf16[16,512,128]{2,1,0:T(8,128)(2,1)S(1)} %get-tuple-element.94.far_ref, ...), custom_call_target="tpu_custom_call" | custom-call | flops 268435456 | tf_op jit(solution)/shard_map/pallas_call | solution.py:508
  53.7 1.6 %collective-permute-start.6 = (f32[2,512]{1,0:T(2,128)S(1)}, f32[2,512]{1,0:T(2,128)S(1)}, u32[]{:S(2)}, u32[]{:S(2)}) collective-permute-start(f32[2,512]{1,0:T(2,128)S(1)} %get-tuple-element.115.refs_0_), channel_id=1, source_target_pairs={{0,16},{16,0},{1,17},{17,1},{2,18},{18,2},{3,19},{19,3},{4,20},{20... | collective-permute-start | bytes 12296 | tf_op jit(solution)/shard_map/ppermute | solution.py:431
  56.1 1.3 %collective-permute-done.6.refs_1_ = f32[2,512]{1,0:T(2,128)S(1)} collective-permute-done((f32[2,512]{1,0:T(2,128)S(1)}, f32[2,512]{1,0:T(2,128)S(1)}, u32[]{:S(2)}, u32[]{:S(2)}) %collective-permute-start.6) | collective-permute-done | bytes 4128 | tf_op jit(solution)/shard_map/ppermute | solution.py:431
  62.1 4.2 %collective-permute-done.14.came_ref = f32[8,32,128]{2,1,0:T(8,128)S(1)} collective-permute-done((f32[8,32,128]{2,1,0:T(8,128)S(1)}, f32[8,32,128]{2,1,0:T(8,128)S(1)}, u32[]{:S(2)}, u32[]{:S(2)}) %collective-permute-start.14) | collective-permute-done | bytes 131104 | tf_op jit(solution)/shard_map/ppermute | solution.py:431
  66.3 1.9 %collective-permute-start.15 = (f32[8,32,128]{2,1,0:T(8,128)S(1)}, f32[8,32,128]{2,1,0:T(8,128)S(1)}, u32[]{:S(2)}, u32[]{:S(2)}) collective-permute-start(f32[8,32,128]{2,1,0:T(8,128)S(1)} %shard_map.130), channel_id=1, source_target_pairs={{4,0},{5,1},{6,2},{7,3},{8,4},{9,5},{10,6},{11,7},{12,8},{13,9},{1... | collective-permute-start | bytes 393224 | tf_op jit(solution)/shard_map/ppermute | solution.py:431
  68.3 1.9 %collective-permute-start.9 = (f32[8,32,128]{2,1,0:T(8,128)S(1)}, f32[8,32,128]{2,1,0:T(8,128)S(1)}, u32[]{:S(2)}, u32[]{:S(2)}) collective-permute-start(f32[8,32,128]{2,1,0:T(8,128)S(1)} %shard_map.126), channel_id=1, source_target_pairs={{4,0},{5,1},{6,2},{7,3},{8,4},{9,5},{10,6},{11,7},{12,8},{13,9},{1... | collective-permute-start | bytes 393224 | tf_op jit(solution)/shard_map/ppermute | solution.py:431
  70.2 4.0 %collective-permute-done.15.refs_0_ = f32[8,32,128]{2,1,0:T(8,128)S(1)} collective-permute-done((f32[8,32,128]{2,1,0:T(8,128)S(1)}, f32[8,32,128]{2,1,0:T(8,128)S(1)}, u32[]{:S(2)}, u32[]{:S(2)}) %collective-permute-start.15) | collective-permute-done | bytes 131104 | tf_op jit(solution)/shard_map/ppermute | solution.py:431
  74.3 1.9 %collective-permute-start.16 = (f32[8,32,128]{2,1,0:T(8,128)S(1)}, f32[8,32,128]{2,1,0:T(8,128)S(1)}, u32[]{:S(2)}, u32[]{:S(2)}) collective-permute-start(f32[8,32,128]{2,1,0:T(8,128)S(1)} %collective-permute-done.15.refs_0_), channel_id=1, source_target_pairs={{4,0},{5,1},{6,2},{7,3},{8,4},{9,5},{10,6},{11,7},{12,8},{13,9},{1... | collective-permute-start | bytes 393224 | tf_op jit(solution)/shard_map/ppermute | solution.py:431
  77.0 2.1 %collective-permute-start.10 = (f32[8,32,128]{2,1,0:T(8,128)S(1)}, f32[8,32,128]{2,1,0:T(8,128)S(1)}, u32[]{:S(2)}, u32[]{:S(2)}) collective-permute-start(f32[8,32,128]{2,1,0:T(8,128)S(1)} %collective-permute-done.9.refs_0_), channel_id=1, source_target_pairs={{4,0},{5,1},{6,2},{7,3},{8,4},{9,5},{10,6},{11,7},{12,8},{13,9},{1... | collective-permute-start | bytes 393224 | tf_op jit(solution)/shard_map/ppermute | solution.py:431
  79.1 3.2 %collective-permute-done.16.refs_1_ = f32[8,32,128]{2,1,0:T(8,128)S(1)} collective-permute-done((f32[8,32,128]{2,1,0:T(8,128)S(1)}, f32[8,32,128]{2,1,0:T(8,128)S(1)}, u32[]{:S(2)}, u32[]{:S(2)}) %collective-permute-start.16) | collective-permute-done | bytes 131104 | tf_op jit(solution)/shard_map/ppermute | solution.py:431
  84.3 1.5 %collective-permute-start.11 = (f32[8,32,128]{2,1,0:T(8,128)S(1)}, f32[8,32,128]{2,1,0:T(8,128)S(1)}, u32[]{:S(2)}, u32[]{:S(2)}) collective-permute-start(f32[8,32,128]{2,1,0:T(8,128)S(1)} %get-tuple-element.144), channel_id=1, source_target_pairs={{0,2},{1,3},{2,0},{3,1},{4,6},{5,7},{6,4},{7,5},{8,10},{9,11},{10,... | collective-permute-start | bytes 393224 | tf_op jit(solution)/shard_map/ppermute | solution.py:431
  85.8 1.3 %shard_map.114 = (bf16[2,512,128]{2,1,0:T(8,128)(2,1)S(1)}, bf16[2,512,128]{2,1,0:T(8,128)(2,1)S(1)}, bf16[2,512,128]{2,1,0:T(8,128)(2,1)S(1)}) custom-call(s32[25]{0:T(128)S(4)} %get-tuple-element.90.info_ref, f32[16]{0:T(128)S(4)} %get-tuple-element.91.rate_ref, bf16[8,512,128]{2,1,0:T(8,128)(2,1)S(1)} %get-tuple-element.117.grad_ref, ...), custom_call_target="tpu_custom_call" | custom-call | flops 536870912 | tf_op jit(solution)/shard_map/pallas_call | solution.py:508
  87.1 1.3 %shard_map.115 = (bf16[2,512,128]{2,1,0:T(8,128)(2,1)S(1)}, bf16[2,512,128]{2,1,0:T(8,128)(2,1)S(1)}, bf16[2,512,128]{2,1,0:T(8,128)(2,1)S(1)}) custom-call(s32[25]{0:T(128)S(4)} %get-tuple-element.90.info_ref, f32[16]{0:T(128)S(4)} %get-tuple-element.91.rate_ref, bf16[8,512,128]{2,1,0:T(8,128)(2,1)S(1)} %get-tuple-element.117.grad_ref, ...), custom_call_target="tpu_custom_call" | custom-call | flops 536870912 | tf_op jit(solution)/shard_map/pallas_call | solution.py:508
  88.6 1.3 %shard_map.116 = (bf16[2,512,128]{2,1,0:T(8,128)(2,1)S(1)}, bf16[2,512,128]{2,1,0:T(8,128)(2,1)S(1)}, bf16[2,512,128]{2,1,0:T(8,128)(2,1)S(1)}) custom-call(s32[25]{0:T(128)S(4)} %get-tuple-element.90.info_ref, f32[16]{0:T(128)S(4)} %get-tuple-element.91.rate_ref, bf16[8,512,128]{2,1,0:T(8,128)(2,1)S(1)} %get-tuple-element.117.grad_ref, ...), custom_call_target="tpu_custom_call" | custom-call | flops 536870912 | tf_op jit(solution)/shard_map/pallas_call | solution.py:508
  90.6 1.3 %shard_map.117 = (bf16[2,512,128]{2,1,0:T(8,128)(2,1)S(1)}, bf16[2,512,128]{2,1,0:T(8,128)(2,1)S(1)}, bf16[2,512,128]{2,1,0:T(8,128)(2,1)S(1)}) custom-call(s32[25]{0:T(128)S(4)} %get-tuple-element.90.info_ref, f32[16]{0:T(128)S(4)} %get-tuple-element.91.rate_ref, bf16[8,512,128]{2,1,0:T(8,128)(2,1)S(1)} %get-tuple-element.117.grad_ref, ...), custom_call_target="tpu_custom_call" | custom-call | flops 536870912 | tf_op jit(solution)/shard_map/pallas_call | solution.py:508
  92.0 1.3 %shard_map.119 = (bf16[2,512,128]{2,1,0:T(8,128)(2,1)S(1)}, bf16[2,512,128]{2,1,0:T(8,128)(2,1)S(1)}, bf16[2,512,128]{2,1,0:T(8,128)(2,1)S(1)}) custom-call(s32[25]{0:T(128)S(4)} %get-tuple-element.90.info_ref, f32[16]{0:T(128)S(4)} %get-tuple-element.91.rate_ref, bf16[8,512,128]{2,1,0:T(8,128)(2,1)S(1)} %get-tuple-element.128.grad_ref, ...), custom_call_target="tpu_custom_call" | custom-call | flops 536870912 | tf_op jit(solution)/shard_map/pallas_call | solution.py:508
  93.3 1.3 %shard_map.120 = (bf16[2,512,128]{2,1,0:T(8,128)(2,1)S(1)}, bf16[2,512,128]{2,1,0:T(8,128)(2,1)S(1)}, bf16[2,512,128]{2,1,0:T(8,128)(2,1)S(1)}) custom-call(s32[25]{0:T(128)S(4)} %get-tuple-element.90.info_ref, f32[16]{0:T(128)S(4)} %get-tuple-element.91.rate_ref, bf16[8,512,128]{2,1,0:T(8,128)(2,1)S(1)} %get-tuple-element.128.grad_ref, ...), custom_call_target="tpu_custom_call" | custom-call | flops 536870912 | tf_op jit(solution)/shard_map/pallas_call | solution.py:508
  94.7 1.3 %shard_map.121 = (bf16[2,512,128]{2,1,0:T(8,128)(2,1)S(1)}, bf16[2,512,128]{2,1,0:T(8,128)(2,1)S(1)}, bf16[2,512,128]{2,1,0:T(8,128)(2,1)S(1)}) custom-call(s32[25]{0:T(128)S(4)} %get-tuple-element.90.info_ref, f32[16]{0:T(128)S(4)} %get-tuple-element.91.rate_ref, bf16[8,512,128]{2,1,0:T(8,128)(2,1)S(1)} %get-tuple-element.128.grad_ref, ...), custom_call_target="tpu_custom_call" | custom-call | flops 536870912 | tf_op jit(solution)/shard_map/pallas_call | solution.py:508
  96.0 1.3 %shard_map.122 = (bf16[2,512,128]{2,1,0:T(8,128)(2,1)S(1)}, bf16[2,512,128]{2,1,0:T(8,128)(2,1)S(1)}, bf16[2,512,128]{2,1,0:T(8,128)(2,1)S(1)}) custom-call(s32[25]{0:T(128)S(4)} %get-tuple-element.90.info_ref, f32[16]{0:T(128)S(4)} %get-tuple-element.91.rate_ref, bf16[8,512,128]{2,1,0:T(8,128)(2,1)S(1)} %get-tuple-element.128.grad_ref, ...), custom_call_target="tpu_custom_call" | custom-call | flops 536870912 | tf_op jit(solution)/shard_map/pallas_call | solution.py:508
  97.3 1.5 %shard_map.123 = bf16[512,16,128]{2,1,0:T(8,128)(2,1)} custom-call(bf16[2,512,128]{2,1,0:T(8,128)(2,1)S(1)} %get-tuple-element.121.refs_0_, bf16[2,512,128]{2,1,0:T(8,128)(2,1)S(1)} %get-tuple-element.123.refs_1_, bf16[2,512,128]{2,1,0:T(8,128)(2,1)S(1)} %get-tuple-element.125.refs_2_, bf16[2,512,128]{2,1,0:T(8,128)(2,1)S(1)} %get-tuple-element.127.refs_3_, ...), custom_call_target="tpu_custom_call" | custom-call | bytes 2097152 | tf_op jit(solution)/shard_map/pallas_call | solution.py:508
  98.8 2.0 %shard_map.133 = (bf16[512,16,128]{2,1,0:T(8,128)(2,1)}, bf16[512,16,128]{2,1,0:T(8,128)(2,1)}) custom-call(s32[25]{0:T(128)S(4)} %get-tuple-element.90.info_ref, f32[16]{0:T(128)S(4)} %get-tuple-element.91.rate_ref, bf16[16,512,128]{2,1,0:T(8,128)(2,1)S(1)} %get-tuple-element.137.far_k_ref, bf16[16,512,128]{2,1,0:T(8,128)(2,1)S(1)} %get-tuple-element.138.far_v_ref, ...), custom_call_target="tpu_custom_call" | custom-call | flops 268435456 | bytes 2097152 | tf_op jit(solution)/shard_map/pallas_call | solution.py:508
  100.8 2.0 %shard_map.134 = (bf16[512,16,128]{2,1,0:T(8,128)(2,1)}, bf16[512,16,128]{2,1,0:T(8,128)(2,1)}) custom-call(s32[25]{0:T(128)S(4)} %get-tuple-element.90.info_ref, f32[16]{0:T(128)S(4)} %get-tuple-element.91.rate_ref, bf16[16,512,128]{2,1,0:T(8,128)(2,1)S(1)} %get-tuple-element.137.far_k_ref, ...), custom_call_target="tpu_custom_call", output_to_operand_aliasing={{0}: (15, {}), {1}: (16, {})} | custom-call | flops 268435456 | bytes 2097152 | tf_op jit(solution)/shard_map/pallas_call | solution.py:508
  (47 shorter events, 17.2 us)
Async XLA Ops:
  4.8 2.0 %collective-permute-start = (f32[16,64,128]{2,1,0:T(8,128)S(1)}, f32[16,64,128]{2,1,0:T(8,128)S(1)}, u32[]{:S(2)}, u32[]{:S(2)}) collective-permute-start(f32[16,64,128]{2,1,0:T(8,128)S(1)} %get-tuple-element.97), channel_id=1, source_target_pairs={{0,1},{1,0},{2,3},{3,2},{4,5},{5,4},{6,7},{7,6},{8,9},{9,8},{10,11... | collective-permute-start | bytes 1572872 | tf_op jit(solution)/shard_map/ppermute | solution.py:431
  6.9 8.8 %collective-permute-start.1 = (f32[16,32,128]{2,1,0:T(8,128)S(1)}, f32[16,32,128]{2,1,0:T(8,128)S(1)}, u32[]{:S(2)}, u32[]{:S(2)}) collective-permute-start(f32[16,32,128]{2,1,0:T(8,128)S(1)} %get-tuple-element.99), channel_id=1, source_target_pairs={{0,2},{1,3},{2,0},{3,1},{4,6},{5,7},{6,4},{7,5},{8,10},{9,11},{10,... | collective-permute-start | bytes 786440 | tf_op jit(solution)/shard_map/ppermute | solution.py:431
  15.7 9.7 %collective-permute-start.2 = (f32[16,32,128]{2,1,0:T(8,128)S(1)}, f32[16,32,128]{2,1,0:T(8,128)S(1)}, u32[]{:S(2)}, u32[]{:S(2)}) collective-permute-start(f32[16,32,128]{2,1,0:T(8,128)S(1)} %shard_map.99), channel_id=1, source_target_pairs={{0,4},{1,5},{2,6},{3,7},{4,8},{5,9},{6,10},{7,11},{8,12},{9,13},{1... | collective-permute-start | bytes 786440 | tf_op jit(solution)/shard_map/ppermute | solution.py:431
  25.5 8.9 %collective-permute-start.3 = (f32[16,32,128]{2,1,0:T(8,128)S(1)}, f32[16,32,128]{2,1,0:T(8,128)S(1)}, u32[]{:S(2)}, u32[]{:S(2)}) collective-permute-start(f32[16,32,128]{2,1,0:T(8,128)S(1)} %collective-permute-done.2.refs_0_), channel_id=1, source_target_pairs={{0,4},{1,5},{2,6},{3,7},{4,8},{5,9},{6,10},{7,11},{8,12},{9,13},{1... | collective-permute-start | bytes 786440 | tf_op jit(solution)/shard_map/ppermute | solution.py:431
  34.4 6.4 %collective-permute-start.4 = (f32[16,32,128]{2,1,0:T(8,128)S(1)}, f32[16,32,128]{2,1,0:T(8,128)S(1)}, u32[]{:S(2)}, u32[]{:S(2)}) collective-permute-start(f32[16,32,128]{2,1,0:T(8,128)S(1)} %get-tuple-element.101), channel_id=1, source_target_pairs={{0,2},{1,3},{2,0},{3,1},{4,6},{5,7},{6,4},{7,5},{8,10},{9,11},{10,... | collective-permute-start | bytes 786440 | tf_op jit(solution)/shard_map/ppermute | solution.py:431
  41.0 11.0 %collective-permute-start.5 = (f32[16,64,128]{2,1,0:T(8,128)S(1)}, f32[16,64,128]{2,1,0:T(8,128)S(1)}, u32[]{:S(2)}, u32[]{:S(2)}) collective-permute-start(f32[16,64,128]{2,1,0:T(8,128)S(1)} %get-tuple-element.103), channel_id=1, source_target_pairs={{0,1},{1,0},{2,3},{3,2},{4,5},{5,4},{6,7},{7,6},{8,9},{9,8},{10,11... | collective-permute-start | bytes 1572872 | tf_op jit(solution)/shard_map/ppermute | solution.py:431
  53.7 3.7 %collective-permute-start.6 = (f32[2,512]{1,0:T(2,128)S(1)}, f32[2,512]{1,0:T(2,128)S(1)}, u32[]{:S(2)}, u32[]{:S(2)}) collective-permute-start(f32[2,512]{1,0:T(2,128)S(1)} %get-tuple-element.115.refs_0_), channel_id=1, source_target_pairs={{0,16},{16,0},{1,17},{17,1},{2,18},{18,2},{3,19},{19,3},{4,20},{20... | collective-permute-start | bytes 12296 | tf_op jit(solution)/shard_map/ppermute | solution.py:431
  58.2 1.6 %collective-permute-start.13 = (f32[8,64,128]{2,1,0:T(8,128)S(1)}, f32[8,64,128]{2,1,0:T(8,128)S(1)}, u32[]{:S(2)}, u32[]{:S(2)}) collective-permute-start(f32[8,64,128]{2,1,0:T(8,128)S(1)} %get-tuple-element.157), channel_id=1, source_target_pairs={{0,1},{1,0},{2,3},{3,2},{4,5},{5,4},{6,7},{7,6},{8,9},{9,8},{10,11... | collective-permute-start | bytes 786440 | tf_op jit(solution)/shard_map/ppermute | solution.py:431
  59.1 1.7 %collective-permute-start.7 = (f32[8,64,128]{2,1,0:T(8,128)S(1)}, f32[8,64,128]{2,1,0:T(8,128)S(1)}, u32[]{:S(2)}, u32[]{:S(2)}) collective-permute-start(f32[8,64,128]{2,1,0:T(8,128)S(1)} %get-tuple-element.140), channel_id=1, source_target_pairs={{0,1},{1,0},{2,3},{3,2},{4,5},{5,4},{6,7},{7,6},{8,9},{9,8},{10,11... | collective-permute-start | bytes 786440 | tf_op jit(solution)/shard_map/ppermute | solution.py:431
  59.9 6.4 %collective-permute-start.14 = (f32[8,32,128]{2,1,0:T(8,128)S(1)}, f32[8,32,128]{2,1,0:T(8,128)S(1)}, u32[]{:S(2)}, u32[]{:S(2)}) collective-permute-start(f32[8,32,128]{2,1,0:T(8,128)S(1)} %get-tuple-element.159), channel_id=1, source_target_pairs={{0,2},{1,3},{2,0},{3,1},{4,6},{5,7},{6,4},{7,5},{8,10},{9,11},{10,... | collective-permute-start | bytes 393224 | tf_op jit(solution)/shard_map/ppermute | solution.py:431
  60.9 7.4 %collective-permute-start.8 = (f32[8,32,128]{2,1,0:T(8,128)S(1)}, f32[8,32,128]{2,1,0:T(8,128)S(1)}, u32[]{:S(2)}, u32[]{:S(2)}) collective-permute-start(f32[8,32,128]{2,1,0:T(8,128)S(1)} %get-tuple-element.142), channel_id=1, source_target_pairs={{0,2},{1,3},{2,0},{3,1},{4,6},{5,7},{6,4},{7,5},{8,10},{9,11},{10,... | collective-permute-start | bytes 393224 | tf_op jit(solution)/shard_map/ppermute | solution.py:431
  66.3 8.0 %collective-permute-start.15 = (f32[8,32,128]{2,1,0:T(8,128)S(1)}, f32[8,32,128]{2,1,0:T(8,128)S(1)}, u32[]{:S(2)}, u32[]{:S(2)}) collective-permute-start(f32[8,32,128]{2,1,0:T(8,128)S(1)} %shard_map.130), channel_id=1, source_target_pairs={{4,0},{5,1},{6,2},{7,3},{8,4},{9,5},{10,6},{11,7},{12,8},{13,9},{1... | collective-permute-start | bytes 393224 | tf_op jit(solution)/shard_map/ppermute | solution.py:431
  68.3 8.7 %collective-permute-start.9 = (f32[8,32,128]{2,1,0:T(8,128)S(1)}, f32[8,32,128]{2,1,0:T(8,128)S(1)}, u32[]{:S(2)}, u32[]{:S(2)}) collective-permute-start(f32[8,32,128]{2,1,0:T(8,128)S(1)} %shard_map.126), channel_id=1, source_target_pairs={{4,0},{5,1},{6,2},{7,3},{8,4},{9,5},{10,6},{11,7},{12,8},{13,9},{1... | collective-permute-start | bytes 393224 | tf_op jit(solution)/shard_map/ppermute | solution.py:431
  74.3 8.0 %collective-permute-start.16 = (f32[8,32,128]{2,1,0:T(8,128)S(1)}, f32[8,32,128]{2,1,0:T(8,128)S(1)}, u32[]{:S(2)}, u32[]{:S(2)}) collective-permute-start(f32[8,32,128]{2,1,0:T(8,128)S(1)} %collective-permute-done.15.refs_0_), channel_id=1, source_target_pairs={{4,0},{5,1},{6,2},{7,3},{8,4},{9,5},{10,6},{11,7},{12,8},{13,9},{1... | collective-permute-start | bytes 393224 | tf_op jit(solution)/shard_map/ppermute | solution.py:431
  77.0 7.2 %collective-permute-start.10 = (f32[8,32,128]{2,1,0:T(8,128)S(1)}, f32[8,32,128]{2,1,0:T(8,128)S(1)}, u32[]{:S(2)}, u32[]{:S(2)}) collective-permute-start(f32[8,32,128]{2,1,0:T(8,128)S(1)} %collective-permute-done.9.refs_0_), channel_id=1, source_target_pairs={{4,0},{5,1},{6,2},{7,3},{8,4},{9,5},{10,6},{11,7},{12,8},{13,9},{1... | collective-permute-start | bytes 393224 | tf_op jit(solution)/shard_map/ppermute | solution.py:431
  82.4 6.1 %collective-permute-start.17 = (f32[8,32,128]{2,1,0:T(8,128)S(1)}, f32[8,32,128]{2,1,0:T(8,128)S(1)}, u32[]{:S(2)}, u32[]{:S(2)}) collective-permute-start(f32[8,32,128]{2,1,0:T(8,128)S(1)} %get-tuple-element.161), channel_id=1, source_target_pairs={{0,2},{1,3},{2,0},{3,1},{4,6},{5,7},{6,4},{7,5},{8,10},{9,11},{10,... | collective-permute-start | bytes 393224 | tf_op jit(solution)/shard_map/ppermute | solution.py:431
  84.3 5.7 %collective-permute-start.11 = (f32[8,32,128]{2,1,0:T(8,128)S(1)}, f32[8,32,128]{2,1,0:T(8,128)S(1)}, u32[]{:S(2)}, u32[]{:S(2)}) collective-permute-start(f32[8,32,128]{2,1,0:T(8,128)S(1)} %get-tuple-element.144), channel_id=1, source_target_pairs={{0,2},{1,3},{2,0},{3,1},{4,6},{5,7},{6,4},{7,5},{8,10},{9,11},{10,... | collective-permute-start | bytes 393224 | tf_op jit(solution)/shard_map/ppermute | solution.py:431
  88.6 10.3 %collective-permute-start.18 = (f32[8,64,128]{2,1,0:T(8,128)S(1)}, f32[8,64,128]{2,1,0:T(8,128)S(1)}, u32[]{:S(2)}, u32[]{:S(2)}) collective-permute-start(f32[8,64,128]{2,1,0:T(8,128)S(1)} %get-tuple-element.163), channel_id=1, source_target_pairs={{0,1},{1,0},{2,3},{3,2},{4,5},{5,4},{6,7},{7,6},{8,9},{9,8},{10,11... | collective-permute-start | bytes 786440 | tf_op jit(solution)/shard_map/ppermute | solution.py:431
  90.1 10.7 %collective-permute-start.12 = (f32[8,64,128]{2,1,0:T(8,128)S(1)}, f32[8,64,128]{2,1,0:T(8,128)S(1)}, u32[]{:S(2)}, u32[]{:S(2)}) collective-permute-start(f32[8,64,128]{2,1,0:T(8,128)S(1)} %get-tuple-element.146), channel_id=1, source_target_pairs={{0,1},{1,0},{2,3},{3,2},{4,5},{5,4},{6,7},{7,6},{8,9},{9,8},{10,11... | collective-permute-start | bytes 786440 | tf_op jit(solution)/shard_map/ppermute | solution.py:431
